TPU v7x, 32 devices: a whole 2x2x4 slice. The times are simulated.
32 devices in a mesh: bf: 4 (over z), sk: 8 (over y, x, core).
Axes of the slice: x: 2, y: 2, z: 4, core: 2. Of those that a mesh axis runs over, the one named last changes fastest.
Arguments:
- kernel: bfloat16 [2, 8192, 16384], P(None, 'bf', 'sk'), may hold values from -1.5625 to 1.5625
- sketch: bfloat16 [3, 16384, 256], P(None, 'sk'), may hold values from -6 to 6
- projections: bfloat16 [2, 4, 2, 256, 128], P(None, 'bf'), may hold values from -0.375 to 0.375
- inverses: bfloat16 [2, 4, 2, 256, 256], P(None, 'bf'), may hold values from -0.375 to 0.375
- norm_gain: float32 [256], replicated, may hold values from 0.5 to 1.5
Outputs:
- factor_sketch: float32 [2, 3, 8192, 256], P(None, None, ('bf', 'sk'))
All inputs are finite; a program needn't handle non-finite values.
Results may differ from a plain program's by a relative error of at most 0.02.
Values may be sent and summed in bfloat16 or wider, within the bound.
No kernel may reach another device: no remote copies, remote signals or barrier semaphores. Data moves between devices by JAX's collectives and lax.ppermute only.
A program may use at most 128 MiB of HBM per device.

v0:
```python
import jax
import jax.numpy as jnp
from jax import lax
from jax.sharding import PartitionSpec as P

epsilon = 1e-06


def swapped(value, axis, bit):
    mask = 2**bit
    pairs = [(source, source ^ mask) for source in range(lax.axis_size(axis))]
    return lax.ppermute(value, axis, pairs)


def complex_block(matrix):
    upper = jnp.concatenate([matrix[0], matrix[1]], axis=1)
    lower = jnp.concatenate([-matrix[1], matrix[0]], axis=1)
    return jnp.concatenate([upper, lower], axis=0)


def shards(kernel, sketch, projections, inverses, norm_gain):
    rank_cols = projections.shape[4]
    first_proj = projections[0, 0]
    both_parts = jnp.concatenate([first_proj[0], first_proj[1]], axis=1)
    sk_proj = jnp.einsum(
        "pcs,sk->pck", sketch, both_parts, preferred_element_type=jnp.float32
    ).astype(jnp.bfloat16)
    turned = jnp.concatenate([-sk_proj[:, :, rank_cols:], sk_proj[:, :, :rank_cols]], axis=2)
    partial_value = jnp.einsum(
        "rc,pck->prk", kernel[0], sk_proj, preferred_element_type=jnp.float32
    )
    partial_value = partial_value + jnp.einsum(
        "rc,pck->prk", kernel[1], turned, preferred_element_type=jnp.float32
    )
    summed = lax.psum_scatter(
        partial_value.astype(jnp.bfloat16), "sk", scatter_dimension=1, tiled=True
    ).astype(jnp.float32)
    own_proj = summed.astype(jnp.bfloat16)
    top_bits = lax.axis_size("bf").bit_length() - 1
    current = summed
    for level_idx in range(projections.shape[0]):
        level_bit = top_bits - 1 - level_idx
        if level_idx > 0:
            rounded = current.astype(jnp.bfloat16)
            level_mat = complex_block(projections[level_idx, 0])
            own_proj = jnp.einsum(
                "prs,sk->prk", rounded, level_mat, preferred_element_type=jnp.float32
            ).astype(jnp.bfloat16)
        partner = swapped(own_proj, "bf", level_bit)
        solver = inverses[level_idx, 0]
        own_mat = complex_block(solver[:, :rank_cols])
        partner_mat = complex_block(solver[:, rank_cols:])
        current = jnp.einsum("prk,ks->prs", own_proj, own_mat, preferred_element_type=jnp.float32)
        current = current + jnp.einsum(
            "prk,ks->prs", partner, partner_mat, preferred_element_type=jnp.float32
        )
    sketch_cols = current.shape[2] // 2
    power = jnp.sum(current * current, axis=-1, keepdims=True) / sketch_cols
    scaled = current * lax.rsqrt(power + epsilon)
    return jnp.stack(
        [scaled[:, :, :sketch_cols] * norm_gain, scaled[:, :, sketch_cols:] * norm_gain]
    )


def solution(mesh):
    placed = (
        P(None, "bf", "sk"),
        P(None, "sk", None),
        P(None, "bf", None, None, None),
        P(None, "bf", None, None, None),
        P(),
    )
    return jax.shard_map(
        shards,
        mesh=mesh,
        in_specs=placed,
        out_specs=P(None, None, ("bf", "sk"), None),
        check_vma=False,
    )
```

profile of v0, /device:TPU:0, one launch (start us, length us, event | category | flops | bytes accessed | tf_op | source)
XLA Modules:
  0.0 120.8 jit_solution(15340014042808696416)
XLA Ops:
  6.5 1.8 %slice_bitcast_fusion.10 = (bf16[256,128]{1,0:T(8,128)(2,1)}, bf16[1,1,1,256,128]{4,3,2,1,0:T(8,128)(2,1)S(1)}, bf16[1,1,1,256,128]{4,3,2,1,0:T(8,128)(2,1)S(1)}, bf16[256,128]{1,0:T(8,128)(2,1)}) fusion(bf16[2,1,2,256,128]{4,3,2,1,0:T(8,128)(2,1)} %param.7), kind=kLoop, calls=%fused_computation.75 | loop fusion | bytes 524288 | tf_op jit(solution)/shard_map/squeeze | solution.py:16
  8.3 0.1 copy.8
  8.4 0.1 copy.9
  8.5 1.0 fusion.11
  9.6 0.2 slice_negate_fusion
  9.8 9.1 %fusion = f32[3,256,2048]{2,1,0:T(8,128)S(1)} fusion(bf16[2,2048,2048]{2,1,0:T(8,128)(2,1)} %param.5, bf16[3,2048,128]{1,2,0:T(8,128)(2,1)S(1)} %get-tuple-element.6, bf16[3,2048,128]{1,2,0:T(8,128)(2,1)S(1)} %get-tuple-element.5), kind=kOutput, calls=%fused_computation | convolution fusion | flops 6448742400 | bytes 17825792 | tf_op jit(solution)/shard_map/rc,pck->prk/dot_general | solution.py:32
  18.9 10.3 %fusion.12 = bf16[3,2048,256]{1,2,0:T(8,128)(2,1)} fusion(f32[3,256,2048]{2,1,0:T(8,128)S(1)} %fusion, bf16[3,2048,256]{1,2,0:T(8,128)(2,1)S(1)} %fusion.11, bf16[2,2048,2048]{2,1,0:T(8,128)(2,1)} %param.5), kind=kOutput, calls=%fused_computation.12 | convolution fusion | flops 6445596672 | bytes 20971520 | tf_op jit(solution)/shard_map/rc,pck->prk/dot_general | solution.py:29
  29.2 1.1 slice_bitcast_fusion
  30.3 0.7 fusion.68
  31.0 0.7 slice_bitcast_fusion.6
  31.7 0.7 slice_bitcast_fusion.2
  32.4 45.8 %reduce-scatter.2.cloned.1.call-done = bf16[3,256,256]{1,2,0:T(8,128)(2,1)} async-done(((bf16[3,2048,256]{1,2,0:T(8,128)(2,1)}), bf16[3,256,256]{1,2,0:T(8,128)(2,1)}) %reduce-scatter.2.cloned.1.call-update) | async-done | bytes 393232 | tf_op jit(solution)/shard_map/reduce_scatter | solution.py:35
  78.2 2.4 %collective-permute-start = (bf16[3,256,256]{1,2,0:T(8,128)(2,1)}, bf16[3,256,256]{1,2,0:T(8,128)(2,1)}, u32[]{:S(2)}, u32[]{:S(2)}) collective-permute-start(bf16[3,256,256]{1,2,0:T(8,128)(2,1)} %reduce-scatter.2.cloned.1.call-done), channel_id=1, source_target_pairs={{0,16},{8,24},{16,0},{24,8},{1,17},{9,25},{17,1},{25,9},{2,18},{10... | collective-permute-start | bytes 1179656 | tf_op jit(solution)/shard_map/ppermute | solution.py:12
  80.5 1.5 %fusion.66 = bf16[256,128]{1,0:T(8,128)(2,1)} fusion(bf16[2,1,2,256,128]{4,3,2,1,0:T(8,128)(2,1)} %param.7), kind=kLoop, calls=%fused_computation.84 | loop fusion | flops 32768 | bytes 131072 | tf_op jit(solution)/shard_map/neg | solution.py:17
  82.0 2.6 %fusion.19 = f32[3,256,512]{2,1,0:T(8,128)} fusion(bf16[3,256,256]{1,2,0:T(8,128)(2,1)} %reduce-scatter.2.cloned.1.call-done, bf16[128,256]{1,0:T(8,128)(2,1)} %get-tuple-element.24, bf16[128,256]{1,0:T(8,128)(2,1)} %get-tuple-element.26, bf16[128,256]{1,0:T(8,128)(2,1)} %get-tuple-element.23), kind=kOutput, calls=%fused_computation.26 | convolution fusion | flops 202375168 | bytes 2162688 | tf_op jit(solution)/shard_map/prk,ks->prs/dot_general | solution.py:53
  84.6 13.9 %collective-permute-done = bf16[3,256,256]{1,2,0:T(8,128)(2,1)} collective-permute-done((bf16[3,256,256]{1,2,0:T(8,128)(2,1)}, bf16[3,256,256]{1,2,0:T(8,128)(2,1)}, u32[]{:S(2)}, u32[]{:S(2)}) %collective-permute-start) | collective-permute-done | bytes 393248 | tf_op jit(solution)/shard_map/ppermute | solution.py:12
  98.5 3.1 %fusion.16 = bf16[3,256,256]{2,1,0:T(8,128)(2,1)} fusion(f32[3,256,512]{2,1,0:T(8,128)} %fusion.19, bf16[3,256,256]{1,2,0:T(8,128)(2,1)} %collective-permute-done, bf16[128,256]{1,0:T(8,128)(2,1)} %get-tuple-element.22, bf16[128,256]{1,0:T(8,128)(2,1)} %get-tuple-element.25, bf16[128,256]{1,0:T(8,128)(2,1)} %get-tuple-element.21, ...), kind=kOutput, calls=%fused_computation.19 | convolution fusion | flops 405733376 | bytes 2752512 | tf_op jit(solution)/shard_map/prs,sk->prk/dot_general | solution.py:46
  101.6 0.5 collective-permute-start.1
  102.1 1.4 %fusion.44 = f32[3,256,512]{2,1,0:T(8,128)S(1)} fusion(bf16[3,256,256]{2,1,0:T(8,128)(2,1)} %fusion.16, bf16[128,256]{1,0:T(8,128)(2,1)} %get-tuple-element.14, bf16[128,256]{1,0:T(8,128)(2,1)S(1)} %get-tuple-element.16, bf16[128,256]{1,0:T(8,128)(2,1)} %get-tuple-element.13), kind=kOutput, calls=%fused_computation.48 | convolution fusion | flops 202375168 | bytes 2162688 | tf_op jit(solution)/shard_map/prk,ks->prs/dot_general | solution.py:53
  103.5 8.4 %collective-permute-done.1 = bf16[3,256,256]{2,1,0:T(8,128)(2,1)S(1)} collective-permute-done((bf16[3,256,256]{2,1,0:T(8,128)(2,1)}, bf16[3,256,256]{2,1,0:T(8,128)(2,1)S(1)}, u32[]{:S(2)}, u32[]{:S(2)}) %collective-permute-start.1) | collective-permute-done | bytes 393248 | tf_op jit(solution)/shard_map/ppermute | solution.py:12
  111.9 0.5 multiply_reduce_fusion
  112.4 0.2 broadcast_multiply_fusion
  112.6 0.1 fusion.18
  112.7 1.2 %pad_maximum_fusion = f32[2,3,256,256]{3,2,1,0:T(8,128)} fusion(f32[1,3,256,256]{3,2,1,0:T(8,128)S(1)} %get-tuple-element.8, f32[1,3,256,256]{3,2,1,0:T(8,128)S(1)} %get-tuple-element.7), kind=kLoop, calls=%fused_computation.14 | loop fusion | flops 393216 | bytes 3145728 | tf_op jit(solution)/shard_map/stack | solution.py:60
  (8 shorter events, 0.1 us)
Async XLA Ops:
  6.5 2.0 %copy-start = (bf16[3,2048,256]{2,1,0:T(8,128)(2,1)S(1)}, bf16[3,2048,256]{2,1,0:T(8,128)(2,1)}, u32[]{:S(2)}) copy-start(bf16[3,2048,256]{2,1,0:T(8,128)(2,1)} %param.6) | copy-start | bytes 9437188
  6.5 71.6 %reduce-scatter.2.cloned.1.call-start = ((), (), s32[]{:S(2)}) async-start(), calls=%async_computation.1 | async-start | bytes 3538944 | tf_op jit(solution)/shard_map/reduce_scatter | solution.py:35
  78.2 20.3 %collective-permute-start = (bf16[3,256,256]{1,2,0:T(8,128)(2,1)}, bf16[3,256,256]{1,2,0:T(8,128)(2,1)}, u32[]{:S(2)}, u32[]{:S(2)}) collective-permute-start(bf16[3,256,256]{1,2,0:T(8,128)(2,1)} %reduce-scatter.2.cloned.1.call-done), channel_id=1, source_target_pairs={{0,16},{8,24},{16,0},{24,8},{1,17},{9,25},{17,1},{25,9},{2,18},{10... | collective-permute-start | bytes 1179656 | tf_op jit(solution)/shard_map/ppermute | solution.py:12
  101.6 10.3 %collective-permute-start.1 = (bf16[3,256,256]{2,1,0:T(8,128)(2,1)}, bf16[3,256,256]{2,1,0:T(8,128)(2,1)S(1)}, u32[]{:S(2)}, u32[]{:S(2)}) collective-permute-start(bf16[3,256,256]{2,1,0:T(8,128)(2,1)} %fusion.16), channel_id=1, source_target_pairs={{0,8},{8,0},{16,24},{24,16},{1,9},{9,1},{17,25},{25,17},{2,10},{10... | collective-permute-start | bytes 1179656 | tf_op jit(solution)/shard_map/ppermute | solution.py:12
  111.9 0.7 copy-start.1
Sparse Core Ops, SparseCore 0:
  29.4 48.7 reduce-scatter.1
where the time goes:
time: 121 us
  waiting for transfers between devices  68.1 us (56%)
  matrix products  28 us (23%)
  between operations  13.5 us (11%)
  local copies, waits for them, and re-layouts  4.46 us (4%)
  other arithmetic  3.93 us (3%)
  starting transfers between devices  2.87 us (2%)
    reduce_scatter x1, waiting for transfers between devices, shards(): lax.psum_scatter(partial_value.astype(jnp.bfloat16), 'sk', scatter_dimens...  45.8 us
    ppermute x2, waiting for transfers between devices, swapped(): return lax.ppermute(value, axis, pairs)  22.3 us
    dot_general x1, matrix products, shards(): jnp.einsum('rc,pck->prk', kernel[0], sk_proj, preferred_element_type=jnp....  10.3 us
    dot_general x1, matrix products, shards(): jnp.einsum('rc,pck->prk', kernel[1], turned, preferred_element_type=jnp.f...  9.11 us
    dot_general x2, matrix products, shards(): jnp.einsum('prk,ks->prs', own_proj, own_mat, preferred_element_type=jnp.f...  3.96 us
    dot_general x1, matrix products, shards(): jnp.einsum('prs,sk->prk', rounded, level_mat, preferred_element_type=jnp....  3.15 us
    squeeze x3, local copies, waits for them, and re-layouts, complex_block(): upper = jnp.concatenate([matrix[0], matrix[1]], axis=1)  3.13 us
    ppermute x2, starting transfers between devices, swapped(): return lax.ppermute(value, axis, pairs)  2.87 us
  transfers between devices with their start and end apart: 3, of which 3 were waited for; matrix products, arithmetic and copies ran while one was open for 7% of the time, Pallas kernels for 0%

commit v1 on v0

v1 whole, which is shorter than its diff:
```python
import functools
import jax
import jax.numpy as jnp
from jax import lax
from jax.experimental import pallas as pl
from jax.experimental.pallas import tpu as pltpu
from jax.sharding import PartitionSpec as P

epsilon = 1e-06
chunk_count = 4
depth_steps = 4
vmem_bytes = 56 * 1024 * 1024


def swapped(value, axis, mask):
    pairs = [(source, source ^ mask) for source in range(lax.axis_size(axis))]
    return lax.ppermute(value, axis, pairs)


def product(left, right):
    return lax.dot_general(left, right, (((1,), (0,)), ((), ())), preferred_element_type=jnp.float32)


def params():
    return pltpu.CompilerParams(vmem_limit_bytes=vmem_bytes)


def whole(shape):
    return pl.BlockSpec(shape, lambda *_: (0,) * len(shape))


def write_pieces(place_ref, acc_ref, keep_ref, send_ref, segments, chunk_rows, passes, rank):
    place = place_ref[0]
    for turn in range(segments):
        target = place ^ turn
        out_ref = send_ref if turn % 2 else keep_ref
        upper = acc_ref[pl.ds(pl.multiple_of(target * chunk_rows, chunk_rows), chunk_rows), :]
        lower = acc_ref[
            pl.ds(pl.multiple_of((segments + target) * chunk_rows, chunk_rows), chunk_rows), :
        ]
        for one in range(passes):
            re = slice(2 * one * rank, (2 * one + 1) * rank)
            im = slice((2 * one + 1) * rank, (2 * one + 2) * rank)
            out_ref[turn // 2, one, :, :rank] = (upper[:, re] - lower[:, im]).astype(jnp.bfloat16)
            out_ref[turn // 2, one, :, rank:] = (upper[:, im] + lower[:, re]).astype(jnp.bfloat16)


def gather_block(step, kernel_ref, value, acc_ref):
    block = kernel_ref[...].reshape(-1, kernel_ref.shape[3])
    part = product(block, value)

    @pl.when(step == 0)
    def _():
        acc_ref[...] = part

    @pl.when(step != 0)
    def _():
        acc_ref[...] += part


def first_body(place_ref, kernel_ref, sketch_ref, proj_ref, keep_ref, send_ref, sk_ref, acc_ref, *, sizes):
    segments, chunk_rows, passes, rank = sizes
    step = pl.program_id(0)
    both = jnp.concatenate([proj_ref[0, 0, 0], proj_ref[0, 0, 1]], axis=1)
    for one in range(passes):
        cols = slice(2 * one * rank, 2 * (one + 1) * rank)
        sk_ref[:, cols] = product(sketch_ref[one], both).astype(jnp.bfloat16)
    gather_block(step, kernel_ref, sk_ref[...], acc_ref)

    @pl.when(step == pl.num_programs(0) - 1)
    def _():
        write_pieces(place_ref, acc_ref, keep_ref, send_ref, segments, chunk_rows, passes, rank)


def later_body(place_ref, kernel_ref, sk_ref, keep_ref, send_ref, acc_ref, *, sizes):
    segments, chunk_rows, passes, rank = sizes
    step = pl.program_id(0)
    gather_block(step, kernel_ref, sk_ref[...], acc_ref)

    @pl.when(step == pl.num_programs(0) - 1)
    def _():
        write_pieces(place_ref, acc_ref, keep_ref, send_ref, segments, chunk_rows, passes, rank)


def gathered(place, kernel, chunk, chunk_rows, sketch, first_proj, sk_value):
    _, segments, _, cols = kernel.shape
    passes, _, sketch_cols = sketch.shape
    rank = first_proj.shape[4]
    width = 2 * passes * rank
    deep = cols // depth_steps
    sizes = (segments, chunk_rows, passes, rank)
    piece = jax.ShapeDtypeStruct((segments // 2, passes, chunk_rows, 2 * rank), jnp.bfloat16)
    place_spec = pl.BlockSpec(memory_space=pltpu.SMEM)
    kernel_spec = pl.BlockSpec((2, segments, chunk_rows, deep), lambda k: (0, 0, chunk, k))
    scratch = [pltpu.VMEM((2 * segments * chunk_rows, width), jnp.float32)]
    cost = pl.CostEstimate(
        flops=4 * segments * chunk_rows * cols * width,
        bytes_accessed=4 * segments * chunk_rows * cols + 2 * cols * width,
        transcendentals=0,
    )
    if sk_value is None:
        return pl.pallas_call(
            functools.partial(first_body, sizes=sizes),
            name="gather_first",
            grid=(depth_steps,),
            in_specs=[
                place_spec,
                kernel_spec,
                pl.BlockSpec((passes, deep, sketch_cols), lambda k: (0, k, 0)),
                pl.BlockSpec((1, 1, 2, sketch_cols, rank), lambda k: (0, 0, 0, 0, 0)),
            ],
            out_specs=[whole(piece.shape), whole(piece.shape), pl.BlockSpec((deep, width), lambda k: (k, 0))],
            out_shape=[piece, piece, jax.ShapeDtypeStruct((cols, width), jnp.bfloat16)],
            scratch_shapes=scratch,
            compiler_params=params(),
            cost_estimate=cost,
        )(place, kernel, sketch, first_proj)
    return pl.pallas_call(
        functools.partial(later_body, sizes=sizes),
        name="gather_later",
        grid=(depth_steps,),
        in_specs=[place_spec, kernel_spec, pl.BlockSpec((deep, width), lambda k: (k, 0))],
        out_specs=[whole(piece.shape), whole(piece.shape)],
        out_shape=[piece, piece],
        scratch_shapes=scratch,
        compiler_params=params(),
        cost_estimate=cost,
    )(place, kernel, sk_value)


def weights_body(proj_ref, inv_ref, *out_refs):
    levels = proj_ref.shape[0]
    rank = proj_ref.shape[4]
    for level in range(levels):
        for half in range(2):
            rows = slice(half * rank, (half + 1) * rank)
            re = inv_ref[level, 0, 0, rows, :]
            im = inv_ref[level, 0, 1, rows, :]
            if level + 1 < levels:
                next_re = proj_ref[level + 1, 0, 0]
                next_im = proj_ref[level + 1, 0, 1]
                re, im = (
                    (product(re, next_re) - product(im, next_im)).astype(jnp.bfloat16),
                    (product(re, next_im) + product(im, next_re)).astype(jnp.bfloat16),
                )
            cols = re.shape[1]
            out_refs[level][half * 2 * rank : half * 2 * rank + rank, :cols] = re
            out_refs[level][half * 2 * rank : half * 2 * rank + rank, cols:] = im
            out_refs[level][half * 2 * rank + rank : (half + 1) * 2 * rank, :cols] = -im
            out_refs[level][half * 2 * rank + rank : (half + 1) * 2 * rank, cols:] = re


def level_weights(projections, inverses):
    levels = projections.shape[0]
    rank = projections.shape[4]
    sketch_cols = inverses.shape[4]
    shapes = [
        jax.ShapeDtypeStruct((4 * rank, 2 * (rank if level + 1 < levels else sketch_cols)), jnp.bfloat16)
        for level in range(levels)
    ]
    return pl.pallas_call(
        weights_body, name="level_weights", out_shape=shapes, compiler_params=params()
    )(projections, inverses)


def paired(own_ref, partner_ref, weight_ref):
    width = own_ref.shape[2]
    own = own_ref[...].reshape(-1, width)
    partner = partner_ref[...].reshape(-1, width)
    return product(own, weight_ref[:width, :]) + product(partner, weight_ref[width:, :])


def middle_body(own_ref, partner_ref, weight_ref, out_ref):
    out_ref[...] = paired(own_ref, partner_ref, weight_ref).astype(jnp.bfloat16).reshape(out_ref.shape)


def middle_level(own, partner, weight):
    return pl.pallas_call(
        middle_body,
        name="middle_level",
        out_shape=jax.ShapeDtypeStruct(own.shape, jnp.bfloat16),
        compiler_params=params(),
    )(own, partner, weight)


def final_body(own_ref, partner_ref, weight_ref, gain_ref, *rest):
    out_ref = rest[-1]
    current = paired(own_ref, partner_ref, weight_ref)
    sketch_cols = gain_ref.shape[1]
    power = jnp.sum(current * current, axis=-1, keepdims=True) / sketch_cols
    scale = lax.rsqrt(power + epsilon)
    shape = out_ref.shape[1:]
    gain = gain_ref[...]
    out_ref[0] = (current[:, :sketch_cols] * scale * gain).reshape(shape)
    out_ref[1] = (current[:, sketch_cols:] * scale * gain).reshape(shape)


def final_level(own, partner, weight, gain, out, chunk, segment_rows):
    passes, chunk_rows, _ = own.shape
    sketch_cols = gain.shape[1]
    operands = [own, partner, weight, gain]
    specs = [whole(value.shape) for value in operands]
    aliases = {}
    if out is not None:
        operands.append(out)
        specs.append(pl.BlockSpec(memory_space=pl.ANY))
        aliases = {4: 0}
    return pl.pallas_call(
        final_body,
        name="final_level",
        grid=(1,),
        in_specs=specs,
        out_specs=pl.BlockSpec((2, passes, chunk_rows, sketch_cols), lambda i: (0, 0, chunk, 0)),
        out_shape=jax.ShapeDtypeStruct((2, passes, segment_rows, sketch_cols), jnp.float32),
        input_output_aliases=aliases,
        compiler_params=params(),
    )(*operands)


def shards(kernel, sketch, projections, inverses, norm_gain):
    members = lax.axis_size("sk")
    levels = projections.shape[0]
    top_bits = lax.axis_size("bf").bit_length() - 1
    _, rows, cols = kernel.shape
    segment_rows = rows // members
    chunk_rows = segment_rows // chunk_count
    kernel = kernel.reshape(2, members, segment_rows, cols)
    place = lax.axis_index("sk").reshape(1).astype(jnp.int32)
    gain = norm_gain.reshape(1, -1)
    weights = level_weights(projections, inverses)
    out = None
    sk_value = None
    for chunk in range(chunk_count):
        results = gathered(place, kernel, chunk, chunk_rows, sketch, projections, sk_value)
        keep, send = results[:2]
        if sk_value is None:
            sk_value = results[2]
        both = keep.astype(jnp.float32) + swapped(send, "sk", 1).astype(jnp.float32)
        own = both[0]
        for turn in range(1, members // 2):
            own = own + swapped(both[turn].astype(jnp.bfloat16), "sk", 2 * turn).astype(jnp.float32)
        own = own.astype(jnp.bfloat16)
        for level in range(levels):
            partner = swapped(own, "bf", 2 ** (top_bits - 1 - level))
            if level + 1 < levels:
                own = middle_level(own, partner, weights[level])
            else:
                out = final_level(own, partner, weights[level], gain, out, chunk, segment_rows)
    return out


def solution(mesh):
    placed = (
        P(None, "bf", "sk"),
        P(None, "sk", None),
        P(None, "bf", None, None, None),
        P(None, "bf", None, None, None),
        P(),
    )
    return jax.shard_map(
        shards,
        mesh=mesh,
        in_specs=placed,
        out_specs=P(None, None, ("bf", "sk"), None),
        check_vma=False,
    )
```

time: 121 us -> 93.1 us (0.77)
  waiting for transfers between devices: 68.1 us -> 5.68 us
  Pallas kernels: 0 us -> 50.9 us
  matrix products: 28 us -> 0 us
  starting transfers between devices: 2.87 us -> 29.9 us
  between operations: 13.5 us -> 0.22 us
  other arithmetic: 3.93 us -> 0.65 us
    pallas_call x0 -> x13, Pallas kernels: none -> 50.9 us  [the longest x3 23 us: gathered(): pl.pallas_call(functools.partial(later_body, sizes=sizes), name='gather_l...]
    reduce_scatter x1 -> x0, waiting for transfers between devices: 45.8 us -> none  [shards(): lax.psum_scatter(partial_value.astype(jnp.bfloat16), 'sk', scatter_dimens...]
    dot_general x7 -> x0, matrix products: 28 us -> none  [the longest x1 10.3 us: shards(): jnp.einsum('rc,pck->prk', kernel[0], sk_proj, preferred_element_type=jnp....]
    ppermute x2 -> x24, starting transfers between devices: 2.87 us -> 29.9 us  [swapped(): return lax.ppermute(value, axis, pairs)]
    ppermute x2 -> x24, waiting for transfers between devices: 22.3 us -> 5.68 us  [swapped(): return lax.ppermute(value, axis, pairs)]
    unnamed x6 -> x32, local copies, waits for them, and re-layouts: 0.26 us -> 5.17 us
    squeeze x4 -> x0, local copies, waits for them, and re-layouts: 4.2 us -> none  [the longest x3 3.13 us: complex_block(): upper = jnp.concatenate([matrix[0], matrix[1]], axis=1)]
    neg x4 -> x0, other arithmetic: 2.37 us -> none  [the longest x3 2.16 us: complex_block(): lower = jnp.concatenate([-matrix[1], matrix[0]], axis=1)]
  transfers between devices with their start and end apart: 3 -> 24, of which waited for: 3 -> 4; matrix products, arithmetic and copies ran while one was open for 7% -> 1% of each run, Pallas kernels for 0% -> 43%
where the time goes in v1:
time: 93.1 us; the launch traced here: 92.5 us
  Pallas kernels  50.9 us (55%)
  starting transfers between devices  29.9 us (32%)
  waiting for transfers between devices  5.68 us (6%)
  local copies, waits for them, and re-layouts  5.25 us (6%)
    ppermute x24, starting transfers between devices, swapped(): return lax.ppermute(value, axis, pairs)  29.9 us
    pallas_call x3, Pallas kernels, gathered(): pl.pallas_call(functools.partial(later_body, sizes=sizes), name='gather_l...  23 us
    pallas_call x4, Pallas kernels, final_level(): pl.pallas_call(final_body, name='final_level', grid=(1,), in_specs=specs,...  9 us
    pallas_call x1, Pallas kernels, gathered(): pl.pallas_call(functools.partial(first_body, sizes=sizes), name='gather_f...  8.98 us
    pallas_call x4, Pallas kernels, middle_level(): pl.pallas_call(middle_body, name='middle_level', out_shape=jax.ShapeDtype...  7.61 us
    ppermute x24, waiting for transfers between devices, swapped(): return lax.ppermute(value, axis, pairs)  5.68 us
    unnamed x32, local copies, waits for them, and re-layouts  5.17 us
    pallas_call x1, Pallas kernels, level_weights(): pl.pallas_call(weights_body, name='level_weights', out_shape=shapes, comp...  2.25 us
  transfers between devices with their start and end apart: 24, of which 4 were waited for; matrix products, arithmetic and copies ran while one was open for 1% of the time, Pallas kernels for 43%

profile of v1, /device:TPU:0, one launch (start us, length us, event | category | flops | bytes accessed | tf_op | source)
XLA Modules:
  0.0 92.5 jit_solution(4198330912273786069)
XLA Ops:
  0.0 9.0 %gather_first.1 = (bf16[4,3,64,256]{3,2,1,0:T(8,128)(2,1)}, bf16[4,3,64,256]{3,2,1,0:T(8,128)(2,1)}, bf16[2048,768]{1,0:T(8,128)(2,1)}) custom-call(s32[1]{0:T(128)} %bitcast.place_ref, bf16[2,8,256,2048]{3,2,1,0:T(8,128)(2,1)} %bitcast.67, bf16[3,2048,256]{2,1,0:T(8,128)(2,1)} %sketch_ref.1, bf16[2,1,2,256,128]{4,3,2,1,0:T(8,128)(2,1)} %proj_ref.3), custom_call_target="tpu_custom_call" | custom-call | flops 3221225472 | bytes 7340032 | tf_op jit(solution)/shard_map/gather_first/pallas_call | solution.py:102
  9.5 7.7 %gather_later.5 = (bf16[4,3,64,256]{3,2,1,0:T(8,128)(2,1)}, bf16[4,3,64,256]{3,2,1,0:T(8,128)(2,1)}) custom-call(s32[1]{0:T(128)} %bitcast.place_ref, bf16[2,8,256,2048]{3,2,1,0:T(8,128)(2,1)} %bitcast.68, bf16[2048,768]{1,0:T(8,128)(2,1)} %get-tuple-element.16.sk_ref), custom_call_target="tpu_custom_call" | custom-call | flops 3221225472 | bytes 7340032 | tf_op jit(solution)/shard_map/gather_later/pallas_call | solution.py:118
  17.2 7.7 %gather_later.4 = (bf16[4,3,64,256]{3,2,1,0:T(8,128)(2,1)}, bf16[4,3,64,256]{3,2,1,0:T(8,128)(2,1)}) custom-call(s32[1]{0:T(128)} %bitcast.place_ref, bf16[2,8,256,2048]{3,2,1,0:T(8,128)(2,1)} %bitcast.69, bf16[2048,768]{1,0:T(8,128)(2,1)} %get-tuple-element.16.sk_ref), custom_call_target="tpu_custom_call" | custom-call | flops 3221225472 | bytes 7340032 | tf_op jit(solution)/shard_map/gather_later/pallas_call | solution.py:118
  25.4 7.7 %gather_later.3 = (bf16[4,3,64,256]{3,2,1,0:T(8,128)(2,1)}, bf16[4,3,64,256]{3,2,1,0:T(8,128)(2,1)}) custom-call(s32[1]{0:T(128)} %bitcast.place_ref, bf16[2,8,256,2048]{3,2,1,0:T(8,128)(2,1)} %bitcast.70, bf16[2048,768]{1,0:T(8,128)(2,1)} %get-tuple-element.16.sk_ref), custom_call_target="tpu_custom_call" | custom-call | flops 3221225472 | bytes 7340032 | tf_op jit(solution)/shard_map/gather_later/pallas_call | solution.py:118
  33.3 3.0 %collective-permute-start.19 = (bf16[3,64,256]{2,1,0:T(8,128)(2,1)S(1)}, bf16[3,64,256]{2,1,0:T(8,128)(2,1)S(1)}, u32[]{:S(2)}, u32[]{:S(2)}) collective-permute-start(bf16[3,64,256]{2,1,0:T(8,128)(2,1)S(1)} %get-tuple-element.35), channel_id=1, source_target_pairs={{0,2},{1,3},{2,0},{3,1},{4,6},{5,7},{6,4},{7,5},{8,10},{9,11},{10,... | collective-permute-start | bytes 294920 | tf_op jit(solution)/shard_map/ppermute | solution.py:17
  38.0 2.0 %collective-permute-start.13 = (bf16[3,64,256]{2,1,0:T(8,128)(2,1)S(1)}, bf16[3,64,256]{2,1,0:T(8,128)(2,1)S(1)}, u32[]{:S(2)}, u32[]{:S(2)}) collective-permute-start(bf16[3,64,256]{2,1,0:T(8,128)(2,1)S(1)} %get-tuple-element.38), channel_id=1, source_target_pairs={{0,2},{1,3},{2,0},{3,1},{4,6},{5,7},{6,4},{7,5},{8,10},{9,11},{10,... | collective-permute-start | bytes 294920 | tf_op jit(solution)/shard_map/ppermute | solution.py:17
  40.1 1.6 %collective-permute-start.15 = (bf16[3,64,256]{2,1,0:T(8,128)(2,1)S(1)}, bf16[3,64,256]{2,1,0:T(8,128)(2,1)S(1)}, u32[]{:S(2)}, u32[]{:S(2)}) collective-permute-start(bf16[3,64,256]{2,1,0:T(8,128)(2,1)S(1)} %get-tuple-element.39), channel_id=1, source_target_pairs={{0,6},{1,7},{2,4},{3,5},{4,2},{5,3},{6,0},{7,1},{8,14},{9,15},{10,... | collective-permute-start | bytes 294920 | tf_op jit(solution)/shard_map/ppermute | solution.py:17
  46.7 1.6 %collective-permute-start.8 = (bf16[3,64,256]{2,1,0:T(8,128)(2,1)S(1)}, bf16[3,64,256]{2,1,0:T(8,128)(2,1)S(1)}, u32[]{:S(2)}, u32[]{:S(2)}) collective-permute-start(bf16[3,64,256]{2,1,0:T(8,128)(2,1)S(1)} %get-tuple-element.43), channel_id=1, source_target_pairs={{0,4},{1,5},{2,6},{3,7},{4,0},{5,1},{6,2},{7,3},{8,12},{9,13},{10,... | collective-permute-start | bytes 294920 | tf_op jit(solution)/shard_map/ppermute | solution.py:17
  49.7 1.6 %collective-permute-start.3 = (bf16[3,64,256]{2,1,0:T(8,128)(2,1)S(1)}, bf16[3,64,256]{2,1,0:T(8,128)(2,1)S(1)}, u32[]{:S(2)}, u32[]{:S(2)}) collective-permute-start(bf16[3,64,256]{2,1,0:T(8,128)(2,1)S(1)} %get-tuple-element.45), channel_id=1, source_target_pairs={{0,6},{1,7},{2,4},{3,5},{4,2},{5,3},{6,0},{7,1},{8,14},{9,15},{10,... | collective-permute-start | bytes 294920 | tf_op jit(solution)/shard_map/ppermute | solution.py:17
  52.8 2.6 %collective-permute-start.22 = (bf16[3,64,256]{2,1,0:T(8,128)(2,1)S(1)}, bf16[3,64,256]{2,1,0:T(8,128)(2,1)S(1)}, u32[]{:S(2)}, u32[]{:S(2)}) collective-permute-start(bf16[3,64,256]{2,1,0:T(8,128)(2,1)S(1)} %fusion.3.own_ref), channel_id=1, source_target_pairs={{0,16},{8,24},{16,0},{24,8},{1,17},{9,25},{17,1},{25,9},{2,18},{10... | collective-permute-start | bytes 294920 | tf_op jit(solution)/shard_map/ppermute | solution.py:17
  55.4 2.5 %collective-permute-start.16 = (bf16[3,64,256]{2,1,0:T(8,128)(2,1)S(1)}, bf16[3,64,256]{2,1,0:T(8,128)(2,1)S(1)}, u32[]{:S(2)}, u32[]{:S(2)}) collective-permute-start(bf16[3,64,256]{2,1,0:T(8,128)(2,1)S(1)} %fusion.7.own_ref), channel_id=1, source_target_pairs={{0,16},{8,24},{16,0},{24,8},{1,17},{9,25},{17,1},{25,9},{2,18},{10... | collective-permute-start | bytes 294920 | tf_op jit(solution)/shard_map/ppermute | solution.py:17
  58.5 2.5 %collective-permute-start.4 = (bf16[3,64,256]{2,1,0:T(8,128)(2,1)S(1)}, bf16[3,64,256]{2,1,0:T(8,128)(2,1)S(1)}, u32[]{:S(2)}, u32[]{:S(2)}) collective-permute-start(bf16[3,64,256]{2,1,0:T(8,128)(2,1)S(1)} %fusion.15.own_ref), channel_id=1, source_target_pairs={{0,16},{8,24},{16,0},{24,8},{1,17},{9,25},{17,1},{25,9},{2,18},{10... | collective-permute-start | bytes 294920 | tf_op jit(solution)/shard_map/ppermute | solution.py:17
  61.0 2.3 %level_weights.1 = (bf16[512,256]{1,0:T(8,128)(2,1)}, bf16[512,512]{1,0:T(8,128)(2,1)}) custom-call(bf16[2,1,2,256,128]{4,3,2,1,0:T(8,128)(2,1)} %proj_ref.3, bf16[2,1,2,256,256]{4,3,2,1,0:T(8,128)(2,1)} %inv_ref.1), custom_call_target="tpu_custom_call" | custom-call | tf_op jit(solution)/shard_map/level_weights/pallas_call | solution.py:161
  63.3 3.4 %collective-permute-done.22.partner_ref = bf16[3,64,256]{2,1,0:T(8,128)(2,1)S(1)} collective-permute-done((bf16[3,64,256]{2,1,0:T(8,128)(2,1)S(1)}, bf16[3,64,256]{2,1,0:T(8,128)(2,1)S(1)}, u32[]{:S(2)}, u32[]{:S(2)}) %collective-permute-start.22) | collective-permute-done | bytes 98336 | tf_op jit(solution)/shard_map/ppermute | solution.py:17
  67.3 1.9 %middle_level.7.own_ref = bf16[3,64,256]{2,1,0:T(8,128)(2,1)} custom-call(bf16[3,64,256]{2,1,0:T(8,128)(2,1)} %copy-done, bf16[3,64,256]{2,1,0:T(8,128)(2,1)} %copy-done.10, bf16[512,256]{1,0:T(8,128)(2,1)} %get-tuple-element.19.weight_ref), custom_call_target="tpu_custom_call" | custom-call | tf_op jit(solution)/shard_map/middle_level/pallas_call | solution.py:178
  69.9 1.9 %middle_level.6.own_ref = bf16[3,64,256]{2,1,0:T(8,128)(2,1)} custom-call(bf16[3,64,256]{2,1,0:T(8,128)(2,1)} %copy-done.1, bf16[3,64,256]{2,1,0:T(8,128)(2,1)} %copy-done.9, bf16[512,256]{1,0:T(8,128)(2,1)} %get-tuple-element.19.weight_ref), custom_call_target="tpu_custom_call" | custom-call | tf_op jit(solution)/shard_map/middle_level/pallas_call | solution.py:178
  71.8 2.0 %collective-permute-start.17 = (bf16[3,64,256]{2,1,0:T(8,128)(2,1)}, bf16[3,64,256]{2,1,0:T(8,128)(2,1)S(1)}, u32[]{:S(2)}, u32[]{:S(2)}) collective-permute-start(bf16[3,64,256]{2,1,0:T(8,128)(2,1)} %middle_level.6.own_ref), channel_id=1, source_target_pairs={{0,8},{8,0},{16,24},{24,16},{1,9},{9,1},{17,25},{25,17},{2,10},{10... | collective-permute-start | bytes 294920 | tf_op jit(solution)/shard_map/ppermute | solution.py:17
  74.4 1.9 %middle_level.5.own_ref = bf16[3,64,256]{2,1,0:T(8,128)(2,1)} custom-call(bf16[3,64,256]{2,1,0:T(8,128)(2,1)} %copy-done.2, bf16[3,64,256]{2,1,0:T(8,128)(2,1)} %copy-done.11, bf16[512,256]{1,0:T(8,128)(2,1)} %get-tuple-element.19.weight_ref), custom_call_target="tpu_custom_call" | custom-call | tf_op jit(solution)/shard_map/middle_level/pallas_call | solution.py:178
  77.0 1.9 %middle_level.4.own_ref = bf16[3,64,256]{2,1,0:T(8,128)(2,1)} custom-call(bf16[3,64,256]{2,1,0:T(8,128)(2,1)} %copy-done.3, bf16[3,64,256]{2,1,0:T(8,128)(2,1)} %copy-done.12, bf16[512,256]{1,0:T(8,128)(2,1)} %get-tuple-element.19.weight_ref), custom_call_target="tpu_custom_call" | custom-call | tf_op jit(solution)/shard_map/middle_level/pallas_call | solution.py:178
  78.9 2.0 %collective-permute-start.5 = (bf16[3,64,256]{2,1,0:T(8,128)(2,1)}, bf16[3,64,256]{2,1,0:T(8,128)(2,1)S(1)}, u32[]{:S(2)}, u32[]{:S(2)}) collective-permute-start(bf16[3,64,256]{2,1,0:T(8,128)(2,1)} %middle_level.4.own_ref), channel_id=1, source_target_pairs={{0,8},{8,0},{16,24},{24,16},{1,9},{9,1},{17,25},{25,17},{2,10},{10... | collective-permute-start | bytes 294920 | tf_op jit(solution)/shard_map/ppermute | solution.py:17
  81.6 2.3 %final_level.4.rest_0_ = f32[2,3,256,256]{3,2,1,0:T(8,128)} custom-call(bf16[3,64,256]{2,1,0:T(8,128)(2,1)} %middle_level.7.own_ref, bf16[3,64,256]{2,1,0:T(8,128)(2,1)} %copy-done.8, bf16[512,512]{1,0:T(8,128)(2,1)} %get-tuple-element.20.weight_ref, f32[1,256]{1,0:T(1,128)} %bitcast.71), custom_call_target="tpu_custom_call" | custom-call | tf_op jit(solution)/shard_map/final_level/pallas_call | solution.py:208
  84.5 2.3 %final_level.5.rest_0_ = f32[2,3,256,256]{3,2,1,0:T(8,128)} custom-call(bf16[3,64,256]{2,1,0:T(8,128)(2,1)} %middle_level.6.own_ref, bf16[3,64,256]{2,1,0:T(8,128)(2,1)} %copy-done.13, bf16[512,512]{1,0:T(8,128)(2,1)} %get-tuple-element.20.weight_ref, f32[1,256]{1,0:T(1,128)} %bitcast.72, ...), custom_call_target="tpu_custom_call", output_to_operand_aliasing={{}: (4, {})} | custom-call | tf_op jit(solution)/shard_map/final_level/pallas_call | solution.py:208
  87.4 2.3 %final_level.6.rest_0_ = f32[2,3,256,256]{3,2,1,0:T(8,128)} custom-call(bf16[3,64,256]{2,1,0:T(8,128)(2,1)} %middle_level.5.own_ref, bf16[3,64,256]{2,1,0:T(8,128)(2,1)} %copy-done.14, bf16[512,512]{1,0:T(8,128)(2,1)} %get-tuple-element.20.weight_ref, f32[1,256]{1,0:T(1,128)} %bitcast.73, ...), custom_call_target="tpu_custom_call", output_to_operand_aliasing={{}: (4, {})} | custom-call | tf_op jit(solution)/shard_map/final_level/pallas_call | solution.py:208
  90.3 2.3 %final_level.7 = f32[2,3,256,256]{3,2,1,0:T(8,128)} custom-call(bf16[3,64,256]{2,1,0:T(8,128)(2,1)} %middle_level.4.own_ref, bf16[3,64,256]{2,1,0:T(8,128)(2,1)} %copy-done.15, bf16[512,512]{1,0:T(8,128)(2,1)} %get-tuple-element.20.weight_ref, f32[1,256]{1,0:T(1,128)} %bitcast.74, f32[2,3,256,256]{3,2,1,0:T(8,128)} %final_level.6.rest_0_), custom_call_target="tpu_custom_call", output_to_operand_aliasing={{}: (4, {})} | custom-call | tf_op jit(solution)/shard_map/final_level/pallas_call | solution.py:208
  (81 shorter events, 16.7 us)
Async XLA Ops:
  9.0 24.1 %collective-permute-start.18 = (bf16[4,3,64,256]{3,2,1,0:T(8,128)(2,1)}, bf16[4,3,64,256]{3,2,1,0:T(8,128)(2,1)S(1)}, u32[]{:S(2)}, u32[]{:S(2)}) collective-permute-start(bf16[4,3,64,256]{3,2,1,0:T(8,128)(2,1)} %get-tuple-element.26), channel_id=1, source_target_pairs={{0,1},{1,0},{2,3},{3,2},{4,5},{5,4},{6,7},{7,6},{8,9},{9,8},{10,11... | collective-permute-start | bytes 1179656 | tf_op jit(solution)/shard_map/ppermute | solution.py:17
  17.1 20.6 %collective-permute-start.12 = (bf16[4,3,64,256]{3,2,1,0:T(8,128)(2,1)}, bf16[4,3,64,256]{3,2,1,0:T(8,128)(2,1)S(1)}, u32[]{:S(2)}, u32[]{:S(2)}) collective-permute-start(bf16[4,3,64,256]{3,2,1,0:T(8,128)(2,1)} %get-tuple-element.24), channel_id=1, source_target_pairs={{0,1},{1,0},{2,3},{3,2},{4,5},{5,4},{6,7},{7,6},{8,9},{9,8},{10,11... | collective-permute-start | bytes 1179656 | tf_op jit(solution)/shard_map/ppermute | solution.py:17
  24.9 13.1 %collective-permute-start.6 = (bf16[4,3,64,256]{3,2,1,0:T(8,128)(2,1)}, bf16[4,3,64,256]{3,2,1,0:T(8,128)(2,1)S(1)}, u32[]{:S(2)}, u32[]{:S(2)}) collective-permute-start(bf16[4,3,64,256]{3,2,1,0:T(8,128)(2,1)} %get-tuple-element.22), channel_id=1, source_target_pairs={{0,1},{1,0},{2,3},{3,2},{4,5},{5,4},{6,7},{7,6},{8,9},{9,8},{10,11... | collective-permute-start | bytes 1179656 | tf_op jit(solution)/shard_map/ppermute | solution.py:17
  33.0 7.1 %collective-permute-start = (bf16[4,3,64,256]{3,2,1,0:T(8,128)(2,1)}, bf16[4,3,64,256]{3,2,1,0:T(8,128)(2,1)S(1)}, u32[]{:S(2)}, u32[]{:S(2)}) collective-permute-start(bf16[4,3,64,256]{3,2,1,0:T(8,128)(2,1)} %get-tuple-element.18), channel_id=1, source_target_pairs={{0,1},{1,0},{2,3},{3,2},{4,5},{5,4},{6,7},{7,6},{8,9},{9,8},{10,11... | collective-permute-start | bytes 1179656 | tf_op jit(solution)/shard_map/ppermute | solution.py:17
  33.3 8.6 %collective-permute-start.19 = (bf16[3,64,256]{2,1,0:T(8,128)(2,1)S(1)}, bf16[3,64,256]{2,1,0:T(8,128)(2,1)S(1)}, u32[]{:S(2)}, u32[]{:S(2)}) collective-permute-start(bf16[3,64,256]{2,1,0:T(8,128)(2,1)S(1)} %get-tuple-element.35), channel_id=1, source_target_pairs={{0,2},{1,3},{2,0},{3,1},{4,6},{5,7},{6,4},{7,5},{8,10},{9,11},{10,... | collective-permute-start | bytes 294920 | tf_op jit(solution)/shard_map/ppermute | solution.py:17
  36.2 7.2 %collective-permute-start.21 = (bf16[3,64,256]{2,1,0:T(8,128)(2,1)S(1)}, bf16[3,64,256]{2,1,0:T(8,128)(2,1)S(1)}, u32[]{:S(2)}, u32[]{:S(2)}) collective-permute-start(bf16[3,64,256]{2,1,0:T(8,128)(2,1)S(1)} %get-tuple-element.36), channel_id=1, source_target_pairs={{0,6},{1,7},{2,4},{3,5},{4,2},{5,3},{6,0},{7,1},{8,14},{9,15},{10,... | collective-permute-start | bytes 294920 | tf_op jit(solution)/shard_map/ppermute | solution.py:17
  37.7 7.5 %collective-permute-start.20 = (bf16[3,64,256]{2,1,0:T(8,128)(2,1)S(1)}, bf16[3,64,256]{2,1,0:T(8,128)(2,1)S(1)}, u32[]{:S(2)}, u32[]{:S(2)}) collective-permute-start(bf16[3,64,256]{2,1,0:T(8,128)(2,1)S(1)} %get-tuple-element.37), channel_id=1, source_target_pairs={{0,4},{1,5},{2,6},{3,7},{4,0},{5,1},{6,2},{7,3},{8,12},{9,13},{10,... | collective-permute-start | bytes 294920 | tf_op jit(solution)/shard_map/ppermute | solution.py:17
  38.0 8.7 %collective-permute-start.13 = (bf16[3,64,256]{2,1,0:T(8,128)(2,1)S(1)}, bf16[3,64,256]{2,1,0:T(8,128)(2,1)S(1)}, u32[]{:S(2)}, u32[]{:S(2)}) collective-permute-start(bf16[3,64,256]{2,1,0:T(8,128)(2,1)S(1)} %get-tuple-element.38), channel_id=1, source_target_pairs={{0,2},{1,3},{2,0},{3,1},{4,6},{5,7},{6,4},{7,5},{8,10},{9,11},{10,... | collective-permute-start | bytes 294920 | tf_op jit(solution)/shard_map/ppermute | solution.py:17
  40.1 8.1 %collective-permute-start.15 = (bf16[3,64,256]{2,1,0:T(8,128)(2,1)S(1)}, bf16[3,64,256]{2,1,0:T(8,128)(2,1)S(1)}, u32[]{:S(2)}, u32[]{:S(2)}) collective-permute-start(bf16[3,64,256]{2,1,0:T(8,128)(2,1)S(1)} %get-tuple-element.39), channel_id=1, source_target_pairs={{0,6},{1,7},{2,4},{3,5},{4,2},{5,3},{6,0},{7,1},{8,14},{9,15},{10,... | collective-permute-start | bytes 294920 | tf_op jit(solution)/shard_map/ppermute | solution.py:17
  41.9 7.8 %collective-permute-start.14 = (bf16[3,64,256]{2,1,0:T(8,128)(2,1)S(1)}, bf16[3,64,256]{2,1,0:T(8,128)(2,1)S(1)}, u32[]{:S(2)}, u32[]{:S(2)}) collective-permute-start(bf16[3,64,256]{2,1,0:T(8,128)(2,1)S(1)} %get-tuple-element.40), channel_id=1, source_target_pairs={{0,4},{1,5},{2,6},{3,7},{4,0},{5,1},{6,2},{7,3},{8,12},{9,13},{10,... | collective-permute-start | bytes 294920 | tf_op jit(solution)/shard_map/ppermute | solution.py:17
  43.5 7.9 %collective-permute-start.7 = (bf16[3,64,256]{2,1,0:T(8,128)(2,1)S(1)}, bf16[3,64,256]{2,1,0:T(8,128)(2,1)S(1)}, u32[]{:S(2)}, u32[]{:S(2)}) collective-permute-start(bf16[3,64,256]{2,1,0:T(8,128)(2,1)S(1)} %get-tuple-element.41), channel_id=1, source_target_pairs={{0,2},{1,3},{2,0},{3,1},{4,6},{5,7},{6,4},{7,5},{8,10},{9,11},{10,... | collective-permute-start | bytes 294920 | tf_op jit(solution)/shard_map/ppermute | solution.py:17
  45.2 7.6 %collective-permute-start.9 = (bf16[3,64,256]{2,1,0:T(8,128)(2,1)S(1)}, bf16[3,64,256]{2,1,0:T(8,128)(2,1)S(1)}, u32[]{:S(2)}, u32[]{:S(2)}) collective-permute-start(bf16[3,64,256]{2,1,0:T(8,128)(2,1)S(1)} %get-tuple-element.42), channel_id=1, source_target_pairs={{0,6},{1,7},{2,4},{3,5},{4,2},{5,3},{6,0},{7,1},{8,14},{9,15},{10,... | collective-permute-start | bytes 294920 | tf_op jit(solution)/shard_map/ppermute | solution.py:17
  46.7 8.7 %collective-permute-start.8 = (bf16[3,64,256]{2,1,0:T(8,128)(2,1)S(1)}, bf16[3,64,256]{2,1,0:T(8,128)(2,1)S(1)}, u32[]{:S(2)}, u32[]{:S(2)}) collective-permute-start(bf16[3,64,256]{2,1,0:T(8,128)(2,1)S(1)} %get-tuple-element.43), channel_id=1, source_target_pairs={{0,4},{1,5},{2,6},{3,7},{4,0},{5,1},{6,2},{7,3},{8,12},{9,13},{10,... | collective-permute-start | bytes 294920 | tf_op jit(solution)/shard_map/ppermute | solution.py:17
  48.3 9.6 %collective-permute-start.1 = (bf16[3,64,256]{2,1,0:T(8,128)(2,1)S(1)}, bf16[3,64,256]{2,1,0:T(8,128)(2,1)S(1)}, u32[]{:S(2)}, u32[]{:S(2)}) collective-permute-start(bf16[3,64,256]{2,1,0:T(8,128)(2,1)S(1)} %get-tuple-element.44), channel_id=1, source_target_pairs={{0,2},{1,3},{2,0},{3,1},{4,6},{5,7},{6,4},{7,5},{8,10},{9,11},{10,... | collective-permute-start | bytes 294920 | tf_op jit(solution)/shard_map/ppermute | solution.py:17
  49.7 8.7 %collective-permute-start.3 = (bf16[3,64,256]{2,1,0:T(8,128)(2,1)S(1)}, bf16[3,64,256]{2,1,0:T(8,128)(2,1)S(1)}, u32[]{:S(2)}, u32[]{:S(2)}) collective-permute-start(bf16[3,64,256]{2,1,0:T(8,128)(2,1)S(1)} %get-tuple-element.45), channel_id=1, source_target_pairs={{0,6},{1,7},{2,4},{3,5},{4,2},{5,3},{6,0},{7,1},{8,14},{9,15},{10,... | collective-permute-start | bytes 294920 | tf_op jit(solution)/shard_map/ppermute | solution.py:17
  51.4 7.0 %collective-permute-start.2 = (bf16[3,64,256]{2,1,0:T(8,128)(2,1)S(1)}, bf16[3,64,256]{2,1,0:T(8,128)(2,1)S(1)}, u32[]{:S(2)}, u32[]{:S(2)}) collective-permute-start(bf16[3,64,256]{2,1,0:T(8,128)(2,1)S(1)} %get-tuple-element.46), channel_id=1, source_target_pairs={{0,4},{1,5},{2,6},{3,7},{4,0},{5,1},{6,2},{7,3},{8,12},{9,13},{10,... | collective-permute-start | bytes 294920 | tf_op jit(solution)/shard_map/ppermute | solution.py:17
  52.8 13.9 %collective-permute-start.22 = (bf16[3,64,256]{2,1,0:T(8,128)(2,1)S(1)}, bf16[3,64,256]{2,1,0:T(8,128)(2,1)S(1)}, u32[]{:S(2)}, u32[]{:S(2)}) collective-permute-start(bf16[3,64,256]{2,1,0:T(8,128)(2,1)S(1)} %fusion.3.own_ref), channel_id=1, source_target_pairs={{0,16},{8,24},{16,0},{24,8},{1,17},{9,25},{17,1},{25,9},{2,18},{10... | collective-permute-start | bytes 294920 | tf_op jit(solution)/shard_map/ppermute | solution.py:17
  55.4 13.8 %collective-permute-start.16 = (bf16[3,64,256]{2,1,0:T(8,128)(2,1)S(1)}, bf16[3,64,256]{2,1,0:T(8,128)(2,1)S(1)}, u32[]{:S(2)}, u32[]{:S(2)}) collective-permute-start(bf16[3,64,256]{2,1,0:T(8,128)(2,1)S(1)} %fusion.7.own_ref), channel_id=1, source_target_pairs={{0,16},{8,24},{16,0},{24,8},{1,17},{9,25},{17,1},{25,9},{2,18},{10... | collective-permute-start | bytes 294920 | tf_op jit(solution)/shard_map/ppermute | solution.py:17
  57.9 15.9 %collective-permute-start.10 = (bf16[3,64,256]{2,1,0:T(8,128)(2,1)S(1)}, bf16[3,64,256]{2,1,0:T(8,128)(2,1)S(1)}, u32[]{:S(2)}, u32[]{:S(2)}) collective-permute-start(bf16[3,64,256]{2,1,0:T(8,128)(2,1)S(1)} %fusion.11.own_ref), channel_id=1, source_target_pairs={{0,16},{8,24},{16,0},{24,8},{1,17},{9,25},{17,1},{25,9},{2,18},{10... | collective-permute-start | bytes 294920 | tf_op jit(solution)/shard_map/ppermute | solution.py:17
  58.5 17.8 %collective-permute-start.4 = (bf16[3,64,256]{2,1,0:T(8,128)(2,1)S(1)}, bf16[3,64,256]{2,1,0:T(8,128)(2,1)S(1)}, u32[]{:S(2)}, u32[]{:S(2)}) collective-permute-start(bf16[3,64,256]{2,1,0:T(8,128)(2,1)S(1)} %fusion.15.own_ref), channel_id=1, source_target_pairs={{0,16},{8,24},{16,0},{24,8},{1,17},{9,25},{17,1},{25,9},{2,18},{10... | collective-permute-start | bytes 294920 | tf_op jit(solution)/shard_map/ppermute | solution.py:17
  69.2 11.7 %collective-permute-start.23 = (bf16[3,64,256]{2,1,0:T(8,128)(2,1)}, bf16[3,64,256]{2,1,0:T(8,128)(2,1)S(1)}, u32[]{:S(2)}, u32[]{:S(2)}) collective-permute-start(bf16[3,64,256]{2,1,0:T(8,128)(2,1)} %middle_level.7.own_ref), channel_id=1, source_target_pairs={{0,8},{8,0},{16,24},{24,16},{1,9},{9,1},{17,25},{25,17},{2,10},{10... | collective-permute-start | bytes 294920 | tf_op jit(solution)/shard_map/ppermute | solution.py:17
  71.8 12.1 %collective-permute-start.17 = (bf16[3,64,256]{2,1,0:T(8,128)(2,1)}, bf16[3,64,256]{2,1,0:T(8,128)(2,1)S(1)}, u32[]{:S(2)}, u32[]{:S(2)}) collective-permute-start(bf16[3,64,256]{2,1,0:T(8,128)(2,1)} %middle_level.6.own_ref), channel_id=1, source_target_pairs={{0,8},{8,0},{16,24},{24,16},{1,9},{9,1},{17,25},{25,17},{2,10},{10... | collective-permute-start | bytes 294920 | tf_op jit(solution)/shard_map/ppermute | solution.py:17
  76.3 10.4 %collective-permute-start.11 = (bf16[3,64,256]{2,1,0:T(8,128)(2,1)}, bf16[3,64,256]{2,1,0:T(8,128)(2,1)S(1)}, u32[]{:S(2)}, u32[]{:S(2)}) collective-permute-start(bf16[3,64,256]{2,1,0:T(8,128)(2,1)} %middle_level.5.own_ref), channel_id=1, source_target_pairs={{0,8},{8,0},{16,24},{24,16},{1,9},{9,1},{17,25},{25,17},{2,10},{10... | collective-permute-start | bytes 294920 | tf_op jit(solution)/shard_map/ppermute | solution.py:17
  78.9 10.7 %collective-permute-start.5 = (bf16[3,64,256]{2,1,0:T(8,128)(2,1)}, bf16[3,64,256]{2,1,0:T(8,128)(2,1)S(1)}, u32[]{:S(2)}, u32[]{:S(2)}) collective-permute-start(bf16[3,64,256]{2,1,0:T(8,128)(2,1)} %middle_level.4.own_ref), channel_id=1, source_target_pairs={{0,8},{8,0},{16,24},{24,16},{1,9},{9,1},{17,25},{25,17},{2,10},{10... | collective-permute-start | bytes 294920 | tf_op jit(solution)/shard_map/ppermute | solution.py:17
  (16 other events, 100.3 us)

commit v2 on v0

v2 whole, which is shorter than its diff:
```python
import functools
import jax
import jax.numpy as jnp
from jax import lax
from jax.experimental import pallas as pl
from jax.experimental.pallas import tpu as pltpu
from jax.sharding import PartitionSpec as P

epsilon = 1e-06
shares = (3, 2, 2, 1)
groups = ((0,), (1,), (2,), (3,))
exchanges = (((0, 0),), ((0, 1),), ((1, 0),), ((1, 1),), ((2, 0),), ((2, 1),), ((3, 0),), ((3, 1),))
project_steps = 4
mib = 1024 * 1024
in_vmem = pl.BlockSpec(memory_space=pltpu.VMEM)
in_hbm = pl.BlockSpec(memory_space=pltpu.HBM)
in_smem = pl.BlockSpec(memory_space=pltpu.SMEM)


def swapped(value, axis, mask):
    pairs = [(source, source ^ mask) for source in range(lax.axis_size(axis))]
    return lax.ppermute(value, axis, pairs)


def phase_count(members):
    return members.bit_length() - 2


def chip_bit(core, step, count):
    return (core + step) % count


def swapped_step(value, step):
    members = lax.axis_size("sk")
    count = phase_count(members)
    pairs = [
        (source, source ^ (2 << chip_bit(source % 2, step, count))) for source in range(members)
    ]
    return lax.ppermute(value, "sk", pairs)


def product(left, right):
    return lax.dot_general(left, right, (((1,), (0,)), ((), ())), preferred_element_type=jnp.float32)


def params(megabytes):
    return pltpu.CompilerParams(vmem_limit_bytes=megabytes * mib)


def local(value):
    return pltpu.with_memory_space_constraint(value, pltpu.VMEM)


def remote(value):
    return pltpu.with_memory_space_constraint(value, pltpu.HBM)


def piece_target(place, index, segments, chunk):
    count = phase_count(segments)
    turns = []
    for core in range(2):
        turn = 0
        for phase in range(count):
            if (index >> (count - 1 - phase)) & 1:
                turn |= 2 << chip_bit(core, chunk + phase, count)
        turns.append(turn)
    return place ^ jnp.where(place % 2 == 0, turns[0], turns[1])


def write_pieces(place, acc_ref, keep_ref, send_ref, chunk):
    halves, passes, chunk_rows, width = keep_ref.shape
    rank = width // 2
    segments = 2 * halves
    for turn in range(segments):
        out_ref = send_ref if turn % 2 else keep_ref
        target = piece_target(place ^ (turn % 2), turn // 2, segments, chunk)
        rows = pl.ds(pl.multiple_of(target * chunk_rows, chunk_rows), chunk_rows)
        upper = acc_ref[0, rows, :]
        lower = acc_ref[1, rows, :]
        for one in range(passes):
            re = slice(2 * one * rank, (2 * one + 1) * rank)
            im = slice((2 * one + 1) * rank, (2 * one + 2) * rank)
            out_ref[turn // 2, one, :, :rank] = (upper[:, re] - lower[:, im]).astype(jnp.bfloat16)
            out_ref[turn // 2, one, :, rank:] = (upper[:, im] + lower[:, re]).astype(jnp.bfloat16)


def block_copies(kernel_ref, block_ref, sems, span, part):
    return [
        pltpu.make_async_copy(
            kernel_ref.at[part, segment, pl.ds(*span), :],
            block_ref.at[part, segment],
            sems.at[part, segment],
        )
        for segment in range(block_ref.shape[1])
    ]


def both_copies(kernel_ref, block_ref, sems, span):
    return [copy for part in range(2) for copy in block_copies(kernel_ref, block_ref, sems, span, part)]


def first_body(place_ref, kernel_ref, sketch_ref, proj_ref, *rest, spans):
    if len(spans) > 1:
        keep_ref, send_ref, sk_ref, next_ref, *rest = rest
        *rest, next_sems = rest
    else:
        keep_ref, send_ref, sk_ref, *rest = rest
    held_ref, parts_ref, block_ref, acc_ref, sketch_sems, proj_sem, block_sems = rest
    passes, cols, _ = sketch_ref.shape
    rank = proj_ref.shape[4]
    deep = cols // project_steps

    def sketch_copy(step):
        rows = pl.ds(pl.multiple_of(step * deep, deep), deep)
        return pltpu.make_async_copy(
            sketch_ref.at[:, rows, :], held_ref.at[:, rows, :], sketch_sems.at[step]
        )

    proj_copy = pltpu.make_async_copy(proj_ref.at[0, 0], parts_ref, proj_sem)
    proj_copy.start()
    for step in range(project_steps):
        sketch_copy(step).start()
    for copy in block_copies(kernel_ref, block_ref, block_sems, spans[0], 0):
        copy.start()
    next_copies = []
    if len(spans) > 1:
        next_copies = both_copies(kernel_ref, next_ref, next_sems, spans[1])
    proj_copy.wait()

    def project(step, carry):
        sketch_copy(step).wait()
        both = jnp.concatenate([parts_ref[0], parts_ref[1]], axis=1)
        rows = pl.ds(pl.multiple_of(step * deep, deep), deep)
        for one in range(passes):
            cols = slice(2 * one * rank, 2 * (one + 1) * rank)
            sk_ref[rows, cols] = product(held_ref[one, rows, :], both).astype(jnp.bfloat16)
        return carry

    def gather(part, carry):
        for copy in block_copies(kernel_ref, block_ref, block_sems, spans[0], part):
            copy.wait()

        @pl.when(part == 0)
        def _():
            for copy in next_copies:
                copy.start()

        acc_ref[part] = product(block_ref[part].reshape(-1, cols), sk_ref[...])
        return carry

    lax.fori_loop(0, 1, project, 0)
    for copy in block_copies(kernel_ref, block_ref, block_sems, spans[0], 1):
        copy.start()
    lax.fori_loop(1, project_steps, project, 0)
    lax.fori_loop(0, 2, gather, 0)
    write_pieces(place_ref[0], acc_ref, keep_ref, send_ref, 0)
    for copy in next_copies:
        copy.wait()


def cost_of(kernel, span, width):
    _, segments, _, cols = kernel.shape
    return pl.CostEstimate(
        flops=4 * segments * span[1] * cols * width,
        bytes_accessed=4 * segments * span[1] * cols,
        transcendentals=0,
    )


def first_gathered(place, kernel, sketch, projections, spans):
    _, segments, _, cols = kernel.shape
    passes, _, sketch_cols = sketch.shape
    rank = projections.shape[4]
    width = 2 * passes * rank
    piece = pltpu.VMEM((segments // 2, passes, spans[0][1], 2 * rank), jnp.bfloat16)
    out_shape = [piece, piece, pltpu.VMEM((cols, width), jnp.bfloat16)]
    scratch = [
        pltpu.VMEM(sketch.shape, sketch.dtype),
        pltpu.VMEM((2, sketch_cols, rank), projections.dtype),
        pltpu.VMEM((2, segments, spans[0][1], cols), kernel.dtype),
        pltpu.VMEM((2, segments * spans[0][1], width), jnp.float32),
        pltpu.SemaphoreType.DMA((project_steps,)),
        pltpu.SemaphoreType.DMA(()),
        pltpu.SemaphoreType.DMA((2, segments)),
    ]
    if len(spans) > 1:
        out_shape.append(pltpu.VMEM((2, segments, spans[1][1], cols), kernel.dtype))
        scratch.append(pltpu.SemaphoreType.DMA((2, segments)))
    return pl.pallas_call(
        functools.partial(first_body, spans=spans),
        name="gather_first",
        in_specs=[in_smem, in_hbm, in_hbm, in_hbm],
        out_specs=[in_vmem] * len(out_shape),
        out_shape=out_shape,
        scratch_shapes=scratch,
        compiler_params=params(28),
        cost_estimate=cost_of(kernel, spans[0], width),
    )(place, remote(kernel), remote(sketch), remote(projections))


def gather_body(place_ref, block_ref, sk_ref, *rest, chunk, next_span):
    step = pl.program_id(0)
    copies = []
    if next_span is None:
        keep_ref, send_ref, acc_ref = rest
    else:
        kernel_ref, keep_ref, send_ref, next_ref, acc_ref, sems = rest
        copies = both_copies(kernel_ref, next_ref, sems, next_span)

        @pl.when(step == 0)
        def _():
            for copy in copies:
                copy.start()

    cols = block_ref.shape[3]
    acc_ref[step] = product(block_ref[step].reshape(-1, cols), sk_ref[...])

    @pl.when(step == 1)
    def _():
        write_pieces(place_ref[0], acc_ref, keep_ref, send_ref, chunk)
        for copy in copies:
            copy.wait()


def gathered(place, block, sk_value, kernel, passes, chunk, spans):
    _, segments, chunk_rows, cols = block.shape
    width = sk_value.shape[1]
    piece = pltpu.VMEM((segments // 2, passes, chunk_rows, width // passes), jnp.bfloat16)
    operands = [place, local(block), local(sk_value)]
    in_specs = [in_smem, in_vmem, in_vmem]
    out_shape = [piece, piece]
    scratch = [pltpu.VMEM((2, segments * chunk_rows, width), jnp.float32)]
    next_span = spans[chunk + 1] if chunk + 1 < len(spans) else None
    if next_span is not None:
        operands.append(remote(kernel))
        in_specs.append(in_hbm)
        out_shape.append(pltpu.VMEM((2, segments, next_span[1], cols), jnp.bfloat16))
        scratch.append(pltpu.SemaphoreType.DMA((2, segments)))
    return pl.pallas_call(
        functools.partial(gather_body, chunk=chunk, next_span=next_span),
        name="gather",
        grid=(2,),
        in_specs=in_specs,
        out_specs=[in_vmem] * len(out_shape),
        out_shape=out_shape,
        scratch_shapes=scratch,
        compiler_params=params(12),
        cost_estimate=cost_of(kernel, spans[chunk], width),
    )(*operands)


def sum_body(*refs, stages):
    for held, got, got_row, hold, send, send_row, own in stages:
        total = refs[held][...].astype(jnp.float32)
        width = total.shape[3]
        if got_row is None:
            total = total + refs[got][...].astype(jnp.float32)
        else:
            rows = total.size // width
            total = total + refs[got][got_row : got_row + rows, :].astype(jnp.float32).reshape(total.shape)
        half = total.shape[0] // 2
        if own is None:
            flat = total[half:].astype(jnp.bfloat16).reshape(-1, width)
            refs[hold][...] = total[:half]
            refs[send][send_row : send_row + flat.shape[0], :] = flat
        else:
            refs[own][...] = total[0].astype(jnp.bfloat16)


def summed(parts, count):
    operands = []
    out_shape = []
    entries = []
    send_row = 0
    for phase, held, got, got_row in parts:
        pieces = 1 << (count - phase)
        passes, chunk_rows, width = held.shape[1:]
        entry = [len(operands), len(operands) + 1, got_row, None, None, None, None]
        operands.extend([local(held), local(got)])
        if phase == count:
            entry[6] = len(out_shape)
            out_shape.append(pltpu.VMEM((passes, chunk_rows, width), jnp.bfloat16))
        else:
            entry[3] = len(out_shape)
            entry[5] = send_row
            send_row += passes * chunk_rows * (pieces // 2)
            out_shape.append(pltpu.VMEM((pieces // 2, passes, chunk_rows, width), jnp.float32))
        entries.append(entry)
    if send_row:
        out_shape.append(pltpu.VMEM((send_row, width), jnp.bfloat16))
    for entry in entries:
        if entry[6] is None:
            entry[3] += len(operands)
            entry[4] = len(operands) + len(out_shape) - 1
        else:
            entry[6] += len(operands)
    results = pl.pallas_call(
        functools.partial(sum_body, stages=tuple(map(tuple, entries))),
        name="sum_parts",
        in_specs=[in_vmem] * len(operands),
        out_specs=[in_vmem] * len(out_shape),
        out_shape=out_shape,
        compiler_params=params(8),
    )(*operands)
    return results


def plan_of(count):
    if count == 2:
        return exchanges
    chunks = len(shares)
    return tuple(
        tuple((step - phase, phase) for phase in range(count) if 0 <= step - phase < chunks)
        for step in range(chunks + count - 1)
    )


def weights_body(proj_ref, inv_ref, *out_refs):
    levels = proj_ref.shape[0]
    rank = proj_ref.shape[4]
    for level in range(levels):
        for half in range(2):
            rows = slice(half * rank, (half + 1) * rank)
            re = inv_ref[level, 0, 0, rows, :]
            im = inv_ref[level, 0, 1, rows, :]
            if level + 1 < levels:
                next_re = proj_ref[level + 1, 0, 0]
                next_im = proj_ref[level + 1, 0, 1]
                re, im = (
                    (product(re, next_re) - product(im, next_im)).astype(jnp.bfloat16),
                    (product(re, next_im) + product(im, next_re)).astype(jnp.bfloat16),
                )
            cols = re.shape[1]
            out_refs[level][half * 2 * rank : half * 2 * rank + rank, :cols] = re
            out_refs[level][half * 2 * rank : half * 2 * rank + rank, cols:] = im
            out_refs[level][half * 2 * rank + rank : (half + 1) * 2 * rank, :cols] = -im
            out_refs[level][half * 2 * rank + rank : (half + 1) * 2 * rank, cols:] = re


def level_weights(projections, inverses):
    levels = projections.shape[0]
    rank = projections.shape[4]
    sketch_cols = inverses.shape[4]
    shapes = [
        pltpu.VMEM((4 * rank, 2 * (rank if level + 1 < levels else sketch_cols)), jnp.bfloat16)
        for level in range(levels)
    ]
    return pl.pallas_call(
        weights_body,
        name="level_weights",
        out_specs=[in_vmem] * levels,
        out_shape=shapes,
        compiler_params=params(8),
    )(projections, inverses)


def paired(own, partner, weight_ref):
    width = own.shape[-1]
    own = own.reshape(-1, width)
    partner = partner.reshape(-1, width)
    return product(own, weight_ref[:width, :]) + product(partner, weight_ref[width:, :])


def middle_body(*refs, count):
    weight_ref = refs[2 * count]
    out_ref = refs[2 * count + 1]
    first = 0
    for place in range(count):
        own = refs[place][...]
        rows = own.shape[1]
        value = paired(own, refs[count + place][...], weight_ref)
        out_ref[:, first : first + rows, :] = value.astype(jnp.bfloat16).reshape(own.shape)
        first += rows


def middle_level(owns, partners, weight):
    passes, _, width = owns[0].shape
    rows = sum(own.shape[1] for own in owns)
    operands = [local(value) for value in (*owns, *partners, weight)]
    return pl.pallas_call(
        functools.partial(middle_body, count=len(owns)),
        name="middle_level",
        in_specs=[in_vmem] * len(operands),
        out_specs=in_vmem,
        out_shape=pltpu.VMEM((passes, rows, width), jnp.bfloat16),
        compiler_params=params(4),
    )(*operands)


def normalized(own_ref, partner_ref, weight_ref, gain_ref):
    current = paired(own_ref[...], partner_ref[...], weight_ref)
    sketch_cols = gain_ref.shape[1]
    power = jnp.sum(current * current, axis=-1, keepdims=True) / sketch_cols
    scale = lax.rsqrt(power + epsilon)
    gain = gain_ref[...]
    shape = own_ref.shape[:2] + (sketch_cols,)
    return (
        (current[:, :sketch_cols] * scale * gain).reshape(shape),
        (current[:, sketch_cols:] * scale * gain).reshape(shape),
    )


def staged_body(own_ref, partner_ref, weight_ref, gain_ref, stage_ref):
    stage_ref[0], stage_ref[1] = normalized(own_ref, partner_ref, weight_ref, gain_ref)


def staged_level(own, partner, weight, gain):
    passes, rows, _ = own.shape
    return pl.pallas_call(
        staged_body,
        name="staged_level",
        in_specs=[in_vmem] * 4,
        out_specs=in_vmem,
        out_shape=pltpu.VMEM((2, passes, rows, gain.shape[1]), jnp.float32),
        compiler_params=params(8),
    )(local(own), local(partner), local(weight), local(gain))


def final_body(own_ref, partner_ref, weight_ref, gain_ref, *rest, firsts):
    stages = rest[: len(firsts) - 1]
    out_ref, stage_ref, sems = rest[len(firsts) - 1 :]
    copies = []
    for place, (first, part_ref) in enumerate(zip(firsts, (*stages, stage_ref))):
        target = out_ref.at[:, :, pl.ds(first, part_ref.shape[2]), :]
        copies.append(pltpu.make_async_copy(part_ref, target, sems.at[place]))
    for copy in copies[:-1]:
        copy.start()
    stage_ref[0], stage_ref[1] = normalized(own_ref, partner_ref, weight_ref, gain_ref)
    copies[-1].start()
    for copy in copies:
        copy.wait()


def final_level(own, partner, weight, gain, stages, firsts, segment_rows):
    passes, rows, _ = own.shape
    sketch_cols = gain.shape[1]
    operands = [local(value) for value in (own, partner, weight, gain, *stages)]
    return pl.pallas_call(
        functools.partial(final_body, firsts=tuple(firsts)),
        name="final_level",
        in_specs=[in_vmem] * len(operands),
        out_specs=in_hbm,
        out_shape=jax.ShapeDtypeStruct((2, passes, segment_rows, sketch_cols), jnp.float32),
        scratch_shapes=[
            pltpu.VMEM((2, passes, rows, sketch_cols), jnp.float32),
            pltpu.SemaphoreType.DMA((len(firsts),)),
        ],
        compiler_params=params(8),
    )(*operands)


def shards(kernel, sketch, projections, inverses, norm_gain):
    members = lax.axis_size("sk")
    count = phase_count(members)
    levels = projections.shape[0]
    passes = sketch.shape[0]
    top_bits = lax.axis_size("bf").bit_length() - 1
    _, rows, cols = kernel.shape
    segment_rows = rows // members
    unit = segment_rows // sum(shares)
    spans = []
    for share in shares:
        first = spans[-1][0] + spans[-1][1] if spans else 0
        spans.append((first, share * unit))
    chunks = len(spans)
    kernel = kernel.reshape(2, members, segment_rows, cols)
    place = lax.axis_index("sk").reshape(1).astype(jnp.int32)
    gain = norm_gain.reshape(1, -1)
    weights = level_weights(projections, inverses)
    keeps = []
    cores = []
    block = None
    for chunk in range(chunks):
        if chunk == 0:
            keep, send, sk_value, *blocks = first_gathered(place, kernel, sketch, projections, spans)
        else:
            keep, send, *blocks = gathered(place, block, sk_value, kernel, passes, chunk, spans)
        if blocks:
            block = blocks[0]
        keeps.append(keep)
        cores.append(swapped(send, "sk", 1))
    held = dict(enumerate(keeps))
    got = {chunk: (core, None) for chunk, core in enumerate(cores)}
    for place, exchange in enumerate(plan_of(count)):
        parts = [(phase, held[chunk], *got[chunk]) for chunk, phase in exchange]
        *kept, send = summed(parts, count)
        chunk, phase = exchange[0]
        received = swapped_step(send, chunk + phase)
        row = 0
        for (chunk, _), value in zip(exchange, kept):
            held[chunk] = value
            got[chunk] = (received, row)
            row += value.size // value.shape[3]
    owns = []
    for chunk in range(chunks):
        owns.extend(summed([(count, held[chunk], *got[chunk])], count))
    partners = []
    for chunk in range(chunks):
        partners.append(swapped(owns[chunk], "bf", 2 ** (top_bits - 1)))
    stages = []
    firsts = []
    for place, group in enumerate(groups):
        own = [owns[chunk] for chunk in group]
        partner = [partners[chunk] for chunk in group]
        for level in range(1, levels):
            merged = middle_level(own, partner, weights[level - 1])
            own = [merged]
            partner = [swapped(merged, "bf", 2 ** (top_bits - 1 - level))]
        firsts.append(spans[group[0]][0])
        if place + 1 < len(groups):
            stages.append(staged_level(own[0], partner[0], weights[levels - 1], gain))
        else:
            out = final_level(
                own[0], partner[0], weights[levels - 1], gain, stages, firsts, segment_rows
            )
    return out


def solution(mesh):
    placed = (
        P(None, "bf", "sk"),
        P(None, "sk", None),
        P(None, "bf", None, None, None),
        P(None, "bf", None, None, None),
        P(),
    )

    return jax.shard_map(
        shards,
        mesh=mesh,
        in_specs=placed,
        out_specs=P(None, None, ("bf", "sk"), None),
        check_vma=False,
    )
```

time: 121 us -> 64.5 us (0.53)
  waiting for transfers between devices: 68.1 us -> 13 us
  matrix products: 28 us -> 0 us
  starting transfers between devices: 2.87 us -> 27.5 us
  Pallas kernels: 0 us -> 23.7 us
  between operations: 13.5 us -> 0.2 us
  local copies, waits for them, and re-layouts: 4.46 us -> 0.02 us
  other arithmetic: 3.93 us -> 0 us
    reduce_scatter x1 -> x0, waiting for transfers between devices: 45.8 us -> none  [shards(): lax.psum_scatter(partial_value.astype(jnp.bfloat16), 'sk', scatter_dimens...]
    dot_general x7 -> x0, matrix products: 28 us -> none  [the longest x1 10.3 us: shards(): jnp.einsum('rc,pck->prk', kernel[0], sk_proj, preferred_element_type=jnp....]
    pallas_call x0 -> x25, Pallas kernels: none -> 23.7 us  [the longest x3 9.97 us: gathered(): pl.pallas_call(functools.partial(gather_body, chunk=chunk, next_span=next...]
    ppermute x0 -> x8, starting transfers between devices: none -> 13.5 us  [swapped_step(): return lax.ppermute(value, 'sk', pairs)]
    ppermute x2 -> x12, waiting for transfers between devices: 22.3 us -> 10.2 us  [swapped(): return lax.ppermute(value, axis, pairs)]
    ppermute x2 -> x12, starting transfers between devices: 2.87 us -> 14 us  [swapped(): return lax.ppermute(value, axis, pairs)]
    squeeze x4 -> x0, local copies, waits for them, and re-layouts: 4.2 us -> none  [the longest x3 3.13 us: complex_block(): upper = jnp.concatenate([matrix[0], matrix[1]], axis=1)]
    ppermute x0 -> x8, waiting for transfers between devices: none -> 2.77 us  [swapped_step(): return lax.ppermute(value, 'sk', pairs)]
  transfers between devices with their start and end apart: 3 -> 20, of which waited for: 3 -> 7; matrix products, arithmetic and copies ran while one was open for 7% -> 0% of each run, Pallas kernels for 0% -> 20%
where the time goes in v2:
time: 64.5 us; the launch traced here: 64.4 us
  starting transfers between devices  27.5 us (43%)
  Pallas kernels  23.7 us (37%)
  waiting for transfers between devices  13 us (20%)
    ppermute x12, starting transfers between devices, swapped(): return lax.ppermute(value, axis, pairs)  14 us
    ppermute x8, starting transfers between devices, swapped_step(): return lax.ppermute(value, 'sk', pairs)  13.5 us
    ppermute x12, waiting for transfers between devices, swapped(): return lax.ppermute(value, axis, pairs)  10.2 us
    pallas_call x3, Pallas kernels, gathered(): pl.pallas_call(functools.partial(gather_body, chunk=chunk, next_span=next...  9.97 us
    pallas_call x1, Pallas kernels, first_gathered(): pl.pallas_call(functools.partial(first_body, spans=spans), name='gather_f...  9.76 us
    ppermute x8, waiting for transfers between devices, swapped_step(): return lax.ppermute(value, 'sk', pairs)  2.77 us
  transfers between devices with their start and end apart: 20, of which 7 were waited for; matrix products, arithmetic and copies ran while one was open for 0% of the time, Pallas kernels for 20%

profile of v2, /device:TPU:0, one launch (start us, length us, event | category | flops | bytes accessed | tf_op | source)
XLA Modules:
  0.0 64.4 jit_solution(4333921899047190270)
XLA Ops:
  0.0 9.8 %gather_first.1 = (bf16[4,3,96,256]{3,2,1,0:T(8,128)(2,1)S(1)}, bf16[4,3,96,256]{3,2,1,0:T(8,128)(2,1)S(1)}, bf16[2048,768]{1,0:T(8,128)(2,1)S(1)}, bf16[2,8,64,2048]{3,2,1,0:T(8,128)(2,1)S(1)}) custom-call(s32[1]{0:T(128)} %bitcast.place_ref, bf16[2,8,256,2048]{3,2,1,0:T(8,128)(2,1)} %bitcast.7, bf16[3,2048,256]{2,1,0:T(8,128)(2,1)} %sketch_ref.1, ...), custom_call_target="tpu_custom_call" | custom-call | flops 4831838208 | bytes 6291456 | tf_op jit(solution)/shard_map/gather_first/pallas_call | solution.py:189
  10.3 3.9 %gather.3 = (bf16[4,3,64,256]{3,2,1,0:T(8,128)(2,1)S(1)}, bf16[4,3,64,256]{3,2,1,0:T(8,128)(2,1)S(1)}, bf16[2,8,64,2048]{3,2,1,0:T(8,128)(2,1)S(1)}) custom-call(s32[1]{0:T(128)} %bitcast.place_ref, bf16[2,8,64,2048]{3,2,1,0:T(8,128)(2,1)S(1)} %get-tuple-element.35.block_ref, bf16[2048,768]{1,0:T(8,128)(2,1)S(1)} %get-tuple-element.36.sk_ref, ...), custom_call_target="tpu_custom_call" | custom-call | flops 3221225472 | bytes 4194304 | tf_op jit(solution)/shard_map/gather/pallas_call | solution.py:239
  14.3 4.0 %gather.4 = (bf16[4,3,64,256]{3,2,1,0:T(8,128)(2,1)S(1)}, bf16[4,3,64,256]{3,2,1,0:T(8,128)(2,1)S(1)}, bf16[2,8,32,2048]{3,2,1,0:T(8,128)(2,1)S(1)}) custom-call(s32[1]{0:T(128)} %bitcast.place_ref, bf16[2,8,64,2048]{3,2,1,0:T(8,128)(2,1)S(1)} %get-tuple-element.37.block_ref, bf16[2048,768]{1,0:T(8,128)(2,1)S(1)} %get-tuple-element.36.sk_ref, ...), custom_call_target="tpu_custom_call" | custom-call | flops 3221225472 | bytes 4194304 | tf_op jit(solution)/shard_map/gather/pallas_call | solution.py:239
  18.9 2.6 %collective-permute-start.6 = (bf16[576,256]{1,0:T(8,128)(2,1)S(1)}, bf16[576,256]{1,0:T(8,128)(2,1)S(1)}, u32[]{:S(2)}, u32[]{:S(2)}) collective-permute-start(bf16[576,256]{1,0:T(8,128)(2,1)S(1)} %get-tuple-element.50), channel_id=1, source_target_pairs={{0,2},{1,5},{2,0},{3,7},{4,6},{5,1},{6,4},{7,3},{8,10},{9,13},{10,... | collective-permute-start | bytes 884744 | tf_op jit(solution)/shard_map/ppermute | solution.py:39
  21.7 1.1 %collective-permute-start.16 = (bf16[384,256]{1,0:T(8,128)(2,1)S(1)}, bf16[384,256]{1,0:T(8,128)(2,1)S(1)}, u32[]{:S(2)}, u32[]{:S(2)}) collective-permute-start(bf16[384,256]{1,0:T(8,128)(2,1)S(1)} %get-tuple-element.62), channel_id=1, source_target_pairs={{0,2},{1,5},{2,0},{3,7},{4,6},{5,1},{6,4},{7,3},{8,10},{9,13},{10,... | collective-permute-start | bytes 589832 | tf_op jit(solution)/shard_map/ppermute | solution.py:39
  22.9 1.6 %collective-permute-start.11 = (bf16[384,256]{1,0:T(8,128)(2,1)S(1)}, bf16[384,256]{1,0:T(8,128)(2,1)S(1)}, u32[]{:S(2)}, u32[]{:S(2)}) collective-permute-start(bf16[384,256]{1,0:T(8,128)(2,1)S(1)} %get-tuple-element.56), channel_id=1, source_target_pairs={{0,4},{1,3},{2,6},{3,1},{4,0},{5,7},{6,2},{7,5},{8,12},{9,11},{10,... | collective-permute-start | bytes 589832 | tf_op jit(solution)/shard_map/ppermute | solution.py:39
  24.5 2.1 %gather.5 = (bf16[4,3,32,256]{3,2,1,0:T(8,128)(2,1)S(1)}, bf16[4,3,32,256]{3,2,1,0:T(8,128)(2,1)S(1)}) custom-call(s32[1]{0:T(128)} %bitcast.place_ref, bf16[2,8,32,2048]{3,2,1,0:T(8,128)(2,1)S(1)} %get-tuple-element.38.block_ref, bf16[2048,768]{1,0:T(8,128)(2,1)S(1)} %get-tuple-element.36.sk_ref), custom_call_target="tpu_custom_call" | custom-call | flops 1610612736 | bytes 2097152 | tf_op jit(solution)/shard_map/gather/pallas_call | solution.py:239
  27.0 3.4 %collective-permute-start.7 = (bf16[288,256]{1,0:T(8,128)(2,1)S(1)}, bf16[288,256]{1,0:T(8,128)(2,1)S(1)}, u32[]{:S(2)}, u32[]{:S(2)}) collective-permute-start(bf16[288,256]{1,0:T(8,128)(2,1)S(1)} %get-tuple-element.52), channel_id=1, source_target_pairs={{0,4},{1,3},{2,6},{3,1},{4,0},{5,7},{6,2},{7,5},{8,12},{9,11},{10,... | collective-permute-start | bytes 442376 | tf_op jit(solution)/shard_map/ppermute | solution.py:39
  30.4 0.8 %collective-permute-done.16.refs_1_ = bf16[384,256]{1,0:T(8,128)(2,1)S(1)} collective-permute-done((bf16[384,256]{1,0:T(8,128)(2,1)S(1)}, bf16[384,256]{1,0:T(8,128)(2,1)S(1)}, u32[]{:S(2)}, u32[]{:S(2)}) %collective-permute-start.16) | collective-permute-done | bytes 196640 | tf_op jit(solution)/shard_map/ppermute | solution.py:39
  31.2 3.0 %collective-permute-start.17 = (bf16[192,256]{1,0:T(8,128)(2,1)S(1)}, bf16[192,256]{1,0:T(8,128)(2,1)S(1)}, u32[]{:S(2)}, u32[]{:S(2)}) collective-permute-start(bf16[192,256]{1,0:T(8,128)(2,1)S(1)} %get-tuple-element.64), channel_id=1, source_target_pairs={{0,4},{1,3},{2,6},{3,1},{4,0},{5,7},{6,2},{7,5},{8,12},{9,11},{10,... | collective-permute-start | bytes 294920 | tf_op jit(solution)/shard_map/ppermute | solution.py:39
  34.3 1.6 %collective-permute-start.12 = (bf16[192,256]{1,0:T(8,128)(2,1)S(1)}, bf16[192,256]{1,0:T(8,128)(2,1)S(1)}, u32[]{:S(2)}, u32[]{:S(2)}) collective-permute-start(bf16[192,256]{1,0:T(8,128)(2,1)S(1)} %get-tuple-element.58), channel_id=1, source_target_pairs={{0,2},{1,5},{2,0},{3,7},{4,6},{5,1},{6,4},{7,3},{8,10},{9,13},{10,... | collective-permute-start | bytes 294920 | tf_op jit(solution)/shard_map/ppermute | solution.py:39
  35.9 2.7 %collective-permute-start.8 = (bf16[3,96,256]{2,1,0:T(8,128)(2,1)S(1)}, bf16[3,96,256]{2,1,0:T(8,128)(2,1)S(1)}, u32[]{:S(2)}, u32[]{:S(2)}) collective-permute-start(bf16[3,96,256]{2,1,0:T(8,128)(2,1)S(1)} %sum_parts.17.refs_0_), channel_id=1, source_target_pairs={{0,16},{8,24},{16,0},{24,8},{1,17},{9,25},{17,1},{25,9},{2,18},{10... | collective-permute-start | bytes 442376 | tf_op jit(solution)/shard_map/ppermute | solution.py:22
  38.7 0.8 %collective-permute-start.18 = (bf16[3,64,256]{2,1,0:T(8,128)(2,1)S(1)}, bf16[3,64,256]{2,1,0:T(8,128)(2,1)S(1)}, u32[]{:S(2)}, u32[]{:S(2)}) collective-permute-start(bf16[3,64,256]{2,1,0:T(8,128)(2,1)S(1)} %sum_parts.23.refs_0_), channel_id=1, source_target_pairs={{0,16},{8,24},{16,0},{24,8},{1,17},{9,25},{17,1},{25,9},{2,18},{10... | collective-permute-start | bytes 294920 | tf_op jit(solution)/shard_map/ppermute | solution.py:22
  39.6 2.2 %collective-permute-start.13 = (bf16[3,64,256]{2,1,0:T(8,128)(2,1)S(1)}, bf16[3,64,256]{2,1,0:T(8,128)(2,1)S(1)}, u32[]{:S(2)}, u32[]{:S(2)}) collective-permute-start(bf16[3,64,256]{2,1,0:T(8,128)(2,1)S(1)} %sum_parts.20.refs_0_), channel_id=1, source_target_pairs={{0,16},{8,24},{16,0},{24,8},{1,17},{9,25},{17,1},{25,9},{2,18},{10... | collective-permute-start | bytes 294920 | tf_op jit(solution)/shard_map/ppermute | solution.py:22
  42.1 1.7 %collective-permute-done.1.refs_1_ = bf16[192,256]{1,0:T(8,128)(2,1)S(1)} collective-permute-done((bf16[192,256]{1,0:T(8,128)(2,1)S(1)}, bf16[192,256]{1,0:T(8,128)(2,1)S(1)}, u32[]{:S(2)}, u32[]{:S(2)}) %collective-permute-start.1) | collective-permute-done | bytes 98336 | tf_op jit(solution)/shard_map/ppermute | solution.py:39
  43.9 5.5 %collective-permute-done.8.refs_1_ = bf16[3,96,256]{2,1,0:T(8,128)(2,1)S(1)} collective-permute-done((bf16[3,96,256]{2,1,0:T(8,128)(2,1)S(1)}, bf16[3,96,256]{2,1,0:T(8,128)(2,1)S(1)}, u32[]{:S(2)}, u32[]{:S(2)}) %collective-permute-start.8) | collective-permute-done | bytes 147488 | tf_op jit(solution)/shard_map/ppermute | solution.py:22
  49.7 0.9 %collective-permute-done.18.refs_1_ = bf16[3,64,256]{2,1,0:T(8,128)(2,1)S(1)} collective-permute-done((bf16[3,64,256]{2,1,0:T(8,128)(2,1)S(1)}, bf16[3,64,256]{2,1,0:T(8,128)(2,1)S(1)}, u32[]{:S(2)}, u32[]{:S(2)}) %collective-permute-start.18) | collective-permute-done | bytes 98336 | tf_op jit(solution)/shard_map/ppermute | solution.py:22
  50.9 1.2 %collective-permute-start.19 = (bf16[3,64,256]{2,1,0:T(8,128)(2,1)S(1)}, bf16[3,64,256]{2,1,0:T(8,128)(2,1)S(1)}, u32[]{:S(2)}, u32[]{:S(2)}) collective-permute-start(bf16[3,64,256]{2,1,0:T(8,128)(2,1)S(1)} %middle_level.7.own_ref), channel_id=1, source_target_pairs={{0,8},{8,0},{16,24},{24,16},{1,9},{9,1},{17,25},{25,17},{2,10},{10... | collective-permute-start | bytes 294920 | tf_op jit(solution)/shard_map/ppermute | solution.py:22
  52.2 1.0 %collective-permute-start.14 = (bf16[3,64,256]{2,1,0:T(8,128)(2,1)S(1)}, bf16[3,64,256]{2,1,0:T(8,128)(2,1)S(1)}, u32[]{:S(2)}, u32[]{:S(2)}) collective-permute-start(bf16[3,64,256]{2,1,0:T(8,128)(2,1)S(1)} %middle_level.6.own_ref), channel_id=1, source_target_pairs={{0,8},{8,0},{16,24},{24,16},{1,9},{9,1},{17,25},{25,17},{2,10},{10... | collective-permute-start | bytes 294920 | tf_op jit(solution)/shard_map/ppermute | solution.py:22
  53.3 2.8 %collective-permute-start.3 = (bf16[3,32,256]{2,1,0:T(8,128)(2,1)S(1)}, bf16[3,32,256]{2,1,0:T(8,128)(2,1)S(1)}, u32[]{:S(2)}, u32[]{:S(2)}) collective-permute-start(bf16[3,32,256]{2,1,0:T(8,128)(2,1)S(1)} %sum_parts.14.refs_0_), channel_id=1, source_target_pairs={{0,16},{8,24},{16,0},{24,8},{1,17},{9,25},{17,1},{25,9},{2,18},{10... | collective-permute-start | bytes 147464 | tf_op jit(solution)/shard_map/ppermute | solution.py:22
  56.1 2.8 %collective-permute-done.3.refs_1_ = bf16[3,32,256]{2,1,0:T(8,128)(2,1)S(1)} collective-permute-done((bf16[3,32,256]{2,1,0:T(8,128)(2,1)S(1)}, bf16[3,32,256]{2,1,0:T(8,128)(2,1)S(1)}, u32[]{:S(2)}, u32[]{:S(2)}) %collective-permute-start.3) | collective-permute-done | bytes 49184 | tf_op jit(solution)/shard_map/ppermute | solution.py:22
  59.1 2.0 %collective-permute-start.4 = (bf16[3,32,256]{2,1,0:T(8,128)(2,1)S(1)}, bf16[3,32,256]{2,1,0:T(8,128)(2,1)S(1)}, u32[]{:S(2)}, u32[]{:S(2)}) collective-permute-start(bf16[3,32,256]{2,1,0:T(8,128)(2,1)S(1)} %middle_level.4.own_ref), channel_id=1, source_target_pairs={{0,8},{8,0},{16,24},{24,16},{1,9},{9,1},{17,25},{25,17},{2,10},{10... | collective-permute-start | bytes 147464 | tf_op jit(solution)/shard_map/ppermute | solution.py:22
  62.3 1.0 %collective-permute-done.4.partner_ref = bf16[3,32,256]{2,1,0:T(8,128)(2,1)S(1)} collective-permute-done((bf16[3,32,256]{2,1,0:T(8,128)(2,1)S(1)}, bf16[3,32,256]{2,1,0:T(8,128)(2,1)S(1)}, u32[]{:S(2)}, u32[]{:S(2)}) %collective-permute-start.4) | collective-permute-done | bytes 49184 | tf_op jit(solution)/shard_map/ppermute | solution.py:22
  63.2 1.2 %final_level.1 = f32[2,3,256,256]{3,2,1,0:T(8,128)} custom-call(bf16[3,32,256]{2,1,0:T(8,128)(2,1)S(1)} %middle_level.4.own_ref, bf16[3,32,256]{2,1,0:T(8,128)(2,1)S(1)} %collective-permute-done.4.partner_ref, bf16[512,512]{1,0:T(8,128)(2,1)S(1)} %get-tuple-element.46.weight_ref, f32[1,256]{1,0:T(1,128)S(1)} %bitcast.6, ...), custom_call_target="tpu_custom_call" | custom-call | tf_op jit(solution)/shard_map/final_level/pallas_call | solution.py:438
  (47 shorter events, 4.6 us)
Async XLA Ops:
  9.8 9.0 %collective-permute-start.5 = (bf16[4,3,96,256]{3,2,1,0:T(8,128)(2,1)S(1)}, bf16[4,3,96,256]{3,2,1,0:T(8,128)(2,1)S(1)}, u32[]{:S(2)}, u32[]{:S(2)}) collective-permute-start(bf16[4,3,96,256]{3,2,1,0:T(8,128)(2,1)S(1)} %get-tuple-element.48), channel_id=1, source_target_pairs={{0,1},{1,0},{2,3},{3,2},{4,5},{5,4},{6,7},{7,6},{8,9},{9,8},{10,11... | collective-permute-start | bytes 1769480 | tf_op jit(solution)/shard_map/ppermute | solution.py:22
  18.2 3.3 %collective-permute-start.15 = (bf16[4,3,64,256]{3,2,1,0:T(8,128)(2,1)S(1)}, bf16[4,3,64,256]{3,2,1,0:T(8,128)(2,1)S(1)}, u32[]{:S(2)}, u32[]{:S(2)}) collective-permute-start(bf16[4,3,64,256]{3,2,1,0:T(8,128)(2,1)S(1)} %get-tuple-element.60), channel_id=1, source_target_pairs={{0,1},{1,0},{2,3},{3,2},{4,5},{5,4},{6,7},{7,6},{8,9},{9,8},{10,11... | collective-permute-start | bytes 1179656 | tf_op jit(solution)/shard_map/ppermute | solution.py:22
  18.3 4.5 %collective-permute-start.10 = (bf16[4,3,64,256]{3,2,1,0:T(8,128)(2,1)S(1)}, bf16[4,3,64,256]{3,2,1,0:T(8,128)(2,1)S(1)}, u32[]{:S(2)}, u32[]{:S(2)}) collective-permute-start(bf16[4,3,64,256]{3,2,1,0:T(8,128)(2,1)S(1)} %get-tuple-element.54), channel_id=1, source_target_pairs={{0,1},{1,0},{2,3},{3,2},{4,5},{5,4},{6,7},{7,6},{8,9},{9,8},{10,11... | collective-permute-start | bytes 1179656 | tf_op jit(solution)/shard_map/ppermute | solution.py:22
  18.9 8.0 %collective-permute-start.6 = (bf16[576,256]{1,0:T(8,128)(2,1)S(1)}, bf16[576,256]{1,0:T(8,128)(2,1)S(1)}, u32[]{:S(2)}, u32[]{:S(2)}) collective-permute-start(bf16[576,256]{1,0:T(8,128)(2,1)S(1)} %get-tuple-element.50), channel_id=1, source_target_pairs={{0,2},{1,5},{2,0},{3,7},{4,6},{5,1},{6,4},{7,3},{8,10},{9,13},{10,... | collective-permute-start | bytes 884744 | tf_op jit(solution)/shard_map/ppermute | solution.py:39
  21.7 9.5 %collective-permute-start.16 = (bf16[384,256]{1,0:T(8,128)(2,1)S(1)}, bf16[384,256]{1,0:T(8,128)(2,1)S(1)}, u32[]{:S(2)}, u32[]{:S(2)}) collective-permute-start(bf16[384,256]{1,0:T(8,128)(2,1)S(1)} %get-tuple-element.62), channel_id=1, source_target_pairs={{0,2},{1,5},{2,0},{3,7},{4,6},{5,1},{6,4},{7,3},{8,10},{9,13},{10,... | collective-permute-start | bytes 589832 | tf_op jit(solution)/shard_map/ppermute | solution.py:39
  22.9 11.3 %collective-permute-start.11 = (bf16[384,256]{1,0:T(8,128)(2,1)S(1)}, bf16[384,256]{1,0:T(8,128)(2,1)S(1)}, u32[]{:S(2)}, u32[]{:S(2)}) collective-permute-start(bf16[384,256]{1,0:T(8,128)(2,1)S(1)} %get-tuple-element.56), channel_id=1, source_target_pairs={{0,4},{1,3},{2,6},{3,1},{4,0},{5,7},{6,2},{7,5},{8,12},{9,11},{10,... | collective-permute-start | bytes 589832 | tf_op jit(solution)/shard_map/ppermute | solution.py:39
  26.6 15.2 %copy-start = (bf16[2,1,2,256,128]{4,3,2,1,0:T(8,128)(2,1)S(1)}, bf16[2,1,2,256,128]{4,3,2,1,0:T(8,128)(2,1)}, u32[]{:S(2)}) copy-start(bf16[2,1,2,256,128]{4,3,2,1,0:T(8,128)(2,1)} %proj_ref.3) | copy-start | bytes 786436
  26.6 15.2 %copy-start.1 = (bf16[2,1,2,256,256]{4,3,2,1,0:T(8,128)(2,1)S(1)}, bf16[2,1,2,256,256]{4,3,2,1,0:T(8,128)(2,1)}, u32[]{:S(2)}) copy-start(bf16[2,1,2,256,256]{4,3,2,1,0:T(8,128)(2,1)} %inv_ref.1) | copy-start | bytes 1572868
  26.6 11.9 %collective-permute-start = (bf16[4,3,32,256]{3,2,1,0:T(8,128)(2,1)S(1)}, bf16[4,3,32,256]{3,2,1,0:T(8,128)(2,1)S(1)}, u32[]{:S(2)}, u32[]{:S(2)}) collective-permute-start(bf16[4,3,32,256]{3,2,1,0:T(8,128)(2,1)S(1)} %get-tuple-element.40), channel_id=1, source_target_pairs={{0,1},{1,0},{2,3},{3,2},{4,5},{5,4},{6,7},{7,6},{8,9},{9,8},{10,11... | collective-permute-start | bytes 589832 | tf_op jit(solution)/shard_map/ppermute | solution.py:22
  27.0 8.8 %collective-permute-start.7 = (bf16[288,256]{1,0:T(8,128)(2,1)S(1)}, bf16[288,256]{1,0:T(8,128)(2,1)S(1)}, u32[]{:S(2)}, u32[]{:S(2)}) collective-permute-start(bf16[288,256]{1,0:T(8,128)(2,1)S(1)} %get-tuple-element.52), channel_id=1, source_target_pairs={{0,4},{1,3},{2,6},{3,1},{4,0},{5,7},{6,2},{7,5},{8,12},{9,11},{10,... | collective-permute-start | bytes 442376 | tf_op jit(solution)/shard_map/ppermute | solution.py:39
  31.2 29.9 %copy-start.2 = (f32[256]{0:T(256)S(1)}, f32[256]{0:T(256)}, u32[]{:S(2)}) copy-start(f32[256]{0:T(256)} %param.9) | copy-start | bytes 3076
  31.2 7.5 %collective-permute-start.17 = (bf16[192,256]{1,0:T(8,128)(2,1)S(1)}, bf16[192,256]{1,0:T(8,128)(2,1)S(1)}, u32[]{:S(2)}, u32[]{:S(2)}) collective-permute-start(bf16[192,256]{1,0:T(8,128)(2,1)S(1)} %get-tuple-element.64), channel_id=1, source_target_pairs={{0,4},{1,3},{2,6},{3,1},{4,0},{5,7},{6,2},{7,5},{8,12},{9,11},{10,... | collective-permute-start | bytes 294920 | tf_op jit(solution)/shard_map/ppermute | solution.py:39
  34.3 5.3 %collective-permute-start.12 = (bf16[192,256]{1,0:T(8,128)(2,1)S(1)}, bf16[192,256]{1,0:T(8,128)(2,1)S(1)}, u32[]{:S(2)}, u32[]{:S(2)}) collective-permute-start(bf16[192,256]{1,0:T(8,128)(2,1)S(1)} %get-tuple-element.58), channel_id=1, source_target_pairs={{0,2},{1,5},{2,0},{3,7},{4,6},{5,1},{6,4},{7,3},{8,10},{9,13},{10,... | collective-permute-start | bytes 294920 | tf_op jit(solution)/shard_map/ppermute | solution.py:39
  35.9 13.6 %collective-permute-start.8 = (bf16[3,96,256]{2,1,0:T(8,128)(2,1)S(1)}, bf16[3,96,256]{2,1,0:T(8,128)(2,1)S(1)}, u32[]{:S(2)}, u32[]{:S(2)}) collective-permute-start(bf16[3,96,256]{2,1,0:T(8,128)(2,1)S(1)} %sum_parts.17.refs_0_), channel_id=1, source_target_pairs={{0,16},{8,24},{16,0},{24,8},{1,17},{9,25},{17,1},{25,9},{2,18},{10... | collective-permute-start | bytes 442376 | tf_op jit(solution)/shard_map/ppermute | solution.py:22
  38.6 5.2 %collective-permute-start.1 = (bf16[192,256]{1,0:T(8,128)(2,1)S(1)}, bf16[192,256]{1,0:T(8,128)(2,1)S(1)}, u32[]{:S(2)}, u32[]{:S(2)}) collective-permute-start(bf16[192,256]{1,0:T(8,128)(2,1)S(1)} %get-tuple-element.42), channel_id=1, source_target_pairs={{0,4},{1,3},{2,6},{3,1},{4,0},{5,7},{6,2},{7,5},{8,12},{9,11},{10,... | collective-permute-start | bytes 294920 | tf_op jit(solution)/shard_map/ppermute | solution.py:39
  38.7 11.9 %collective-permute-start.18 = (bf16[3,64,256]{2,1,0:T(8,128)(2,1)S(1)}, bf16[3,64,256]{2,1,0:T(8,128)(2,1)S(1)}, u32[]{:S(2)}, u32[]{:S(2)}) collective-permute-start(bf16[3,64,256]{2,1,0:T(8,128)(2,1)S(1)} %sum_parts.23.refs_0_), channel_id=1, source_target_pairs={{0,16},{8,24},{16,0},{24,8},{1,17},{9,25},{17,1},{25,9},{2,18},{10... | collective-permute-start | bytes 294920 | tf_op jit(solution)/shard_map/ppermute | solution.py:22
  39.6 12.5 %collective-permute-start.13 = (bf16[3,64,256]{2,1,0:T(8,128)(2,1)S(1)}, bf16[3,64,256]{2,1,0:T(8,128)(2,1)S(1)}, u32[]{:S(2)}, u32[]{:S(2)}) collective-permute-start(bf16[3,64,256]{2,1,0:T(8,128)(2,1)S(1)} %sum_parts.20.refs_0_), channel_id=1, source_target_pairs={{0,16},{8,24},{16,0},{24,8},{1,17},{9,25},{17,1},{25,9},{2,18},{10... | collective-permute-start | bytes 294920 | tf_op jit(solution)/shard_map/ppermute | solution.py:22
  43.8 9.5 %collective-permute-start.2 = (bf16[96,256]{1,0:T(8,128)(2,1)S(1)}, bf16[96,256]{1,0:T(8,128)(2,1)S(1)}, u32[]{:S(2)}, u32[]{:S(2)}) collective-permute-start(bf16[96,256]{1,0:T(8,128)(2,1)S(1)} %get-tuple-element.44), channel_id=1, source_target_pairs={{0,2},{1,5},{2,0},{3,7},{4,6},{5,1},{6,4},{7,3},{8,10},{9,13},{10,... | collective-permute-start | bytes 147464 | tf_op jit(solution)/shard_map/ppermute | solution.py:39
  49.7 12.2 %collective-permute-start.9 = (bf16[3,96,256]{2,1,0:T(8,128)(2,1)S(1)}, bf16[3,96,256]{2,1,0:T(8,128)(2,1)S(1)}, u32[]{:S(2)}, u32[]{:S(2)}) collective-permute-start(bf16[3,96,256]{2,1,0:T(8,128)(2,1)S(1)} %middle_level.5.own_ref), channel_id=1, source_target_pairs={{0,8},{8,0},{16,24},{24,16},{1,9},{9,1},{17,25},{25,17},{2,10},{10... | collective-permute-start | bytes 442376 | tf_op jit(solution)/shard_map/ppermute | solution.py:22
  50.9 10.2 %collective-permute-start.19 = (bf16[3,64,256]{2,1,0:T(8,128)(2,1)S(1)}, bf16[3,64,256]{2,1,0:T(8,128)(2,1)S(1)}, u32[]{:S(2)}, u32[]{:S(2)}) collective-permute-start(bf16[3,64,256]{2,1,0:T(8,128)(2,1)S(1)} %middle_level.7.own_ref), channel_id=1, source_target_pairs={{0,8},{8,0},{16,24},{24,16},{1,9},{9,1},{17,25},{25,17},{2,10},{10... | collective-permute-start | bytes 294920 | tf_op jit(solution)/shard_map/ppermute | solution.py:22
  52.2 9.2 %collective-permute-start.14 = (bf16[3,64,256]{2,1,0:T(8,128)(2,1)S(1)}, bf16[3,64,256]{2,1,0:T(8,128)(2,1)S(1)}, u32[]{:S(2)}, u32[]{:S(2)}) collective-permute-start(bf16[3,64,256]{2,1,0:T(8,128)(2,1)S(1)} %middle_level.6.own_ref), channel_id=1, source_target_pairs={{0,8},{8,0},{16,24},{24,16},{1,9},{9,1},{17,25},{25,17},{2,10},{10... | collective-permute-start | bytes 294920 | tf_op jit(solution)/shard_map/ppermute | solution.py:22
  53.3 5.6 %collective-permute-start.3 = (bf16[3,32,256]{2,1,0:T(8,128)(2,1)S(1)}, bf16[3,32,256]{2,1,0:T(8,128)(2,1)S(1)}, u32[]{:S(2)}, u32[]{:S(2)}) collective-permute-start(bf16[3,32,256]{2,1,0:T(8,128)(2,1)S(1)} %sum_parts.14.refs_0_), channel_id=1, source_target_pairs={{0,16},{8,24},{16,0},{24,8},{1,17},{9,25},{17,1},{25,9},{2,18},{10... | collective-permute-start | bytes 147464 | tf_op jit(solution)/shard_map/ppermute | solution.py:22
  59.1 4.2 %collective-permute-start.4 = (bf16[3,32,256]{2,1,0:T(8,128)(2,1)S(1)}, bf16[3,32,256]{2,1,0:T(8,128)(2,1)S(1)}, u32[]{:S(2)}, u32[]{:S(2)}) collective-permute-start(bf16[3,32,256]{2,1,0:T(8,128)(2,1)S(1)} %middle_level.4.own_ref), channel_id=1, source_target_pairs={{0,8},{8,0},{16,24},{24,16},{1,9},{9,1},{17,25},{25,17},{2,10},{10... | collective-permute-start | bytes 147464 | tf_op jit(solution)/shard_map/ppermute | solution.py:22

commit v3 on v2

--- a/solution.py
+++ b/solution.py
@@ -7,9 +7,10 @@
 from jax.sharding import PartitionSpec as P
 
 epsilon = 1e-06
-shares = (3, 2, 2, 1)
+shares = (2, 2, 2, 2)
+splits = (1, 1, 1, 1)
 groups = ((0,), (1,), (2,), (3,))
-exchanges = (((0, 0),), ((0, 1),), ((1, 0),), ((1, 1),), ((2, 0),), ((2, 1),), ((3, 0),), ((3, 1),))
+exchanges = (((0, 0),), ((0, 1), (1, 0)), ((1, 1),), ((2, 0),), ((2, 1),), ((3, 0),), ((3, 1),))
 project_steps = 4
 mib = 1024 * 1024
 in_vmem = pl.BlockSpec(memory_space=pltpu.VMEM)
@@ -67,8 +68,9 @@
     return place ^ jnp.where(place % 2 == 0, turns[0], turns[1])
 
 
-def write_pieces(place, acc_ref, keep_ref, send_ref, chunk):
-    halves, passes, chunk_rows, width = keep_ref.shape
+def write_pieces(place, acc_ref, keep_ref, send_ref, chunk, first, chunk_rows):
+    halves, passes, _, width = keep_ref.shape
+    kept = slice(first, first + chunk_rows)
     rank = width // 2
     segments = 2 * halves
     for turn in range(segments):
@@ -80,8 +82,8 @@
         for one in range(passes):
             re = slice(2 * one * rank, (2 * one + 1) * rank)
             im = slice((2 * one + 1) * rank, (2 * one + 2) * rank)
-            out_ref[turn // 2, one, :, :rank] = (upper[:, re] - lower[:, im]).astype(jnp.bfloat16)
-            out_ref[turn // 2, one, :, rank:] = (upper[:, im] + lower[:, re]).astype(jnp.bfloat16)
+            out_ref[turn // 2, one, kept, :rank] = (upper[:, re] - lower[:, im]).astype(jnp.bfloat16)
+            out_ref[turn // 2, one, kept, rank:] = (upper[:, im] + lower[:, re]).astype(jnp.bfloat16)
 
 
 def block_copies(kernel_ref, block_ref, sems, span, part):
@@ -120,8 +122,6 @@
     proj_copy.start()
     for step in range(project_steps):
         sketch_copy(step).start()
-    for copy in block_copies(kernel_ref, block_ref, block_sems, spans[0], 0):
-        copy.start()
     next_copies = []
     if len(spans) > 1:
         next_copies = both_copies(kernel_ref, next_ref, next_sems, spans[1])
@@ -148,14 +148,15 @@
         acc_ref[part] = product(block_ref[part].reshape(-1, cols), sk_ref[...])
         return carry
 
-    lax.fori_loop(0, 1, project, 0)
-    for copy in block_copies(kernel_ref, block_ref, block_sems, spans[0], 1):
-        copy.start()
-    lax.fori_loop(1, project_steps, project, 0)
+    for part in range(2):
+        lax.fori_loop(part, part + 1, project, 0)
+        for copy in block_copies(kernel_ref, block_ref, block_sems, spans[0], part):
+            copy.start()
+    lax.fori_loop(2, project_steps, project, 0)
     lax.fori_loop(0, 2, gather, 0)
-    write_pieces(place_ref[0], acc_ref, keep_ref, send_ref, 0)
-    for copy in next_copies:
-        copy.wait()
+    write_pieces(place_ref[0], acc_ref, keep_ref, send_ref, 0, 0, spans[0][1])
+    if len(spans) > 1:
+        wait_all(kernel_ref, next_ref, next_sems, spans[1])
 
 
 def cost_of(kernel, span, width):
@@ -167,12 +168,12 @@
     )
 
 
-def first_gathered(place, kernel, sketch, projections, spans):
+def first_gathered(place, kernel, sketch, projections, spans, chunk_rows):
     _, segments, _, cols = kernel.shape
     passes, _, sketch_cols = sketch.shape
     rank = projections.shape[4]
     width = 2 * passes * rank
-    piece = pltpu.VMEM((segments // 2, passes, spans[0][1], 2 * rank), jnp.bfloat16)
+    piece = pltpu.VMEM((segments // 2, passes, chunk_rows, 2 * rank), jnp.bfloat16)
     out_shape = [piece, piece, pltpu.VMEM((cols, width), jnp.bfloat16)]
     scratch = [
         pltpu.VMEM(sketch.shape, sketch.dtype),
@@ -198,54 +199,74 @@
     )(place, remote(kernel), remote(sketch), remote(projections))
 
 
-def gather_body(place_ref, block_ref, sk_ref, *rest, chunk, next_span):
-    step = pl.program_id(0)
-    copies = []
-    if next_span is None:
-        keep_ref, send_ref, acc_ref = rest
+def wait_all(kernel_ref, block_ref, sems, span):
+    def part_wait(part, carry):
+        for copy in block_copies(kernel_ref, block_ref, sems, span, part):
+            copy.wait()
+        return carry
+
+    lax.fori_loop(0, 2, part_wait, 0)
+
+
+def start_all(kernel_ref, block_ref, sems, span):
+    def part_start(part, carry):
+        for copy in block_copies(kernel_ref, block_ref, sems, span, part):
+            copy.start()
+        return carry
+
+    lax.fori_loop(0, 2, part_start, 0)
+
+
+def gather_body(place_ref, block_ref, sk_ref, *rest, chunk, first, next_span, filled):
+    rest = list(rest)
+    if next_span is not None:
+        kernel_ref = rest.pop(0)
+    if filled:
+        del rest[:2]
+    keep_ref, send_ref, *rest = rest
+    if next_span is not None:
+        next_ref, acc_ref, sems = rest
+        start_all(kernel_ref, next_ref, sems, next_span)
     else:
-        kernel_ref, keep_ref, send_ref, next_ref, acc_ref, sems = rest
-        copies = both_copies(kernel_ref, next_ref, sems, next_span)
-
-        @pl.when(step == 0)
-        def _():
-            for copy in copies:
-                copy.start()
-
-    cols = block_ref.shape[3]
-    acc_ref[step] = product(block_ref[step].reshape(-1, cols), sk_ref[...])
-
-    @pl.when(step == 1)
-    def _():
-        write_pieces(place_ref[0], acc_ref, keep_ref, send_ref, chunk)
-        for copy in copies:
-            copy.wait()
-
-
-def gathered(place, block, sk_value, kernel, passes, chunk, spans):
-    _, segments, chunk_rows, cols = block.shape
+        (acc_ref,) = rest
+    rows, cols = block_ref.shape[2:]
+    both = product(block_ref[...].reshape(-1, cols), sk_ref[...])
+    acc_ref[...] = both.reshape(acc_ref.shape)
+    write_pieces(place_ref[0], acc_ref, keep_ref, send_ref, chunk, first, rows)
+    if next_span is not None:
+        wait_all(kernel_ref, next_ref, sems, next_span)
+
+
+def gathered(place, block, sk_value, kernel, passes, chunk, first, chunk_rows, next_span, partly):
+    _, segments, rows, cols = block.shape
     width = sk_value.shape[1]
     piece = pltpu.VMEM((segments // 2, passes, chunk_rows, width // passes), jnp.bfloat16)
     operands = [place, local(block), local(sk_value)]
     in_specs = [in_smem, in_vmem, in_vmem]
     out_shape = [piece, piece]
-    scratch = [pltpu.VMEM((2, segments * chunk_rows, width), jnp.float32)]
-    next_span = spans[chunk + 1] if chunk + 1 < len(spans) else None
+    scratch = [pltpu.VMEM((2, segments * rows, width), jnp.float32)]
+    aliases = {}
     if next_span is not None:
         operands.append(remote(kernel))
         in_specs.append(in_hbm)
         out_shape.append(pltpu.VMEM((2, segments, next_span[1], cols), jnp.bfloat16))
         scratch.append(pltpu.SemaphoreType.DMA((2, segments)))
+    if partly is not None:
+        aliases = {len(operands): 0, len(operands) + 1: 1}
+        operands.extend(map(local, partly))
+        in_specs.extend([in_vmem, in_vmem])
     return pl.pallas_call(
-        functools.partial(gather_body, chunk=chunk, next_span=next_span),
+        functools.partial(
+            gather_body, chunk=chunk, first=first, next_span=next_span, filled=partly is not None
+        ),
         name="gather",
-        grid=(2,),
         in_specs=in_specs,
         out_specs=[in_vmem] * len(out_shape),
         out_shape=out_shape,
         scratch_shapes=scratch,
+        input_output_aliases=aliases,
         compiler_params=params(12),
-        cost_estimate=cost_of(kernel, spans[chunk], width),
+        cost_estimate=cost_of(kernel, (0, rows), width),
     )(*operands)
 
 
@@ -470,15 +491,30 @@
     keeps = []
     cores = []
     block = None
-    for chunk in range(chunks):
-        if chunk == 0:
-            keep, send, sk_value, *blocks = first_gathered(place, kernel, sketch, projections, spans)
+    pieces = []
+    for chunk, span in enumerate(spans):
+        rows = span[1] // splits[chunk]
+        pieces.extend((chunk, part * rows, (span[0] + part * rows, rows)) for part in range(splits[chunk]))
+    filled = None
+    for number, (chunk, first, span) in enumerate(pieces):
+        next_span = pieces[number + 1][2] if number + 1 < len(pieces) else None
+        chunk_rows = spans[chunk][1]
+        if number == 0:
+            both = [span] if next_span is None else [span, next_span]
+            keep, send, sk_value, *blocks = first_gathered(
+                place, kernel, sketch, projections, both, chunk_rows
+            )
         else:
-            keep, send, *blocks = gathered(place, block, sk_value, kernel, passes, chunk, spans)
+            keep, send, *blocks = gathered(
+                place, block, sk_value, kernel, passes, chunk, first, chunk_rows, next_span, filled
+            )
+        filled = (keep, send)
         if blocks:
             block = blocks[0]
-        keeps.append(keep)
-        cores.append(swapped(send, "sk", 1))
+        if first + span[1] == chunk_rows:
+            filled = None
+            keeps.append(keep)
+            cores.append(swapped(send, "sk", 1))
     held = dict(enumerate(keeps))
     got = {chunk: (core, None) for chunk, core in enumerate(cores)}
     for place, exchange in enumerate(plan_of(count)):

time: 64.5 us -> 69.1 us (1.071)
  waiting for transfers between devices: 13 us -> 26 us
  starting transfers between devices: 27.5 us -> 20 us
  Pallas kernels: 23.7 us -> 22.6 us
    ppermute x8 -> x7, waiting for transfers between devices: 2.77 us -> 10.8 us  [swapped_step(): return lax.ppermute(value, 'sk', pairs)]
    ppermute x12, waiting for transfers between devices: 10.2 us -> 15.2 us  [swapped(): return lax.ppermute(value, axis, pairs)]
    ppermute x12, starting transfers between devices: 14 us -> 9.97 us  [swapped(): return lax.ppermute(value, axis, pairs)]
    ppermute x8 -> x7, starting transfers between devices: 13.5 us -> 10 us  [swapped_step(): return lax.ppermute(value, 'sk', pairs)]
    pallas_call x1, Pallas kernels: 9.76 us -> 7.39 us  [first_gathered(): pl.pallas_call(functools.partial(first_body, spans=spans), name='gather_f...]
    pallas_call x3, Pallas kernels: 9.97 us -> 11.3 us  [gathered(): pl.pallas_call(functools.partial(gather_body, chunk=chunk, first=first, n...]
  transfers between devices with their start and end apart: 20 -> 19, of which waited for: 7 -> 10; matrix products, arithmetic and copies ran while one was open for 0% -> 0% of each run, Pallas kernels for 20% -> 20%
where the time goes in v3:
time: 69.1 us; the launch traced here: 68.9 us
  waiting for transfers between devices  26 us (38%)
  Pallas kernels  22.6 us (33%)
  starting transfers between devices  20 us (29%)
    ppermute x12, waiting for transfers between devices, swapped(): return lax.ppermute(value, axis, pairs)  15.2 us
    pallas_call x3, Pallas kernels, gathered(): pl.pallas_call(functools.partial(gather_body, chunk=chunk, first=first, n...  11.3 us
    ppermute x7, waiting for transfers between devices, swapped_step(): return lax.ppermute(value, 'sk', pairs)  10.8 us
    ppermute x7, starting transfers between devices, swapped_step(): return lax.ppermute(value, 'sk', pairs)  10 us
    ppermute x12, starting transfers between devices, swapped(): return lax.ppermute(value, axis, pairs)  9.97 us
    pallas_call x1, Pallas kernels, first_gathered(): pl.pallas_call(functools.partial(first_body, spans=spans), name='gather_f...  7.39 us
  transfers between devices with their start and end apart: 19, of which 10 were waited for; matrix products, arithmetic and copies ran while one was open for 0% of the time, Pallas kernels for 20%

profile of v3, /device:TPU:0, one launch (start us, length us, event | category | flops | bytes accessed | tf_op | source)
XLA Modules:
  0.0 68.9 jit_solution(11237593482995274982)
XLA Ops:
  0.0 7.4 %gather_first.1 = (bf16[4,3,64,256]{3,2,1,0:T(8,128)(2,1)S(1)}, bf16[4,3,64,256]{3,2,1,0:T(8,128)(2,1)S(1)}, bf16[2048,768]{1,0:T(8,128)(2,1)S(1)}, bf16[2,8,64,2048]{3,2,1,0:T(8,128)(2,1)S(1)}) custom-call(s32[1]{0:T(128)} %bitcast.place_ref, bf16[2,8,256,2048]{3,2,1,0:T(8,128)(2,1)} %bitcast.7, bf16[3,2048,256]{2,1,0:T(8,128)(2,1)} %sketch_ref.1, ...), custom_call_target="tpu_custom_call" | custom-call | flops 3221225472 | bytes 4194304 | tf_op jit(solution)/shard_map/gather_first/pallas_call | solution.py:190
  8.0 3.8 %gather.3 = (bf16[4,3,64,256]{3,2,1,0:T(8,128)(2,1)S(1)}, bf16[4,3,64,256]{3,2,1,0:T(8,128)(2,1)S(1)}, bf16[2,8,64,2048]{3,2,1,0:T(8,128)(2,1)S(1)}) custom-call(s32[1]{0:T(128)} %bitcast.place_ref, bf16[2,8,64,2048]{3,2,1,0:T(8,128)(2,1)S(1)} %get-tuple-element.34.block_ref, bf16[2048,768]{1,0:T(8,128)(2,1)S(1)} %get-tuple-element.35.sk_ref, ...), custom_call_target="tpu_custom_call" | custom-call | flops 3221225472 | bytes 4194304 | tf_op jit(solution)/shard_map/gather/pallas_call | solution.py:258
  11.8 3.9 %gather.4 = (bf16[4,3,64,256]{3,2,1,0:T(8,128)(2,1)S(1)}, bf16[4,3,64,256]{3,2,1,0:T(8,128)(2,1)S(1)}, bf16[2,8,64,2048]{3,2,1,0:T(8,128)(2,1)S(1)}) custom-call(s32[1]{0:T(128)} %bitcast.place_ref, bf16[2,8,64,2048]{3,2,1,0:T(8,128)(2,1)S(1)} %get-tuple-element.36.block_ref, bf16[2048,768]{1,0:T(8,128)(2,1)S(1)} %get-tuple-element.35.sk_ref, ...), custom_call_target="tpu_custom_call" | custom-call | flops 3221225472 | bytes 4194304 | tf_op jit(solution)/shard_map/gather/pallas_call | solution.py:258
  16.3 3.6 %gather.5 = (bf16[4,3,64,256]{3,2,1,0:T(8,128)(2,1)S(1)}, bf16[4,3,64,256]{3,2,1,0:T(8,128)(2,1)S(1)}) custom-call(s32[1]{0:T(128)} %bitcast.place_ref, bf16[2,8,64,2048]{3,2,1,0:T(8,128)(2,1)S(1)} %get-tuple-element.37.block_ref, bf16[2048,768]{1,0:T(8,128)(2,1)S(1)} %get-tuple-element.35.sk_ref), custom_call_target="tpu_custom_call" | custom-call | flops 3221225472 | bytes 4194304 | tf_op jit(solution)/shard_map/gather/pallas_call | solution.py:258
  20.1 3.0 %collective-permute-start.6 = (bf16[384,256]{1,0:T(8,128)(2,1)S(1)}, bf16[384,256]{1,0:T(8,128)(2,1)S(1)}, u32[]{:S(2)}, u32[]{:S(2)}) collective-permute-start(bf16[384,256]{1,0:T(8,128)(2,1)S(1)} %get-tuple-element.49), channel_id=1, source_target_pairs={{0,2},{1,5},{2,0},{3,7},{4,6},{5,1},{6,4},{7,3},{8,10},{9,13},{10,... | collective-permute-start | bytes 589832 | tf_op jit(solution)/shard_map/ppermute | solution.py:40
  23.1 3.6 %collective-permute-done.6.refs_1_ = bf16[384,256]{1,0:T(8,128)(2,1)S(1)} collective-permute-done((bf16[384,256]{1,0:T(8,128)(2,1)S(1)}, bf16[384,256]{1,0:T(8,128)(2,1)S(1)}, u32[]{:S(2)}, u32[]{:S(2)}) %collective-permute-start.6) | collective-permute-done | bytes 196640 | tf_op jit(solution)/shard_map/ppermute | solution.py:40
  26.9 2.1 %collective-permute-start.8 = (bf16[576,256]{1,0:T(8,128)(2,1)S(1)}, bf16[576,256]{1,0:T(8,128)(2,1)S(1)}, u32[]{:S(2)}, u32[]{:S(2)}) collective-permute-start(bf16[576,256]{1,0:T(8,128)(2,1)S(1)} %get-tuple-element.53), channel_id=1, source_target_pairs={{0,4},{1,3},{2,6},{3,1},{4,0},{5,7},{6,2},{7,5},{8,12},{9,11},{10,... | collective-permute-start | bytes 884744 | tf_op jit(solution)/shard_map/ppermute | solution.py:40
  29.1 1.6 %collective-permute-start.15 = (bf16[384,256]{1,0:T(8,128)(2,1)S(1)}, bf16[384,256]{1,0:T(8,128)(2,1)S(1)}, u32[]{:S(2)}, u32[]{:S(2)}) collective-permute-start(bf16[384,256]{1,0:T(8,128)(2,1)S(1)} %get-tuple-element.60), channel_id=1, source_target_pairs={{0,2},{1,5},{2,0},{3,7},{4,6},{5,1},{6,4},{7,3},{8,10},{9,13},{10,... | collective-permute-start | bytes 589832 | tf_op jit(solution)/shard_map/ppermute | solution.py:40
  30.8 0.6 collective-permute-start.1
  31.3 5.1 %collective-permute-done.15.refs_1_ = bf16[384,256]{1,0:T(8,128)(2,1)S(1)} collective-permute-done((bf16[384,256]{1,0:T(8,128)(2,1)S(1)}, bf16[384,256]{1,0:T(8,128)(2,1)S(1)}, u32[]{:S(2)}, u32[]{:S(2)}) %collective-permute-start.15) | collective-permute-done | bytes 196640 | tf_op jit(solution)/shard_map/ppermute | solution.py:40
  36.5 0.6 collective-permute-start.16
  37.1 2.0 %collective-permute-start.11 = (bf16[192,256]{1,0:T(8,128)(2,1)S(1)}, bf16[192,256]{1,0:T(8,128)(2,1)S(1)}, u32[]{:S(2)}, u32[]{:S(2)}) collective-permute-start(bf16[192,256]{1,0:T(8,128)(2,1)S(1)} %get-tuple-element.56), channel_id=1, source_target_pairs={{0,2},{1,5},{2,0},{3,7},{4,6},{5,1},{6,4},{7,3},{8,10},{9,13},{10,... | collective-permute-start | bytes 294920 | tf_op jit(solution)/shard_map/ppermute | solution.py:40
  39.4 2.0 %collective-permute-done.16.refs_1_ = bf16[192,256]{1,0:T(8,128)(2,1)S(1)} collective-permute-done((bf16[192,256]{1,0:T(8,128)(2,1)S(1)}, bf16[192,256]{1,0:T(8,128)(2,1)S(1)}, u32[]{:S(2)}, u32[]{:S(2)}) %collective-permute-start.16) | collective-permute-done | bytes 98336 | tf_op jit(solution)/shard_map/ppermute | solution.py:40
  41.4 2.7 %collective-permute-start.17 = (bf16[3,64,256]{2,1,0:T(8,128)(2,1)S(1)}, bf16[3,64,256]{2,1,0:T(8,128)(2,1)S(1)}, u32[]{:S(2)}, u32[]{:S(2)}) collective-permute-start(bf16[3,64,256]{2,1,0:T(8,128)(2,1)S(1)} %sum_parts.21.refs_0_), channel_id=1, source_target_pairs={{0,16},{8,24},{16,0},{24,8},{1,17},{9,25},{17,1},{25,9},{2,18},{10... | collective-permute-start | bytes 294920 | tf_op jit(solution)/shard_map/ppermute | solution.py:23
  44.5 2.7 %collective-permute-start.12 = (bf16[3,64,256]{2,1,0:T(8,128)(2,1)S(1)}, bf16[3,64,256]{2,1,0:T(8,128)(2,1)S(1)}, u32[]{:S(2)}, u32[]{:S(2)}) collective-permute-start(bf16[3,64,256]{2,1,0:T(8,128)(2,1)S(1)} %sum_parts.18.refs_0_), channel_id=1, source_target_pairs={{0,16},{8,24},{16,0},{24,8},{1,17},{9,25},{17,1},{25,9},{2,18},{10... | collective-permute-start | bytes 294920 | tf_op jit(solution)/shard_map/ppermute | solution.py:23
  47.9 7.2 %collective-permute-done.17.refs_1_ = bf16[3,64,256]{2,1,0:T(8,128)(2,1)S(1)} collective-permute-done((bf16[3,64,256]{2,1,0:T(8,128)(2,1)S(1)}, bf16[3,64,256]{2,1,0:T(8,128)(2,1)S(1)}, u32[]{:S(2)}, u32[]{:S(2)}) %collective-permute-start.17) | collective-permute-done | bytes 98336 | tf_op jit(solution)/shard_map/ppermute | solution.py:23
  55.4 1.8 %collective-permute-done.9.refs_1_ = bf16[3,64,256]{2,1,0:T(8,128)(2,1)S(1)} collective-permute-done((bf16[3,64,256]{2,1,0:T(8,128)(2,1)S(1)}, bf16[3,64,256]{2,1,0:T(8,128)(2,1)S(1)}, u32[]{:S(2)}, u32[]{:S(2)}) %collective-permute-start.9) | collective-permute-done | bytes 98336 | tf_op jit(solution)/shard_map/ppermute | solution.py:23
  58.4 1.3 %collective-permute-start.13 = (bf16[3,64,256]{2,1,0:T(8,128)(2,1)S(1)}, bf16[3,64,256]{2,1,0:T(8,128)(2,1)S(1)}, u32[]{:S(2)}, u32[]{:S(2)}) collective-permute-start(bf16[3,64,256]{2,1,0:T(8,128)(2,1)S(1)} %middle_level.6.own_ref), channel_id=1, source_target_pairs={{0,8},{8,0},{16,24},{24,16},{1,9},{9,1},{17,25},{25,17},{2,10},{10... | collective-permute-start | bytes 294920 | tf_op jit(solution)/shard_map/ppermute | solution.py:23
  60.0 0.8 %collective-permute-start.4 = (bf16[3,64,256]{2,1,0:T(8,128)(2,1)S(1)}, bf16[3,64,256]{2,1,0:T(8,128)(2,1)S(1)}, u32[]{:S(2)}, u32[]{:S(2)}) collective-permute-start(bf16[3,64,256]{2,1,0:T(8,128)(2,1)S(1)} %middle_level.4.own_ref), channel_id=1, source_target_pairs={{0,8},{8,0},{16,24},{24,16},{1,9},{9,1},{17,25},{25,17},{2,10},{10... | collective-permute-start | bytes 294920 | tf_op jit(solution)/shard_map/ppermute | solution.py:23
  60.8 0.6 collective-permute-done.18.partner_ref
  61.7 1.7 %collective-permute-done.10.partner_ref = bf16[3,64,256]{2,1,0:T(8,128)(2,1)S(1)} collective-permute-done((bf16[3,64,256]{2,1,0:T(8,128)(2,1)S(1)}, bf16[3,64,256]{2,1,0:T(8,128)(2,1)S(1)}, u32[]{:S(2)}, u32[]{:S(2)}) %collective-permute-start.10) | collective-permute-done | bytes 98336 | tf_op jit(solution)/shard_map/ppermute | solution.py:23
  63.8 1.7 %collective-permute-done.13.partner_ref = bf16[3,64,256]{2,1,0:T(8,128)(2,1)S(1)} collective-permute-done((bf16[3,64,256]{2,1,0:T(8,128)(2,1)S(1)}, bf16[3,64,256]{2,1,0:T(8,128)(2,1)S(1)}, u32[]{:S(2)}, u32[]{:S(2)}) %collective-permute-start.13) | collective-permute-done | bytes 98336 | tf_op jit(solution)/shard_map/ppermute | solution.py:23
  65.9 1.7 %collective-permute-done.4.partner_ref = bf16[3,64,256]{2,1,0:T(8,128)(2,1)S(1)} collective-permute-done((bf16[3,64,256]{2,1,0:T(8,128)(2,1)S(1)}, bf16[3,64,256]{2,1,0:T(8,128)(2,1)S(1)}, u32[]{:S(2)}, u32[]{:S(2)}) %collective-permute-start.4) | collective-permute-done | bytes 98336 | tf_op jit(solution)/shard_map/ppermute | solution.py:23
  67.6 1.2 %final_level.1 = f32[2,3,256,256]{3,2,1,0:T(8,128)} custom-call(bf16[3,64,256]{2,1,0:T(8,128)(2,1)S(1)} %middle_level.4.own_ref, bf16[3,64,256]{2,1,0:T(8,128)(2,1)S(1)} %collective-permute-done.4.partner_ref, bf16[512,512]{1,0:T(8,128)(2,1)S(1)} %get-tuple-element.45.weight_ref, f32[1,256]{1,0:T(1,128)S(1)} %bitcast.6, ...), custom_call_target="tpu_custom_call" | custom-call | tf_op jit(solution)/shard_map/final_level/pallas_call | solution.py:459
  (44 shorter events, 5.9 us)
Async XLA Ops:
  7.4 12.6 %collective-permute-start.5 = (bf16[4,3,64,256]{3,2,1,0:T(8,128)(2,1)S(1)}, bf16[4,3,64,256]{3,2,1,0:T(8,128)(2,1)S(1)}, u32[]{:S(2)}, u32[]{:S(2)}) collective-permute-start(bf16[4,3,64,256]{3,2,1,0:T(8,128)(2,1)S(1)} %get-tuple-element.47), channel_id=1, source_target_pairs={{0,1},{1,0},{2,3},{3,2},{4,5},{5,4},{6,7},{7,6},{8,9},{9,8},{10,11... | collective-permute-start | bytes 1179656 | tf_op jit(solution)/shard_map/ppermute | solution.py:23
  11.7 11.4 %collective-permute-start.7 = (bf16[4,3,64,256]{3,2,1,0:T(8,128)(2,1)S(1)}, bf16[4,3,64,256]{3,2,1,0:T(8,128)(2,1)S(1)}, u32[]{:S(2)}, u32[]{:S(2)}) collective-permute-start(bf16[4,3,64,256]{3,2,1,0:T(8,128)(2,1)S(1)} %get-tuple-element.51), channel_id=1, source_target_pairs={{0,1},{1,0},{2,3},{3,2},{4,5},{5,4},{6,7},{7,6},{8,9},{9,8},{10,11... | collective-permute-start | bytes 1179656 | tf_op jit(solution)/shard_map/ppermute | solution.py:23
  15.8 13.3 %collective-permute-start.14 = (bf16[4,3,64,256]{3,2,1,0:T(8,128)(2,1)S(1)}, bf16[4,3,64,256]{3,2,1,0:T(8,128)(2,1)S(1)}, u32[]{:S(2)}, u32[]{:S(2)}) collective-permute-start(bf16[4,3,64,256]{3,2,1,0:T(8,128)(2,1)S(1)} %get-tuple-element.58), channel_id=1, source_target_pairs={{0,1},{1,0},{2,3},{3,2},{4,5},{5,4},{6,7},{7,6},{8,9},{9,8},{10,11... | collective-permute-start | bytes 1179656 | tf_op jit(solution)/shard_map/ppermute | solution.py:23
  19.9 27.7 %copy-start = (bf16[2,1,2,256,128]{4,3,2,1,0:T(8,128)(2,1)S(1)}, bf16[2,1,2,256,128]{4,3,2,1,0:T(8,128)(2,1)}, u32[]{:S(2)}) copy-start(bf16[2,1,2,256,128]{4,3,2,1,0:T(8,128)(2,1)} %proj_ref.3) | copy-start | bytes 786436
  19.9 27.7 %copy-start.1 = (bf16[2,1,2,256,256]{4,3,2,1,0:T(8,128)(2,1)S(1)}, bf16[2,1,2,256,256]{4,3,2,1,0:T(8,128)(2,1)}, u32[]{:S(2)}) copy-start(bf16[2,1,2,256,256]{4,3,2,1,0:T(8,128)(2,1)} %inv_ref.1) | copy-start | bytes 1572868
  19.9 10.8 %collective-permute-start = (bf16[4,3,64,256]{3,2,1,0:T(8,128)(2,1)S(1)}, bf16[4,3,64,256]{3,2,1,0:T(8,128)(2,1)S(1)}, u32[]{:S(2)}, u32[]{:S(2)}) collective-permute-start(bf16[4,3,64,256]{3,2,1,0:T(8,128)(2,1)S(1)} %get-tuple-element.39), channel_id=1, source_target_pairs={{0,1},{1,0},{2,3},{3,2},{4,5},{5,4},{6,7},{7,6},{8,9},{9,8},{10,11... | collective-permute-start | bytes 1179656 | tf_op jit(solution)/shard_map/ppermute | solution.py:23
  20.1 6.7 %collective-permute-start.6 = (bf16[384,256]{1,0:T(8,128)(2,1)S(1)}, bf16[384,256]{1,0:T(8,128)(2,1)S(1)}, u32[]{:S(2)}, u32[]{:S(2)}) collective-permute-start(bf16[384,256]{1,0:T(8,128)(2,1)S(1)} %get-tuple-element.49), channel_id=1, source_target_pairs={{0,2},{1,5},{2,0},{3,7},{4,6},{5,1},{6,4},{7,3},{8,10},{9,13},{10,... | collective-permute-start | bytes 589832 | tf_op jit(solution)/shard_map/ppermute | solution.py:40
  26.9 34.5 %copy-start.2 = (f32[256]{0:T(256)S(1)}, f32[256]{0:T(256)}, u32[]{:S(2)}) copy-start(f32[256]{0:T(256)} %param.9) | copy-start | bytes 3076
  26.9 10.2 %collective-permute-start.8 = (bf16[576,256]{1,0:T(8,128)(2,1)S(1)}, bf16[576,256]{1,0:T(8,128)(2,1)S(1)}, u32[]{:S(2)}, u32[]{:S(2)}) collective-permute-start(bf16[576,256]{1,0:T(8,128)(2,1)S(1)} %get-tuple-element.53), channel_id=1, source_target_pairs={{0,4},{1,3},{2,6},{3,1},{4,0},{5,7},{6,2},{7,5},{8,12},{9,11},{10,... | collective-permute-start | bytes 884744 | tf_op jit(solution)/shard_map/ppermute | solution.py:40
  29.1 7.3 %collective-permute-start.15 = (bf16[384,256]{1,0:T(8,128)(2,1)S(1)}, bf16[384,256]{1,0:T(8,128)(2,1)S(1)}, u32[]{:S(2)}, u32[]{:S(2)}) collective-permute-start(bf16[384,256]{1,0:T(8,128)(2,1)S(1)} %get-tuple-element.60), channel_id=1, source_target_pairs={{0,2},{1,5},{2,0},{3,7},{4,6},{5,1},{6,4},{7,3},{8,10},{9,13},{10,... | collective-permute-start | bytes 589832 | tf_op jit(solution)/shard_map/ppermute | solution.py:40
  30.8 8.4 %collective-permute-start.1 = (bf16[384,256]{1,0:T(8,128)(2,1)S(1)}, bf16[384,256]{1,0:T(8,128)(2,1)S(1)}, u32[]{:S(2)}, u32[]{:S(2)}) collective-permute-start(bf16[384,256]{1,0:T(8,128)(2,1)S(1)} %get-tuple-element.41), channel_id=1, source_target_pairs={{0,4},{1,3},{2,6},{3,1},{4,0},{5,7},{6,2},{7,5},{8,12},{9,11},{10,... | collective-permute-start | bytes 589832 | tf_op jit(solution)/shard_map/ppermute | solution.py:40
  36.5 4.9 %collective-permute-start.16 = (bf16[192,256]{1,0:T(8,128)(2,1)S(1)}, bf16[192,256]{1,0:T(8,128)(2,1)S(1)}, u32[]{:S(2)}, u32[]{:S(2)}) collective-permute-start(bf16[192,256]{1,0:T(8,128)(2,1)S(1)} %get-tuple-element.62), channel_id=1, source_target_pairs={{0,4},{1,3},{2,6},{3,1},{4,0},{5,7},{6,2},{7,5},{8,12},{9,11},{10,... | collective-permute-start | bytes 294920 | tf_op jit(solution)/shard_map/ppermute | solution.py:40
  37.1 7.3 %collective-permute-start.11 = (bf16[192,256]{1,0:T(8,128)(2,1)S(1)}, bf16[192,256]{1,0:T(8,128)(2,1)S(1)}, u32[]{:S(2)}, u32[]{:S(2)}) collective-permute-start(bf16[192,256]{1,0:T(8,128)(2,1)S(1)} %get-tuple-element.56), channel_id=1, source_target_pairs={{0,2},{1,5},{2,0},{3,7},{4,6},{5,1},{6,4},{7,3},{8,10},{9,13},{10,... | collective-permute-start | bytes 294920 | tf_op jit(solution)/shard_map/ppermute | solution.py:40
  39.2 8.0 %collective-permute-start.2 = (bf16[192,256]{1,0:T(8,128)(2,1)S(1)}, bf16[192,256]{1,0:T(8,128)(2,1)S(1)}, u32[]{:S(2)}, u32[]{:S(2)}) collective-permute-start(bf16[192,256]{1,0:T(8,128)(2,1)S(1)} %get-tuple-element.43), channel_id=1, source_target_pairs={{0,2},{1,5},{2,0},{3,7},{4,6},{5,1},{6,4},{7,3},{8,10},{9,13},{10,... | collective-permute-start | bytes 294920 | tf_op jit(solution)/shard_map/ppermute | solution.py:40
  41.4 13.7 %collective-permute-start.17 = (bf16[3,64,256]{2,1,0:T(8,128)(2,1)S(1)}, bf16[3,64,256]{2,1,0:T(8,128)(2,1)S(1)}, u32[]{:S(2)}, u32[]{:S(2)}) collective-permute-start(bf16[3,64,256]{2,1,0:T(8,128)(2,1)S(1)} %sum_parts.21.refs_0_), channel_id=1, source_target_pairs={{0,16},{8,24},{16,0},{24,8},{1,17},{9,25},{17,1},{25,9},{2,18},{10... | collective-permute-start | bytes 294920 | tf_op jit(solution)/shard_map/ppermute | solution.py:23
  44.1 13.1 %collective-permute-start.9 = (bf16[3,64,256]{2,1,0:T(8,128)(2,1)S(1)}, bf16[3,64,256]{2,1,0:T(8,128)(2,1)S(1)}, u32[]{:S(2)}, u32[]{:S(2)}) collective-permute-start(bf16[3,64,256]{2,1,0:T(8,128)(2,1)S(1)} %sum_parts.16.refs_0_), channel_id=1, source_target_pairs={{0,16},{8,24},{16,0},{24,8},{1,17},{9,25},{17,1},{25,9},{2,18},{10... | collective-permute-start | bytes 294920 | tf_op jit(solution)/shard_map/ppermute | solution.py:23
  44.5 13.7 %collective-permute-start.12 = (bf16[3,64,256]{2,1,0:T(8,128)(2,1)S(1)}, bf16[3,64,256]{2,1,0:T(8,128)(2,1)S(1)}, u32[]{:S(2)}, u32[]{:S(2)}) collective-permute-start(bf16[3,64,256]{2,1,0:T(8,128)(2,1)S(1)} %sum_parts.18.refs_0_), channel_id=1, source_target_pairs={{0,16},{8,24},{16,0},{24,8},{1,17},{9,25},{17,1},{25,9},{2,18},{10... | collective-permute-start | bytes 294920 | tf_op jit(solution)/shard_map/ppermute | solution.py:23
  47.2 12.5 %collective-permute-start.3 = (bf16[3,64,256]{2,1,0:T(8,128)(2,1)S(1)}, bf16[3,64,256]{2,1,0:T(8,128)(2,1)S(1)}, u32[]{:S(2)}, u32[]{:S(2)}) collective-permute-start(bf16[3,64,256]{2,1,0:T(8,128)(2,1)S(1)} %sum_parts.13.refs_0_), channel_id=1, source_target_pairs={{0,16},{8,24},{16,0},{24,8},{1,17},{9,25},{17,1},{25,9},{2,18},{10... | collective-permute-start | bytes 294920 | tf_op jit(solution)/shard_map/ppermute | solution.py:23
  55.3 6.0 %collective-permute-start.18 = (bf16[3,64,256]{2,1,0:T(8,128)(2,1)S(1)}, bf16[3,64,256]{2,1,0:T(8,128)(2,1)S(1)}, u32[]{:S(2)}, u32[]{:S(2)}) collective-permute-start(bf16[3,64,256]{2,1,0:T(8,128)(2,1)S(1)} %middle_level.7.own_ref), channel_id=1, source_target_pairs={{0,8},{8,0},{16,24},{24,16},{1,9},{9,1},{17,25},{25,17},{2,10},{10... | collective-permute-start | bytes 294920 | tf_op jit(solution)/shard_map/ppermute | solution.py:23
  57.4 6.1 %collective-permute-start.10 = (bf16[3,64,256]{2,1,0:T(8,128)(2,1)S(1)}, bf16[3,64,256]{2,1,0:T(8,128)(2,1)S(1)}, u32[]{:S(2)}, u32[]{:S(2)}) collective-permute-start(bf16[3,64,256]{2,1,0:T(8,128)(2,1)S(1)} %middle_level.5.own_ref), channel_id=1, source_target_pairs={{0,8},{8,0},{16,24},{24,16},{1,9},{9,1},{17,25},{25,17},{2,10},{10... | collective-permute-start | bytes 294920 | tf_op jit(solution)/shard_map/ppermute | solution.py:23
  58.4 7.2 %collective-permute-start.13 = (bf16[3,64,256]{2,1,0:T(8,128)(2,1)S(1)}, bf16[3,64,256]{2,1,0:T(8,128)(2,1)S(1)}, u32[]{:S(2)}, u32[]{:S(2)}) collective-permute-start(bf16[3,64,256]{2,1,0:T(8,128)(2,1)S(1)} %middle_level.6.own_ref), channel_id=1, source_target_pairs={{0,8},{8,0},{16,24},{24,16},{1,9},{9,1},{17,25},{25,17},{2,10},{10... | collective-permute-start | bytes 294920 | tf_op jit(solution)/shard_map/ppermute | solution.py:23
  60.0 7.6 %collective-permute-start.4 = (bf16[3,64,256]{2,1,0:T(8,128)(2,1)S(1)}, bf16[3,64,256]{2,1,0:T(8,128)(2,1)S(1)}, u32[]{:S(2)}, u32[]{:S(2)}) collective-permute-start(bf16[3,64,256]{2,1,0:T(8,128)(2,1)S(1)} %middle_level.4.own_ref), channel_id=1, source_target_pairs={{0,8},{8,0},{16,24},{24,16},{1,9},{9,1},{17,25},{25,17},{2,10},{10... | collective-permute-start | bytes 294920 | tf_op jit(solution)/shard_map/ppermute | solution.py:23

commit v4 on v3

--- a/solution.py
+++ b/solution.py
@@ -11,7 +11,8 @@
 splits = (1, 1, 1, 1)
 groups = ((0,), (1,), (2,), (3,))
 exchanges = (((0, 0),), ((0, 1), (1, 0)), ((1, 1),), ((2, 0),), ((2, 1),), ((3, 0),), ((3, 1),))
-project_steps = 4
+project_steps = 2
+row_tile = 16
 mib = 1024 * 1024
 in_vmem = pl.BlockSpec(memory_space=pltpu.VMEM)
 in_hbm = pl.BlockSpec(memory_space=pltpu.HBM)
@@ -68,22 +69,29 @@
     return place ^ jnp.where(place % 2 == 0, turns[0], turns[1])
 
 
-def write_pieces(place, acc_ref, keep_ref, send_ref, chunk, first, chunk_rows):
-    halves, passes, _, width = keep_ref.shape
+def write_pieces(place, acc_ref, keep_ref, send_ref, chunk, first, chunk_rows, one):
+    halves = keep_ref.shape[0]
+    rank = keep_ref.shape[3] // 2
+    segments = 2 * halves
     kept = slice(first, first + chunk_rows)
-    rank = width // 2
-    segments = 2 * halves
     for turn in range(segments):
         out_ref = send_ref if turn % 2 else keep_ref
         target = piece_target(place ^ (turn % 2), turn // 2, segments, chunk)
         rows = pl.ds(pl.multiple_of(target * chunk_rows, chunk_rows), chunk_rows)
         upper = acc_ref[0, rows, :]
         lower = acc_ref[1, rows, :]
-        for one in range(passes):
-            re = slice(2 * one * rank, (2 * one + 1) * rank)
-            im = slice((2 * one + 1) * rank, (2 * one + 2) * rank)
-            out_ref[turn // 2, one, kept, :rank] = (upper[:, re] - lower[:, im]).astype(jnp.bfloat16)
-            out_ref[turn // 2, one, kept, rank:] = (upper[:, im] + lower[:, re]).astype(jnp.bfloat16)
+        out_ref[turn // 2, one, kept, :rank] = (upper[:, :rank] - lower[:, rank:]).astype(jnp.bfloat16)
+        out_ref[turn // 2, one, kept, rank:] = (upper[:, rank:] + lower[:, :rank]).astype(jnp.bfloat16)
+
+
+def gather_passes(place, block_ref, sk_ref, acc_refs, keep_ref, send_ref, chunk, first):
+    rows, cols = block_ref.shape[2:]
+    width = keep_ref.shape[3]
+    for one, acc_ref in enumerate(acc_refs):
+        part = sk_ref[:, one * width : (one + 1) * width]
+        both = product(block_ref[...].reshape(-1, cols), part)
+        acc_ref[...] = both.reshape(acc_ref.shape)
+        write_pieces(place, acc_ref, keep_ref, send_ref, chunk, first, rows, one)
 
 
 def block_copies(kernel_ref, block_ref, sems, span, part):
@@ -97,8 +105,22 @@
     ]
 
 
-def both_copies(kernel_ref, block_ref, sems, span):
-    return [copy for part in range(2) for copy in block_copies(kernel_ref, block_ref, sems, span, part)]
+def wait_all(kernel_ref, block_ref, sems, span):
+    def part_wait(part, carry):
+        for copy in block_copies(kernel_ref, block_ref, sems, span, part):
+            copy.wait()
+        return carry
+
+    lax.fori_loop(0, 2, part_wait, 0)
+
+
+def start_all(kernel_ref, block_ref, sems, span):
+    def part_start(part, carry):
+        for copy in block_copies(kernel_ref, block_ref, sems, span, part):
+            copy.start()
+        return carry
+
+    lax.fori_loop(0, 2, part_start, 0)
 
 
 def first_body(place_ref, kernel_ref, sketch_ref, proj_ref, *rest, spans):
@@ -107,7 +129,7 @@
         *rest, next_sems = rest
     else:
         keep_ref, send_ref, sk_ref, *rest = rest
-    held_ref, parts_ref, block_ref, acc_ref, sketch_sems, proj_sem, block_sems = rest
+    held_ref, parts_ref, block_ref, *acc_refs, sketch_sems, proj_sem, block_sems = rest
     passes, cols, _ = sketch_ref.shape
     rank = proj_ref.shape[4]
     deep = cols // project_steps
@@ -122,9 +144,6 @@
     proj_copy.start()
     for step in range(project_steps):
         sketch_copy(step).start()
-    next_copies = []
-    if len(spans) > 1:
-        next_copies = both_copies(kernel_ref, next_ref, next_sems, spans[1])
     proj_copy.wait()
 
     def project(step, carry):
@@ -136,25 +155,35 @@
             sk_ref[rows, cols] = product(held_ref[one, rows, :], both).astype(jnp.bfloat16)
         return carry
 
-    def gather(part, carry):
-        for copy in block_copies(kernel_ref, block_ref, block_sems, spans[0], part):
-            copy.wait()
-
-        @pl.when(part == 0)
-        def _():
-            for copy in next_copies:
-                copy.start()
-
-        acc_ref[part] = product(block_ref[part].reshape(-1, cols), sk_ref[...])
-        return carry
-
     for part in range(2):
         lax.fori_loop(part, part + 1, project, 0)
         for copy in block_copies(kernel_ref, block_ref, block_sems, spans[0], part):
             copy.start()
     lax.fori_loop(2, project_steps, project, 0)
+    width = 2 * rank
+
+    next_copies = []
+    if len(spans) > 1:
+        for part in range(2):
+            next_copies.extend(block_copies(kernel_ref, next_ref, next_sems, spans[1], part))
+
+    def gather(part, carry):
+        for copy in block_copies(kernel_ref, block_ref, block_sems, spans[0], part):
+            copy.wait()
+
+        @pl.when(part == 0)
+        def _():
+            for copy in next_copies:
+                copy.start()
+
+        both = product(block_ref[part].reshape(-1, cols), sk_ref[...])
+        for one, acc_ref in enumerate(acc_refs):
+            acc_ref[part] = both[:, one * width : (one + 1) * width]
+        return carry
+
     lax.fori_loop(0, 2, gather, 0)
-    write_pieces(place_ref[0], acc_ref, keep_ref, send_ref, 0, 0, spans[0][1])
+    for one, acc_ref in enumerate(acc_refs):
+        write_pieces(place_ref[0], acc_ref, keep_ref, send_ref, 0, 0, spans[0][1], one)
     if len(spans) > 1:
         wait_all(kernel_ref, next_ref, next_sems, spans[1])
 
@@ -179,7 +208,7 @@
         pltpu.VMEM(sketch.shape, sketch.dtype),
         pltpu.VMEM((2, sketch_cols, rank), projections.dtype),
         pltpu.VMEM((2, segments, spans[0][1], cols), kernel.dtype),
-        pltpu.VMEM((2, segments * spans[0][1], width), jnp.float32),
+        *[pltpu.VMEM((2, segments * spans[0][1], 2 * rank), jnp.float32)] * passes,
         pltpu.SemaphoreType.DMA((project_steps,)),
         pltpu.SemaphoreType.DMA(()),
         pltpu.SemaphoreType.DMA((2, segments)),
@@ -199,24 +228,6 @@
     )(place, remote(kernel), remote(sketch), remote(projections))
 
 
-def wait_all(kernel_ref, block_ref, sems, span):
-    def part_wait(part, carry):
-        for copy in block_copies(kernel_ref, block_ref, sems, span, part):
-            copy.wait()
-        return carry
-
-    lax.fori_loop(0, 2, part_wait, 0)
-
-
-def start_all(kernel_ref, block_ref, sems, span):
-    def part_start(part, carry):
-        for copy in block_copies(kernel_ref, block_ref, sems, span, part):
-            copy.start()
-        return carry
-
-    lax.fori_loop(0, 2, part_start, 0)
-
-
 def gather_body(place_ref, block_ref, sk_ref, *rest, chunk, first, next_span, filled):
     rest = list(rest)
     if next_span is not None:
@@ -224,15 +235,11 @@
     if filled:
         del rest[:2]
     keep_ref, send_ref, *rest = rest
+    acc_refs = rest
     if next_span is not None:
-        next_ref, acc_ref, sems = rest
+        next_ref, *acc_refs, sems = rest
         start_all(kernel_ref, next_ref, sems, next_span)
-    else:
-        (acc_ref,) = rest
-    rows, cols = block_ref.shape[2:]
-    both = product(block_ref[...].reshape(-1, cols), sk_ref[...])
-    acc_ref[...] = both.reshape(acc_ref.shape)
-    write_pieces(place_ref[0], acc_ref, keep_ref, send_ref, chunk, first, rows)
+    gather_passes(place_ref[0], block_ref, sk_ref, acc_refs, keep_ref, send_ref, chunk, first)
     if next_span is not None:
         wait_all(kernel_ref, next_ref, sems, next_span)
 
@@ -244,7 +251,7 @@
     operands = [place, local(block), local(sk_value)]
     in_specs = [in_smem, in_vmem, in_vmem]
     out_shape = [piece, piece]
-    scratch = [pltpu.VMEM((2, segments * rows, width), jnp.float32)]
+    scratch = [pltpu.VMEM((2, segments * rows, width // passes), jnp.float32)] * passes
     aliases = {}
     if next_span is not None:
         operands.append(remote(kernel))
@@ -478,11 +485,9 @@
     top_bits = lax.axis_size("bf").bit_length() - 1
     _, rows, cols = kernel.shape
     segment_rows = rows // members
-    unit = segment_rows // sum(shares)
-    spans = []
-    for share in shares:
-        first = spans[-1][0] + spans[-1][1] if spans else 0
-        spans.append((first, share * unit))
+    tiles = segment_rows // row_tile
+    bounds = [tiles * sum(shares[:end]) // sum(shares) * row_tile for end in range(len(shares) + 1)]
+    spans = [(first, last - first) for first, last in zip(bounds, bounds[1:])]
     chunks = len(spans)
     kernel = kernel.reshape(2, members, segment_rows, cols)
     place = lax.axis_index("sk").reshape(1).astype(jnp.int32)

time: 69.1 us -> 68.7 us (level)
  no operation moved by 1% of the time
where the time goes in v4:
time: 68.7 us; the launch traced here: 68.6 us
  waiting for transfers between devices  26 us (38%)
  Pallas kernels  22.2 us (32%)
  starting transfers between devices  20 us (29%)
    ppermute x12, waiting for transfers between devices, swapped(): return lax.ppermute(value, axis, pairs)  15.2 us
    pallas_call x3, Pallas kernels, gathered(): pl.pallas_call(functools.partial(gather_body, chunk=chunk, first=first, n...  11.1 us
    ppermute x7, waiting for transfers between devices, swapped_step(): return lax.ppermute(value, 'sk', pairs)  10.8 us
    ppermute x7, starting transfers between devices, swapped_step(): return lax.ppermute(value, 'sk', pairs)  10 us
    ppermute x12, starting transfers between devices, swapped(): return lax.ppermute(value, axis, pairs)  9.97 us
    pallas_call x1, Pallas kernels, first_gathered(): pl.pallas_call(functools.partial(first_body, spans=spans), name='gather_f...  7.15 us
  transfers between devices with their start and end apart: 19, of which 10 were waited for; matrix products, arithmetic and copies ran while one was open for 0% of the time, Pallas kernels for 20%

profile of v4, /device:TPU:0, one launch (start us, length us, event | category | flops | bytes accessed | tf_op | source)
XLA Modules:
  0.0 68.6 jit_solution(12826434462489486304)
XLA Ops:
  0.0 7.2 %gather_first.1 = (bf16[4,3,64,256]{3,2,1,0:T(8,128)(2,1)S(1)}, bf16[4,3,64,256]{3,2,1,0:T(8,128)(2,1)S(1)}, bf16[2048,768]{1,0:T(8,128)(2,1)S(1)}, bf16[2,8,64,2048]{3,2,1,0:T(8,128)(2,1)S(1)}) custom-call(s32[1]{0:T(128)} %bitcast.place_ref, bf16[2,8,256,2048]{3,2,1,0:T(8,128)(2,1)} %bitcast.7, bf16[3,2048,256]{2,1,0:T(8,128)(2,1)} %sketch_ref.1, ...), custom_call_target="tpu_custom_call" | custom-call | flops 3221225472 | bytes 4194304 | tf_op jit(solution)/shard_map/gather_first/pallas_call | solution.py:219
  7.7 3.7 %gather.3 = (bf16[4,3,64,256]{3,2,1,0:T(8,128)(2,1)S(1)}, bf16[4,3,64,256]{3,2,1,0:T(8,128)(2,1)S(1)}, bf16[2,8,64,2048]{3,2,1,0:T(8,128)(2,1)S(1)}) custom-call(s32[1]{0:T(128)} %bitcast.place_ref, bf16[2,8,64,2048]{3,2,1,0:T(8,128)(2,1)S(1)} %get-tuple-element.34.block_ref, bf16[2048,768]{1,0:T(8,128)(2,1)S(1)} %get-tuple-element.35.sk_ref, ...), custom_call_target="tpu_custom_call" | custom-call | flops 3221225472 | bytes 4194304 | tf_op jit(solution)/shard_map/gather/pallas_call | solution.py:265
  11.5 3.9 %gather.4 = (bf16[4,3,64,256]{3,2,1,0:T(8,128)(2,1)S(1)}, bf16[4,3,64,256]{3,2,1,0:T(8,128)(2,1)S(1)}, bf16[2,8,64,2048]{3,2,1,0:T(8,128)(2,1)S(1)}) custom-call(s32[1]{0:T(128)} %bitcast.place_ref, bf16[2,8,64,2048]{3,2,1,0:T(8,128)(2,1)S(1)} %get-tuple-element.36.block_ref, bf16[2048,768]{1,0:T(8,128)(2,1)S(1)} %get-tuple-element.35.sk_ref, ...), custom_call_target="tpu_custom_call" | custom-call | flops 3221225472 | bytes 4194304 | tf_op jit(solution)/shard_map/gather/pallas_call | solution.py:265
  16.0 3.5 %gather.5 = (bf16[4,3,64,256]{3,2,1,0:T(8,128)(2,1)S(1)}, bf16[4,3,64,256]{3,2,1,0:T(8,128)(2,1)S(1)}) custom-call(s32[1]{0:T(128)} %bitcast.place_ref, bf16[2,8,64,2048]{3,2,1,0:T(8,128)(2,1)S(1)} %get-tuple-element.37.block_ref, bf16[2048,768]{1,0:T(8,128)(2,1)S(1)} %get-tuple-element.35.sk_ref), custom_call_target="tpu_custom_call" | custom-call | flops 3221225472 | bytes 4194304 | tf_op jit(solution)/shard_map/gather/pallas_call | solution.py:265
  19.7 3.0 %collective-permute-start.6 = (bf16[384,256]{1,0:T(8,128)(2,1)S(1)}, bf16[384,256]{1,0:T(8,128)(2,1)S(1)}, u32[]{:S(2)}, u32[]{:S(2)}) collective-permute-start(bf16[384,256]{1,0:T(8,128)(2,1)S(1)} %get-tuple-element.49), channel_id=1, source_target_pairs={{0,2},{1,5},{2,0},{3,7},{4,6},{5,1},{6,4},{7,3},{8,10},{9,13},{10,... | collective-permute-start | bytes 589832 | tf_op jit(solution)/shard_map/ppermute | solution.py:41
  22.7 3.6 %collective-permute-done.6.refs_1_ = bf16[384,256]{1,0:T(8,128)(2,1)S(1)} collective-permute-done((bf16[384,256]{1,0:T(8,128)(2,1)S(1)}, bf16[384,256]{1,0:T(8,128)(2,1)S(1)}, u32[]{:S(2)}, u32[]{:S(2)}) %collective-permute-start.6) | collective-permute-done | bytes 196640 | tf_op jit(solution)/shard_map/ppermute | solution.py:41
  26.5 2.1 %collective-permute-start.8 = (bf16[576,256]{1,0:T(8,128)(2,1)S(1)}, bf16[576,256]{1,0:T(8,128)(2,1)S(1)}, u32[]{:S(2)}, u32[]{:S(2)}) collective-permute-start(bf16[576,256]{1,0:T(8,128)(2,1)S(1)} %get-tuple-element.53), channel_id=1, source_target_pairs={{0,4},{1,3},{2,6},{3,1},{4,0},{5,7},{6,2},{7,5},{8,12},{9,11},{10,... | collective-permute-start | bytes 884744 | tf_op jit(solution)/shard_map/ppermute | solution.py:41
  28.7 1.6 %collective-permute-start.15 = (bf16[384,256]{1,0:T(8,128)(2,1)S(1)}, bf16[384,256]{1,0:T(8,128)(2,1)S(1)}, u32[]{:S(2)}, u32[]{:S(2)}) collective-permute-start(bf16[384,256]{1,0:T(8,128)(2,1)S(1)} %get-tuple-element.60), channel_id=1, source_target_pairs={{0,2},{1,5},{2,0},{3,7},{4,6},{5,1},{6,4},{7,3},{8,10},{9,13},{10,... | collective-permute-start | bytes 589832 | tf_op jit(solution)/shard_map/ppermute | solution.py:41
  30.4 0.6 collective-permute-start.1
  31.0 5.1 %collective-permute-done.15.refs_1_ = bf16[384,256]{1,0:T(8,128)(2,1)S(1)} collective-permute-done((bf16[384,256]{1,0:T(8,128)(2,1)S(1)}, bf16[384,256]{1,0:T(8,128)(2,1)S(1)}, u32[]{:S(2)}, u32[]{:S(2)}) %collective-permute-start.15) | collective-permute-done | bytes 196640 | tf_op jit(solution)/shard_map/ppermute | solution.py:41
  36.1 0.6 collective-permute-start.16
  36.8 2.0 %collective-permute-start.11 = (bf16[192,256]{1,0:T(8,128)(2,1)S(1)}, bf16[192,256]{1,0:T(8,128)(2,1)S(1)}, u32[]{:S(2)}, u32[]{:S(2)}) collective-permute-start(bf16[192,256]{1,0:T(8,128)(2,1)S(1)} %get-tuple-element.56), channel_id=1, source_target_pairs={{0,2},{1,5},{2,0},{3,7},{4,6},{5,1},{6,4},{7,3},{8,10},{9,13},{10,... | collective-permute-start | bytes 294920 | tf_op jit(solution)/shard_map/ppermute | solution.py:41
  39.0 2.0 %collective-permute-done.16.refs_1_ = bf16[192,256]{1,0:T(8,128)(2,1)S(1)} collective-permute-done((bf16[192,256]{1,0:T(8,128)(2,1)S(1)}, bf16[192,256]{1,0:T(8,128)(2,1)S(1)}, u32[]{:S(2)}, u32[]{:S(2)}) %collective-permute-start.16) | collective-permute-done | bytes 98336 | tf_op jit(solution)/shard_map/ppermute | solution.py:41
  41.0 2.7 %collective-permute-start.17 = (bf16[3,64,256]{2,1,0:T(8,128)(2,1)S(1)}, bf16[3,64,256]{2,1,0:T(8,128)(2,1)S(1)}, u32[]{:S(2)}, u32[]{:S(2)}) collective-permute-start(bf16[3,64,256]{2,1,0:T(8,128)(2,1)S(1)} %sum_parts.21.refs_0_), channel_id=1, source_target_pairs={{0,16},{8,24},{16,0},{24,8},{1,17},{9,25},{17,1},{25,9},{2,18},{10... | collective-permute-start | bytes 294920 | tf_op jit(solution)/shard_map/ppermute | solution.py:24
  44.1 2.7 %collective-permute-start.12 = (bf16[3,64,256]{2,1,0:T(8,128)(2,1)S(1)}, bf16[3,64,256]{2,1,0:T(8,128)(2,1)S(1)}, u32[]{:S(2)}, u32[]{:S(2)}) collective-permute-start(bf16[3,64,256]{2,1,0:T(8,128)(2,1)S(1)} %sum_parts.18.refs_0_), channel_id=1, source_target_pairs={{0,16},{8,24},{16,0},{24,8},{1,17},{9,25},{17,1},{25,9},{2,18},{10... | collective-permute-start | bytes 294920 | tf_op jit(solution)/shard_map/ppermute | solution.py:24
  47.5 7.2 %collective-permute-done.17.refs_1_ = bf16[3,64,256]{2,1,0:T(8,128)(2,1)S(1)} collective-permute-done((bf16[3,64,256]{2,1,0:T(8,128)(2,1)S(1)}, bf16[3,64,256]{2,1,0:T(8,128)(2,1)S(1)}, u32[]{:S(2)}, u32[]{:S(2)}) %collective-permute-start.17) | collective-permute-done | bytes 98336 | tf_op jit(solution)/shard_map/ppermute | solution.py:24
  55.0 1.8 %collective-permute-done.9.refs_1_ = bf16[3,64,256]{2,1,0:T(8,128)(2,1)S(1)} collective-permute-done((bf16[3,64,256]{2,1,0:T(8,128)(2,1)S(1)}, bf16[3,64,256]{2,1,0:T(8,128)(2,1)S(1)}, u32[]{:S(2)}, u32[]{:S(2)}) %collective-permute-start.9) | collective-permute-done | bytes 98336 | tf_op jit(solution)/shard_map/ppermute | solution.py:24
  58.1 1.3 %collective-permute-start.13 = (bf16[3,64,256]{2,1,0:T(8,128)(2,1)S(1)}, bf16[3,64,256]{2,1,0:T(8,128)(2,1)S(1)}, u32[]{:S(2)}, u32[]{:S(2)}) collective-permute-start(bf16[3,64,256]{2,1,0:T(8,128)(2,1)S(1)} %middle_level.6.own_ref), channel_id=1, source_target_pairs={{0,8},{8,0},{16,24},{24,16},{1,9},{9,1},{17,25},{25,17},{2,10},{10... | collective-permute-start | bytes 294920 | tf_op jit(solution)/shard_map/ppermute | solution.py:24
  59.6 0.8 %collective-permute-start.4 = (bf16[3,64,256]{2,1,0:T(8,128)(2,1)S(1)}, bf16[3,64,256]{2,1,0:T(8,128)(2,1)S(1)}, u32[]{:S(2)}, u32[]{:S(2)}) collective-permute-start(bf16[3,64,256]{2,1,0:T(8,128)(2,1)S(1)} %middle_level.4.own_ref), channel_id=1, source_target_pairs={{0,8},{8,0},{16,24},{24,16},{1,9},{9,1},{17,25},{25,17},{2,10},{10... | collective-permute-start | bytes 294920 | tf_op jit(solution)/shard_map/ppermute | solution.py:24
  60.4 0.6 collective-permute-done.18.partner_ref
  61.4 1.7 %collective-permute-done.10.partner_ref = bf16[3,64,256]{2,1,0:T(8,128)(2,1)S(1)} collective-permute-done((bf16[3,64,256]{2,1,0:T(8,128)(2,1)S(1)}, bf16[3,64,256]{2,1,0:T(8,128)(2,1)S(1)}, u32[]{:S(2)}, u32[]{:S(2)}) %collective-permute-start.10) | collective-permute-done | bytes 98336 | tf_op jit(solution)/shard_map/ppermute | solution.py:24
  63.5 1.7 %collective-permute-done.13.partner_ref = bf16[3,64,256]{2,1,0:T(8,128)(2,1)S(1)} collective-permute-done((bf16[3,64,256]{2,1,0:T(8,128)(2,1)S(1)}, bf16[3,64,256]{2,1,0:T(8,128)(2,1)S(1)}, u32[]{:S(2)}, u32[]{:S(2)}) %collective-permute-start.13) | collective-permute-done | bytes 98336 | tf_op jit(solution)/shard_map/ppermute | solution.py:24
  65.6 1.7 %collective-permute-done.4.partner_ref = bf16[3,64,256]{2,1,0:T(8,128)(2,1)S(1)} collective-permute-done((bf16[3,64,256]{2,1,0:T(8,128)(2,1)S(1)}, bf16[3,64,256]{2,1,0:T(8,128)(2,1)S(1)}, u32[]{:S(2)}, u32[]{:S(2)}) %collective-permute-start.4) | collective-permute-done | bytes 98336 | tf_op jit(solution)/shard_map/ppermute | solution.py:24
  67.2 1.2 %final_level.1 = f32[2,3,256,256]{3,2,1,0:T(8,128)} custom-call(bf16[3,64,256]{2,1,0:T(8,128)(2,1)S(1)} %middle_level.4.own_ref, bf16[3,64,256]{2,1,0:T(8,128)(2,1)S(1)} %collective-permute-done.4.partner_ref, bf16[512,512]{1,0:T(8,128)(2,1)S(1)} %get-tuple-element.45.weight_ref, f32[1,256]{1,0:T(1,128)S(1)} %bitcast.6, ...), custom_call_target="tpu_custom_call" | custom-call | tf_op jit(solution)/shard_map/final_level/pallas_call | solution.py:466
  (44 shorter events, 5.9 us)
Async XLA Ops:
  7.2 12.5 %collective-permute-start.5 = (bf16[4,3,64,256]{3,2,1,0:T(8,128)(2,1)S(1)}, bf16[4,3,64,256]{3,2,1,0:T(8,128)(2,1)S(1)}, u32[]{:S(2)}, u32[]{:S(2)}) collective-permute-start(bf16[4,3,64,256]{3,2,1,0:T(8,128)(2,1)S(1)} %get-tuple-element.47), channel_id=1, source_target_pairs={{0,1},{1,0},{2,3},{3,2},{4,5},{5,4},{6,7},{7,6},{8,9},{9,8},{10,11... | collective-permute-start | bytes 1179656 | tf_op jit(solution)/shard_map/ppermute | solution.py:24
  11.4 11.3 %collective-permute-start.7 = (bf16[4,3,64,256]{3,2,1,0:T(8,128)(2,1)S(1)}, bf16[4,3,64,256]{3,2,1,0:T(8,128)(2,1)S(1)}, u32[]{:S(2)}, u32[]{:S(2)}) collective-permute-start(bf16[4,3,64,256]{3,2,1,0:T(8,128)(2,1)S(1)} %get-tuple-element.51), channel_id=1, source_target_pairs={{0,1},{1,0},{2,3},{3,2},{4,5},{5,4},{6,7},{7,6},{8,9},{9,8},{10,11... | collective-permute-start | bytes 1179656 | tf_op jit(solution)/shard_map/ppermute | solution.py:24
  15.4 13.2 %collective-permute-start.14 = (bf16[4,3,64,256]{3,2,1,0:T(8,128)(2,1)S(1)}, bf16[4,3,64,256]{3,2,1,0:T(8,128)(2,1)S(1)}, u32[]{:S(2)}, u32[]{:S(2)}) collective-permute-start(bf16[4,3,64,256]{3,2,1,0:T(8,128)(2,1)S(1)} %get-tuple-element.58), channel_id=1, source_target_pairs={{0,1},{1,0},{2,3},{3,2},{4,5},{5,4},{6,7},{7,6},{8,9},{9,8},{10,11... | collective-permute-start | bytes 1179656 | tf_op jit(solution)/shard_map/ppermute | solution.py:24
  19.5 27.7 %copy-start = (bf16[2,1,2,256,128]{4,3,2,1,0:T(8,128)(2,1)S(1)}, bf16[2,1,2,256,128]{4,3,2,1,0:T(8,128)(2,1)}, u32[]{:S(2)}) copy-start(bf16[2,1,2,256,128]{4,3,2,1,0:T(8,128)(2,1)} %proj_ref.3) | copy-start | bytes 786436
  19.5 27.7 %copy-start.1 = (bf16[2,1,2,256,256]{4,3,2,1,0:T(8,128)(2,1)S(1)}, bf16[2,1,2,256,256]{4,3,2,1,0:T(8,128)(2,1)}, u32[]{:S(2)}) copy-start(bf16[2,1,2,256,256]{4,3,2,1,0:T(8,128)(2,1)} %inv_ref.1) | copy-start | bytes 1572868
  19.5 10.8 %collective-permute-start = (bf16[4,3,64,256]{3,2,1,0:T(8,128)(2,1)S(1)}, bf16[4,3,64,256]{3,2,1,0:T(8,128)(2,1)S(1)}, u32[]{:S(2)}, u32[]{:S(2)}) collective-permute-start(bf16[4,3,64,256]{3,2,1,0:T(8,128)(2,1)S(1)} %get-tuple-element.39), channel_id=1, source_target_pairs={{0,1},{1,0},{2,3},{3,2},{4,5},{5,4},{6,7},{7,6},{8,9},{9,8},{10,11... | collective-permute-start | bytes 1179656 | tf_op jit(solution)/shard_map/ppermute | solution.py:24
  19.7 6.7 %collective-permute-start.6 = (bf16[384,256]{1,0:T(8,128)(2,1)S(1)}, bf16[384,256]{1,0:T(8,128)(2,1)S(1)}, u32[]{:S(2)}, u32[]{:S(2)}) collective-permute-start(bf16[384,256]{1,0:T(8,128)(2,1)S(1)} %get-tuple-element.49), channel_id=1, source_target_pairs={{0,2},{1,5},{2,0},{3,7},{4,6},{5,1},{6,4},{7,3},{8,10},{9,13},{10,... | collective-permute-start | bytes 589832 | tf_op jit(solution)/shard_map/ppermute | solution.py:41
  26.5 34.5 %copy-start.2 = (f32[256]{0:T(256)S(1)}, f32[256]{0:T(256)}, u32[]{:S(2)}) copy-start(f32[256]{0:T(256)} %param.9) | copy-start | bytes 3076
  26.5 10.2 %collective-permute-start.8 = (bf16[576,256]{1,0:T(8,128)(2,1)S(1)}, bf16[576,256]{1,0:T(8,128)(2,1)S(1)}, u32[]{:S(2)}, u32[]{:S(2)}) collective-permute-start(bf16[576,256]{1,0:T(8,128)(2,1)S(1)} %get-tuple-element.53), channel_id=1, source_target_pairs={{0,4},{1,3},{2,6},{3,1},{4,0},{5,7},{6,2},{7,5},{8,12},{9,11},{10,... | collective-permute-start | bytes 884744 | tf_op jit(solution)/shard_map/ppermute | solution.py:41
  28.7 7.3 %collective-permute-start.15 = (bf16[384,256]{1,0:T(8,128)(2,1)S(1)}, bf16[384,256]{1,0:T(8,128)(2,1)S(1)}, u32[]{:S(2)}, u32[]{:S(2)}) collective-permute-start(bf16[384,256]{1,0:T(8,128)(2,1)S(1)} %get-tuple-element.60), channel_id=1, source_target_pairs={{0,2},{1,5},{2,0},{3,7},{4,6},{5,1},{6,4},{7,3},{8,10},{9,13},{10,... | collective-permute-start | bytes 589832 | tf_op jit(solution)/shard_map/ppermute | solution.py:41
  30.4 8.4 %collective-permute-start.1 = (bf16[384,256]{1,0:T(8,128)(2,1)S(1)}, bf16[384,256]{1,0:T(8,128)(2,1)S(1)}, u32[]{:S(2)}, u32[]{:S(2)}) collective-permute-start(bf16[384,256]{1,0:T(8,128)(2,1)S(1)} %get-tuple-element.41), channel_id=1, source_target_pairs={{0,4},{1,3},{2,6},{3,1},{4,0},{5,7},{6,2},{7,5},{8,12},{9,11},{10,... | collective-permute-start | bytes 589832 | tf_op jit(solution)/shard_map/ppermute | solution.py:41
  36.1 4.9 %collective-permute-start.16 = (bf16[192,256]{1,0:T(8,128)(2,1)S(1)}, bf16[192,256]{1,0:T(8,128)(2,1)S(1)}, u32[]{:S(2)}, u32[]{:S(2)}) collective-permute-start(bf16[192,256]{1,0:T(8,128)(2,1)S(1)} %get-tuple-element.62), channel_id=1, source_target_pairs={{0,4},{1,3},{2,6},{3,1},{4,0},{5,7},{6,2},{7,5},{8,12},{9,11},{10,... | collective-permute-start | bytes 294920 | tf_op jit(solution)/shard_map/ppermute | solution.py:41
  36.8 7.3 %collective-permute-start.11 = (bf16[192,256]{1,0:T(8,128)(2,1)S(1)}, bf16[192,256]{1,0:T(8,128)(2,1)S(1)}, u32[]{:S(2)}, u32[]{:S(2)}) collective-permute-start(bf16[192,256]{1,0:T(8,128)(2,1)S(1)} %get-tuple-element.56), channel_id=1, source_target_pairs={{0,2},{1,5},{2,0},{3,7},{4,6},{5,1},{6,4},{7,3},{8,10},{9,13},{10,... | collective-permute-start | bytes 294920 | tf_op jit(solution)/shard_map/ppermute | solution.py:41
  38.8 8.0 %collective-permute-start.2 = (bf16[192,256]{1,0:T(8,128)(2,1)S(1)}, bf16[192,256]{1,0:T(8,128)(2,1)S(1)}, u32[]{:S(2)}, u32[]{:S(2)}) collective-permute-start(bf16[192,256]{1,0:T(8,128)(2,1)S(1)} %get-tuple-element.43), channel_id=1, source_target_pairs={{0,2},{1,5},{2,0},{3,7},{4,6},{5,1},{6,4},{7,3},{8,10},{9,13},{10,... | collective-permute-start | bytes 294920 | tf_op jit(solution)/shard_map/ppermute | solution.py:41
  41.0 13.7 %collective-permute-start.17 = (bf16[3,64,256]{2,1,0:T(8,128)(2,1)S(1)}, bf16[3,64,256]{2,1,0:T(8,128)(2,1)S(1)}, u32[]{:S(2)}, u32[]{:S(2)}) collective-permute-start(bf16[3,64,256]{2,1,0:T(8,128)(2,1)S(1)} %sum_parts.21.refs_0_), channel_id=1, source_target_pairs={{0,16},{8,24},{16,0},{24,8},{1,17},{9,25},{17,1},{25,9},{2,18},{10... | collective-permute-start | bytes 294920 | tf_op jit(solution)/shard_map/ppermute | solution.py:24
  43.7 13.1 %collective-permute-start.9 = (bf16[3,64,256]{2,1,0:T(8,128)(2,1)S(1)}, bf16[3,64,256]{2,1,0:T(8,128)(2,1)S(1)}, u32[]{:S(2)}, u32[]{:S(2)}) collective-permute-start(bf16[3,64,256]{2,1,0:T(8,128)(2,1)S(1)} %sum_parts.16.refs_0_), channel_id=1, source_target_pairs={{0,16},{8,24},{16,0},{24,8},{1,17},{9,25},{17,1},{25,9},{2,18},{10... | collective-permute-start | bytes 294920 | tf_op jit(solution)/shard_map/ppermute | solution.py:24
  44.1 13.7 %collective-permute-start.12 = (bf16[3,64,256]{2,1,0:T(8,128)(2,1)S(1)}, bf16[3,64,256]{2,1,0:T(8,128)(2,1)S(1)}, u32[]{:S(2)}, u32[]{:S(2)}) collective-permute-start(bf16[3,64,256]{2,1,0:T(8,128)(2,1)S(1)} %sum_parts.18.refs_0_), channel_id=1, source_target_pairs={{0,16},{8,24},{16,0},{24,8},{1,17},{9,25},{17,1},{25,9},{2,18},{10... | collective-permute-start | bytes 294920 | tf_op jit(solution)/shard_map/ppermute | solution.py:24
  46.8 12.6 %collective-permute-start.3 = (bf16[3,64,256]{2,1,0:T(8,128)(2,1)S(1)}, bf16[3,64,256]{2,1,0:T(8,128)(2,1)S(1)}, u32[]{:S(2)}, u32[]{:S(2)}) collective-permute-start(bf16[3,64,256]{2,1,0:T(8,128)(2,1)S(1)} %sum_parts.13.refs_0_), channel_id=1, source_target_pairs={{0,16},{8,24},{16,0},{24,8},{1,17},{9,25},{17,1},{25,9},{2,18},{10... | collective-permute-start | bytes 294920 | tf_op jit(solution)/shard_map/ppermute | solution.py:24
  54.9 6.1 %collective-permute-start.18 = (bf16[3,64,256]{2,1,0:T(8,128)(2,1)S(1)}, bf16[3,64,256]{2,1,0:T(8,128)(2,1)S(1)}, u32[]{:S(2)}, u32[]{:S(2)}) collective-permute-start(bf16[3,64,256]{2,1,0:T(8,128)(2,1)S(1)} %middle_level.7.own_ref), channel_id=1, source_target_pairs={{0,8},{8,0},{16,24},{24,16},{1,9},{9,1},{17,25},{25,17},{2,10},{10... | collective-permute-start | bytes 294920 | tf_op jit(solution)/shard_map/ppermute | solution.py:24
  57.0 6.1 %collective-permute-start.10 = (bf16[3,64,256]{2,1,0:T(8,128)(2,1)S(1)}, bf16[3,64,256]{2,1,0:T(8,128)(2,1)S(1)}, u32[]{:S(2)}, u32[]{:S(2)}) collective-permute-start(bf16[3,64,256]{2,1,0:T(8,128)(2,1)S(1)} %middle_level.5.own_ref), channel_id=1, source_target_pairs={{0,8},{8,0},{16,24},{24,16},{1,9},{9,1},{17,25},{25,17},{2,10},{10... | collective-permute-start | bytes 294920 | tf_op jit(solution)/shard_map/ppermute | solution.py:24
  58.1 7.2 %collective-permute-start.13 = (bf16[3,64,256]{2,1,0:T(8,128)(2,1)S(1)}, bf16[3,64,256]{2,1,0:T(8,128)(2,1)S(1)}, u32[]{:S(2)}, u32[]{:S(2)}) collective-permute-start(bf16[3,64,256]{2,1,0:T(8,128)(2,1)S(1)} %middle_level.6.own_ref), channel_id=1, source_target_pairs={{0,8},{8,0},{16,24},{24,16},{1,9},{9,1},{17,25},{25,17},{2,10},{10... | collective-permute-start | bytes 294920 | tf_op jit(solution)/shard_map/ppermute | solution.py:24
  59.6 7.6 %collective-permute-start.4 = (bf16[3,64,256]{2,1,0:T(8,128)(2,1)S(1)}, bf16[3,64,256]{2,1,0:T(8,128)(2,1)S(1)}, u32[]{:S(2)}, u32[]{:S(2)}) collective-permute-start(bf16[3,64,256]{2,1,0:T(8,128)(2,1)S(1)} %middle_level.4.own_ref), channel_id=1, source_target_pairs={{0,8},{8,0},{16,24},{24,16},{1,9},{9,1},{17,25},{25,17},{2,10},{10... | collective-permute-start | bytes 294920 | tf_op jit(solution)/shard_map/ppermute | solution.py:24

commit v5 on v4

--- a/solution.py
+++ b/solution.py
@@ -446,15 +446,20 @@
 
 def final_body(own_ref, partner_ref, weight_ref, gain_ref, *rest, firsts):
     stages = rest[: len(firsts) - 1]
-    out_ref, stage_ref, sems = rest[len(firsts) - 1 :]
+    out_ref, stage_ref, sems, pass_sems = rest[len(firsts) - 1 :]
     copies = []
-    for place, (first, part_ref) in enumerate(zip(firsts, (*stages, stage_ref))):
+    for place, (first, part_ref) in enumerate(zip(firsts, stages)):
         target = out_ref.at[:, :, pl.ds(first, part_ref.shape[2]), :]
         copies.append(pltpu.make_async_copy(part_ref, target, sems.at[place]))
-    for copy in copies[:-1]:
+    for copy in copies:
         copy.start()
-    stage_ref[0], stage_ref[1] = normalized(own_ref, partner_ref, weight_ref, gain_ref)
-    copies[-1].start()
+    re, im = normalized(own_ref, partner_ref, weight_ref, gain_ref)
+    for one in range(stage_ref.shape[1]):
+        stage_ref[0, one] = re[one]
+        stage_ref[1, one] = im[one]
+        target = out_ref.at[:, one, pl.ds(firsts[-1], stage_ref.shape[2]), :]
+        copies.append(pltpu.make_async_copy(stage_ref.at[:, one], target, pass_sems.at[one]))
+        copies[-1].start()
     for copy in copies:
         copy.wait()
 
@@ -471,7 +476,8 @@
         out_shape=jax.ShapeDtypeStruct((2, passes, segment_rows, sketch_cols), jnp.float32),
         scratch_shapes=[
             pltpu.VMEM((2, passes, rows, sketch_cols), jnp.float32),
-            pltpu.SemaphoreType.DMA((len(firsts),)),
+            pltpu.SemaphoreType.DMA((max(len(firsts) - 1, 1),)),
+            pltpu.SemaphoreType.DMA((passes,)),
         ],
         compiler_params=params(8),
     )(*operands)

time: 68.7 us -> 68.7 us (level)
  no operation moved by 1% of the time
where the time goes in v5:
time: 68.7 us; the launch traced here: 68.6 us
  waiting for transfers between devices  26 us (38%)
  Pallas kernels  22.2 us (32%)
  starting transfers between devices  20 us (29%)
    ppermute x12, waiting for transfers between devices, swapped(): return lax.ppermute(value, axis, pairs)  15.2 us
    pallas_call x3, Pallas kernels, gathered(): pl.pallas_call(functools.partial(gather_body, chunk=chunk, first=first, n...  11.1 us
    ppermute x7, waiting for transfers between devices, swapped_step(): return lax.ppermute(value, 'sk', pairs)  10.8 us
    ppermute x7, starting transfers between devices, swapped_step(): return lax.ppermute(value, 'sk', pairs)  10 us
    ppermute x12, starting transfers between devices, swapped(): return lax.ppermute(value, axis, pairs)  9.97 us
    pallas_call x1, Pallas kernels, first_gathered(): pl.pallas_call(functools.partial(first_body, spans=spans), name='gather_f...  7.15 us
  transfers between devices with their start and end apart: 19, of which 10 were waited for; matrix products, arithmetic and copies ran while one was open for 0% of the time, Pallas kernels for 20%

profile of v5, /device:TPU:0, one launch (start us, length us, event | category | flops | bytes accessed | tf_op | source)
XLA Modules:
  0.0 68.6 jit_solution(549013863170201226)
XLA Ops:
  0.0 7.2 %gather_first.1 = (bf16[4,3,64,256]{3,2,1,0:T(8,128)(2,1)S(1)}, bf16[4,3,64,256]{3,2,1,0:T(8,128)(2,1)S(1)}, bf16[2048,768]{1,0:T(8,128)(2,1)S(1)}, bf16[2,8,64,2048]{3,2,1,0:T(8,128)(2,1)S(1)}) custom-call(s32[1]{0:T(128)} %bitcast.place_ref, bf16[2,8,256,2048]{3,2,1,0:T(8,128)(2,1)} %bitcast.7, bf16[3,2048,256]{2,1,0:T(8,128)(2,1)} %sketch_ref.1, ...), custom_call_target="tpu_custom_call" | custom-call | flops 3221225472 | bytes 4194304 | tf_op jit(solution)/shard_map/gather_first/pallas_call | solution.py:219
  7.7 3.7 %gather.3 = (bf16[4,3,64,256]{3,2,1,0:T(8,128)(2,1)S(1)}, bf16[4,3,64,256]{3,2,1,0:T(8,128)(2,1)S(1)}, bf16[2,8,64,2048]{3,2,1,0:T(8,128)(2,1)S(1)}) custom-call(s32[1]{0:T(128)} %bitcast.place_ref, bf16[2,8,64,2048]{3,2,1,0:T(8,128)(2,1)S(1)} %get-tuple-element.34.block_ref, bf16[2048,768]{1,0:T(8,128)(2,1)S(1)} %get-tuple-element.35.sk_ref, ...), custom_call_target="tpu_custom_call" | custom-call | flops 3221225472 | bytes 4194304 | tf_op jit(solution)/shard_map/gather/pallas_call | solution.py:265
  11.5 3.9 %gather.4 = (bf16[4,3,64,256]{3,2,1,0:T(8,128)(2,1)S(1)}, bf16[4,3,64,256]{3,2,1,0:T(8,128)(2,1)S(1)}, bf16[2,8,64,2048]{3,2,1,0:T(8,128)(2,1)S(1)}) custom-call(s32[1]{0:T(128)} %bitcast.place_ref, bf16[2,8,64,2048]{3,2,1,0:T(8,128)(2,1)S(1)} %get-tuple-element.36.block_ref, bf16[2048,768]{1,0:T(8,128)(2,1)S(1)} %get-tuple-element.35.sk_ref, ...), custom_call_target="tpu_custom_call" | custom-call | flops 3221225472 | bytes 4194304 | tf_op jit(solution)/shard_map/gather/pallas_call | solution.py:265
  16.0 3.5 %gather.5 = (bf16[4,3,64,256]{3,2,1,0:T(8,128)(2,1)S(1)}, bf16[4,3,64,256]{3,2,1,0:T(8,128)(2,1)S(1)}) custom-call(s32[1]{0:T(128)} %bitcast.place_ref, bf16[2,8,64,2048]{3,2,1,0:T(8,128)(2,1)S(1)} %get-tuple-element.37.block_ref, bf16[2048,768]{1,0:T(8,128)(2,1)S(1)} %get-tuple-element.35.sk_ref), custom_call_target="tpu_custom_call" | custom-call | flops 3221225472 | bytes 4194304 | tf_op jit(solution)/shard_map/gather/pallas_call | solution.py:265
  19.7 3.0 %collective-permute-start.6 = (bf16[384,256]{1,0:T(8,128)(2,1)S(1)}, bf16[384,256]{1,0:T(8,128)(2,1)S(1)}, u32[]{:S(2)}, u32[]{:S(2)}) collective-permute-start(bf16[384,256]{1,0:T(8,128)(2,1)S(1)} %get-tuple-element.49), channel_id=1, source_target_pairs={{0,2},{1,5},{2,0},{3,7},{4,6},{5,1},{6,4},{7,3},{8,10},{9,13},{10,... | collective-permute-start | bytes 589832 | tf_op jit(solution)/shard_map/ppermute | solution.py:41
  22.7 3.6 %collective-permute-done.6.refs_1_ = bf16[384,256]{1,0:T(8,128)(2,1)S(1)} collective-permute-done((bf16[384,256]{1,0:T(8,128)(2,1)S(1)}, bf16[384,256]{1,0:T(8,128)(2,1)S(1)}, u32[]{:S(2)}, u32[]{:S(2)}) %collective-permute-start.6) | collective-permute-done | bytes 196640 | tf_op jit(solution)/shard_map/ppermute | solution.py:41
  26.5 2.1 %collective-permute-start.8 = (bf16[576,256]{1,0:T(8,128)(2,1)S(1)}, bf16[576,256]{1,0:T(8,128)(2,1)S(1)}, u32[]{:S(2)}, u32[]{:S(2)}) collective-permute-start(bf16[576,256]{1,0:T(8,128)(2,1)S(1)} %get-tuple-element.53), channel_id=1, source_target_pairs={{0,4},{1,3},{2,6},{3,1},{4,0},{5,7},{6,2},{7,5},{8,12},{9,11},{10,... | collective-permute-start | bytes 884744 | tf_op jit(solution)/shard_map/ppermute | solution.py:41
  28.7 1.6 %collective-permute-start.15 = (bf16[384,256]{1,0:T(8,128)(2,1)S(1)}, bf16[384,256]{1,0:T(8,128)(2,1)S(1)}, u32[]{:S(2)}, u32[]{:S(2)}) collective-permute-start(bf16[384,256]{1,0:T(8,128)(2,1)S(1)} %get-tuple-element.60), channel_id=1, source_target_pairs={{0,2},{1,5},{2,0},{3,7},{4,6},{5,1},{6,4},{7,3},{8,10},{9,13},{10,... | collective-permute-start | bytes 589832 | tf_op jit(solution)/shard_map/ppermute | solution.py:41
  30.4 0.6 collective-permute-start.1
  31.0 5.1 %collective-permute-done.15.refs_1_ = bf16[384,256]{1,0:T(8,128)(2,1)S(1)} collective-permute-done((bf16[384,256]{1,0:T(8,128)(2,1)S(1)}, bf16[384,256]{1,0:T(8,128)(2,1)S(1)}, u32[]{:S(2)}, u32[]{:S(2)}) %collective-permute-start.15) | collective-permute-done | bytes 196640 | tf_op jit(solution)/shard_map/ppermute | solution.py:41
  36.1 0.6 collective-permute-start.16
  36.8 2.0 %collective-permute-start.11 = (bf16[192,256]{1,0:T(8,128)(2,1)S(1)}, bf16[192,256]{1,0:T(8,128)(2,1)S(1)}, u32[]{:S(2)}, u32[]{:S(2)}) collective-permute-start(bf16[192,256]{1,0:T(8,128)(2,1)S(1)} %get-tuple-element.56), channel_id=1, source_target_pairs={{0,2},{1,5},{2,0},{3,7},{4,6},{5,1},{6,4},{7,3},{8,10},{9,13},{10,... | collective-permute-start | bytes 294920 | tf_op jit(solution)/shard_map/ppermute | solution.py:41
  39.0 2.0 %collective-permute-done.16.refs_1_ = bf16[192,256]{1,0:T(8,128)(2,1)S(1)} collective-permute-done((bf16[192,256]{1,0:T(8,128)(2,1)S(1)}, bf16[192,256]{1,0:T(8,128)(2,1)S(1)}, u32[]{:S(2)}, u32[]{:S(2)}) %collective-permute-start.16) | collective-permute-done | bytes 98336 | tf_op jit(solution)/shard_map/ppermute | solution.py:41
  41.0 2.7 %collective-permute-start.17 = (bf16[3,64,256]{2,1,0:T(8,128)(2,1)S(1)}, bf16[3,64,256]{2,1,0:T(8,128)(2,1)S(1)}, u32[]{:S(2)}, u32[]{:S(2)}) collective-permute-start(bf16[3,64,256]{2,1,0:T(8,128)(2,1)S(1)} %sum_parts.21.refs_0_), channel_id=1, source_target_pairs={{0,16},{8,24},{16,0},{24,8},{1,17},{9,25},{17,1},{25,9},{2,18},{10... | collective-permute-start | bytes 294920 | tf_op jit(solution)/shard_map/ppermute | solution.py:24
  44.1 2.7 %collective-permute-start.12 = (bf16[3,64,256]{2,1,0:T(8,128)(2,1)S(1)}, bf16[3,64,256]{2,1,0:T(8,128)(2,1)S(1)}, u32[]{:S(2)}, u32[]{:S(2)}) collective-permute-start(bf16[3,64,256]{2,1,0:T(8,128)(2,1)S(1)} %sum_parts.18.refs_0_), channel_id=1, source_target_pairs={{0,16},{8,24},{16,0},{24,8},{1,17},{9,25},{17,1},{25,9},{2,18},{10... | collective-permute-start | bytes 294920 | tf_op jit(solution)/shard_map/ppermute | solution.py:24
  47.5 7.2 %collective-permute-done.17.refs_1_ = bf16[3,64,256]{2,1,0:T(8,128)(2,1)S(1)} collective-permute-done((bf16[3,64,256]{2,1,0:T(8,128)(2,1)S(1)}, bf16[3,64,256]{2,1,0:T(8,128)(2,1)S(1)}, u32[]{:S(2)}, u32[]{:S(2)}) %collective-permute-start.17) | collective-permute-done | bytes 98336 | tf_op jit(solution)/shard_map/ppermute | solution.py:24
  55.0 1.8 %collective-permute-done.9.refs_1_ = bf16[3,64,256]{2,1,0:T(8,128)(2,1)S(1)} collective-permute-done((bf16[3,64,256]{2,1,0:T(8,128)(2,1)S(1)}, bf16[3,64,256]{2,1,0:T(8,128)(2,1)S(1)}, u32[]{:S(2)}, u32[]{:S(2)}) %collective-permute-start.9) | collective-permute-done | bytes 98336 | tf_op jit(solution)/shard_map/ppermute | solution.py:24
  58.1 1.3 %collective-permute-start.13 = (bf16[3,64,256]{2,1,0:T(8,128)(2,1)S(1)}, bf16[3,64,256]{2,1,0:T(8,128)(2,1)S(1)}, u32[]{:S(2)}, u32[]{:S(2)}) collective-permute-start(bf16[3,64,256]{2,1,0:T(8,128)(2,1)S(1)} %middle_level.6.own_ref), channel_id=1, source_target_pairs={{0,8},{8,0},{16,24},{24,16},{1,9},{9,1},{17,25},{25,17},{2,10},{10... | collective-permute-start | bytes 294920 | tf_op jit(solution)/shard_map/ppermute | solution.py:24
  59.6 0.8 %collective-permute-start.4 = (bf16[3,64,256]{2,1,0:T(8,128)(2,1)S(1)}, bf16[3,64,256]{2,1,0:T(8,128)(2,1)S(1)}, u32[]{:S(2)}, u32[]{:S(2)}) collective-permute-start(bf16[3,64,256]{2,1,0:T(8,128)(2,1)S(1)} %middle_level.4.own_ref), channel_id=1, source_target_pairs={{0,8},{8,0},{16,24},{24,16},{1,9},{9,1},{17,25},{25,17},{2,10},{10... | collective-permute-start | bytes 294920 | tf_op jit(solution)/shard_map/ppermute | solution.py:24
  60.4 0.6 collective-permute-done.18.partner_ref
  61.4 1.7 %collective-permute-done.10.partner_ref = bf16[3,64,256]{2,1,0:T(8,128)(2,1)S(1)} collective-permute-done((bf16[3,64,256]{2,1,0:T(8,128)(2,1)S(1)}, bf16[3,64,256]{2,1,0:T(8,128)(2,1)S(1)}, u32[]{:S(2)}, u32[]{:S(2)}) %collective-permute-start.10) | collective-permute-done | bytes 98336 | tf_op jit(solution)/shard_map/ppermute | solution.py:24
  63.5 1.7 %collective-permute-done.13.partner_ref = bf16[3,64,256]{2,1,0:T(8,128)(2,1)S(1)} collective-permute-done((bf16[3,64,256]{2,1,0:T(8,128)(2,1)S(1)}, bf16[3,64,256]{2,1,0:T(8,128)(2,1)S(1)}, u32[]{:S(2)}, u32[]{:S(2)}) %collective-permute-start.13) | collective-permute-done | bytes 98336 | tf_op jit(solution)/shard_map/ppermute | solution.py:24
  65.6 1.7 %collective-permute-done.4.partner_ref = bf16[3,64,256]{2,1,0:T(8,128)(2,1)S(1)} collective-permute-done((bf16[3,64,256]{2,1,0:T(8,128)(2,1)S(1)}, bf16[3,64,256]{2,1,0:T(8,128)(2,1)S(1)}, u32[]{:S(2)}, u32[]{:S(2)}) %collective-permute-start.4) | collective-permute-done | bytes 98336 | tf_op jit(solution)/shard_map/ppermute | solution.py:24
  67.2 1.2 %final_level.1 = f32[2,3,256,256]{3,2,1,0:T(8,128)} custom-call(bf16[3,64,256]{2,1,0:T(8,128)(2,1)S(1)} %middle_level.4.own_ref, bf16[3,64,256]{2,1,0:T(8,128)(2,1)S(1)} %collective-permute-done.4.partner_ref, bf16[512,512]{1,0:T(8,128)(2,1)S(1)} %get-tuple-element.45.weight_ref, f32[1,256]{1,0:T(1,128)S(1)} %bitcast.6, ...), custom_call_target="tpu_custom_call" | custom-call | tf_op jit(solution)/shard_map/final_level/pallas_call | solution.py:471
  (44 shorter events, 5.9 us)
Async XLA Ops:
  7.2 12.5 %collective-permute-start.5 = (bf16[4,3,64,256]{3,2,1,0:T(8,128)(2,1)S(1)}, bf16[4,3,64,256]{3,2,1,0:T(8,128)(2,1)S(1)}, u32[]{:S(2)}, u32[]{:S(2)}) collective-permute-start(bf16[4,3,64,256]{3,2,1,0:T(8,128)(2,1)S(1)} %get-tuple-element.47), channel_id=1, source_target_pairs={{0,1},{1,0},{2,3},{3,2},{4,5},{5,4},{6,7},{7,6},{8,9},{9,8},{10,11... | collective-permute-start | bytes 1179656 | tf_op jit(solution)/shard_map/ppermute | solution.py:24
  11.4 11.3 %collective-permute-start.7 = (bf16[4,3,64,256]{3,2,1,0:T(8,128)(2,1)S(1)}, bf16[4,3,64,256]{3,2,1,0:T(8,128)(2,1)S(1)}, u32[]{:S(2)}, u32[]{:S(2)}) collective-permute-start(bf16[4,3,64,256]{3,2,1,0:T(8,128)(2,1)S(1)} %get-tuple-element.51), channel_id=1, source_target_pairs={{0,1},{1,0},{2,3},{3,2},{4,5},{5,4},{6,7},{7,6},{8,9},{9,8},{10,11... | collective-permute-start | bytes 1179656 | tf_op jit(solution)/shard_map/ppermute | solution.py:24
  15.4 13.2 %collective-permute-start.14 = (bf16[4,3,64,256]{3,2,1,0:T(8,128)(2,1)S(1)}, bf16[4,3,64,256]{3,2,1,0:T(8,128)(2,1)S(1)}, u32[]{:S(2)}, u32[]{:S(2)}) collective-permute-start(bf16[4,3,64,256]{3,2,1,0:T(8,128)(2,1)S(1)} %get-tuple-element.58), channel_id=1, source_target_pairs={{0,1},{1,0},{2,3},{3,2},{4,5},{5,4},{6,7},{7,6},{8,9},{9,8},{10,11... | collective-permute-start | bytes 1179656 | tf_op jit(solution)/shard_map/ppermute | solution.py:24
  19.5 27.7 %copy-start = (bf16[2,1,2,256,128]{4,3,2,1,0:T(8,128)(2,1)S(1)}, bf16[2,1,2,256,128]{4,3,2,1,0:T(8,128)(2,1)}, u32[]{:S(2)}) copy-start(bf16[2,1,2,256,128]{4,3,2,1,0:T(8,128)(2,1)} %proj_ref.3) | copy-start | bytes 786436
  19.5 27.7 %copy-start.1 = (bf16[2,1,2,256,256]{4,3,2,1,0:T(8,128)(2,1)S(1)}, bf16[2,1,2,256,256]{4,3,2,1,0:T(8,128)(2,1)}, u32[]{:S(2)}) copy-start(bf16[2,1,2,256,256]{4,3,2,1,0:T(8,128)(2,1)} %inv_ref.1) | copy-start | bytes 1572868
  19.5 10.8 %collective-permute-start = (bf16[4,3,64,256]{3,2,1,0:T(8,128)(2,1)S(1)}, bf16[4,3,64,256]{3,2,1,0:T(8,128)(2,1)S(1)}, u32[]{:S(2)}, u32[]{:S(2)}) collective-permute-start(bf16[4,3,64,256]{3,2,1,0:T(8,128)(2,1)S(1)} %get-tuple-element.39), channel_id=1, source_target_pairs={{0,1},{1,0},{2,3},{3,2},{4,5},{5,4},{6,7},{7,6},{8,9},{9,8},{10,11... | collective-permute-start | bytes 1179656 | tf_op jit(solution)/shard_map/ppermute | solution.py:24
  19.7 6.7 %collective-permute-start.6 = (bf16[384,256]{1,0:T(8,128)(2,1)S(1)}, bf16[384,256]{1,0:T(8,128)(2,1)S(1)}, u32[]{:S(2)}, u32[]{:S(2)}) collective-permute-start(bf16[384,256]{1,0:T(8,128)(2,1)S(1)} %get-tuple-element.49), channel_id=1, source_target_pairs={{0,2},{1,5},{2,0},{3,7},{4,6},{5,1},{6,4},{7,3},{8,10},{9,13},{10,... | collective-permute-start | bytes 589832 | tf_op jit(solution)/shard_map/ppermute | solution.py:41
  26.5 34.5 %copy-start.2 = (f32[256]{0:T(256)S(1)}, f32[256]{0:T(256)}, u32[]{:S(2)}) copy-start(f32[256]{0:T(256)} %param.9) | copy-start | bytes 3076
  26.5 10.2 %collective-permute-start.8 = (bf16[576,256]{1,0:T(8,128)(2,1)S(1)}, bf16[576,256]{1,0:T(8,128)(2,1)S(1)}, u32[]{:S(2)}, u32[]{:S(2)}) collective-permute-start(bf16[576,256]{1,0:T(8,128)(2,1)S(1)} %get-tuple-element.53), channel_id=1, source_target_pairs={{0,4},{1,3},{2,6},{3,1},{4,0},{5,7},{6,2},{7,5},{8,12},{9,11},{10,... | collective-permute-start | bytes 884744 | tf_op jit(solution)/shard_map/ppermute | solution.py:41
  28.7 7.3 %collective-permute-start.15 = (bf16[384,256]{1,0:T(8,128)(2,1)S(1)}, bf16[384,256]{1,0:T(8,128)(2,1)S(1)}, u32[]{:S(2)}, u32[]{:S(2)}) collective-permute-start(bf16[384,256]{1,0:T(8,128)(2,1)S(1)} %get-tuple-element.60), channel_id=1, source_target_pairs={{0,2},{1,5},{2,0},{3,7},{4,6},{5,1},{6,4},{7,3},{8,10},{9,13},{10,... | collective-permute-start | bytes 589832 | tf_op jit(solution)/shard_map/ppermute | solution.py:41
  30.4 8.4 %collective-permute-start.1 = (bf16[384,256]{1,0:T(8,128)(2,1)S(1)}, bf16[384,256]{1,0:T(8,128)(2,1)S(1)}, u32[]{:S(2)}, u32[]{:S(2)}) collective-permute-start(bf16[384,256]{1,0:T(8,128)(2,1)S(1)} %get-tuple-element.41), channel_id=1, source_target_pairs={{0,4},{1,3},{2,6},{3,1},{4,0},{5,7},{6,2},{7,5},{8,12},{9,11},{10,... | collective-permute-start | bytes 589832 | tf_op jit(solution)/shard_map/ppermute | solution.py:41
  36.1 4.9 %collective-permute-start.16 = (bf16[192,256]{1,0:T(8,128)(2,1)S(1)}, bf16[192,256]{1,0:T(8,128)(2,1)S(1)}, u32[]{:S(2)}, u32[]{:S(2)}) collective-permute-start(bf16[192,256]{1,0:T(8,128)(2,1)S(1)} %get-tuple-element.62), channel_id=1, source_target_pairs={{0,4},{1,3},{2,6},{3,1},{4,0},{5,7},{6,2},{7,5},{8,12},{9,11},{10,... | collective-permute-start | bytes 294920 | tf_op jit(solution)/shard_map/ppermute | solution.py:41
  36.8 7.3 %collective-permute-start.11 = (bf16[192,256]{1,0:T(8,128)(2,1)S(1)}, bf16[192,256]{1,0:T(8,128)(2,1)S(1)}, u32[]{:S(2)}, u32[]{:S(2)}) collective-permute-start(bf16[192,256]{1,0:T(8,128)(2,1)S(1)} %get-tuple-element.56), channel_id=1, source_target_pairs={{0,2},{1,5},{2,0},{3,7},{4,6},{5,1},{6,4},{7,3},{8,10},{9,13},{10,... | collective-permute-start | bytes 294920 | tf_op jit(solution)/shard_map/ppermute | solution.py:41
  38.8 8.0 %collective-permute-start.2 = (bf16[192,256]{1,0:T(8,128)(2,1)S(1)}, bf16[192,256]{1,0:T(8,128)(2,1)S(1)}, u32[]{:S(2)}, u32[]{:S(2)}) collective-permute-start(bf16[192,256]{1,0:T(8,128)(2,1)S(1)} %get-tuple-element.43), channel_id=1, source_target_pairs={{0,2},{1,5},{2,0},{3,7},{4,6},{5,1},{6,4},{7,3},{8,10},{9,13},{10,... | collective-permute-start | bytes 294920 | tf_op jit(solution)/shard_map/ppermute | solution.py:41
  41.0 13.7 %collective-permute-start.17 = (bf16[3,64,256]{2,1,0:T(8,128)(2,1)S(1)}, bf16[3,64,256]{2,1,0:T(8,128)(2,1)S(1)}, u32[]{:S(2)}, u32[]{:S(2)}) collective-permute-start(bf16[3,64,256]{2,1,0:T(8,128)(2,1)S(1)} %sum_parts.21.refs_0_), channel_id=1, source_target_pairs={{0,16},{8,24},{16,0},{24,8},{1,17},{9,25},{17,1},{25,9},{2,18},{10... | collective-permute-start | bytes 294920 | tf_op jit(solution)/shard_map/ppermute | solution.py:24
  43.7 13.1 %collective-permute-start.9 = (bf16[3,64,256]{2,1,0:T(8,128)(2,1)S(1)}, bf16[3,64,256]{2,1,0:T(8,128)(2,1)S(1)}, u32[]{:S(2)}, u32[]{:S(2)}) collective-permute-start(bf16[3,64,256]{2,1,0:T(8,128)(2,1)S(1)} %sum_parts.16.refs_0_), channel_id=1, source_target_pairs={{0,16},{8,24},{16,0},{24,8},{1,17},{9,25},{17,1},{25,9},{2,18},{10... | collective-permute-start | bytes 294920 | tf_op jit(solution)/shard_map/ppermute | solution.py:24
  44.1 13.7 %collective-permute-start.12 = (bf16[3,64,256]{2,1,0:T(8,128)(2,1)S(1)}, bf16[3,64,256]{2,1,0:T(8,128)(2,1)S(1)}, u32[]{:S(2)}, u32[]{:S(2)}) collective-permute-start(bf16[3,64,256]{2,1,0:T(8,128)(2,1)S(1)} %sum_parts.18.refs_0_), channel_id=1, source_target_pairs={{0,16},{8,24},{16,0},{24,8},{1,17},{9,25},{17,1},{25,9},{2,18},{10... | collective-permute-start | bytes 294920 | tf_op jit(solution)/shard_map/ppermute | solution.py:24
  46.8 12.6 %collective-permute-start.3 = (bf16[3,64,256]{2,1,0:T(8,128)(2,1)S(1)}, bf16[3,64,256]{2,1,0:T(8,128)(2,1)S(1)}, u32[]{:S(2)}, u32[]{:S(2)}) collective-permute-start(bf16[3,64,256]{2,1,0:T(8,128)(2,1)S(1)} %sum_parts.13.refs_0_), channel_id=1, source_target_pairs={{0,16},{8,24},{16,0},{24,8},{1,17},{9,25},{17,1},{25,9},{2,18},{10... | collective-permute-start | bytes 294920 | tf_op jit(solution)/shard_map/ppermute | solution.py:24
  54.9 6.1 %collective-permute-start.18 = (bf16[3,64,256]{2,1,0:T(8,128)(2,1)S(1)}, bf16[3,64,256]{2,1,0:T(8,128)(2,1)S(1)}, u32[]{:S(2)}, u32[]{:S(2)}) collective-permute-start(bf16[3,64,256]{2,1,0:T(8,128)(2,1)S(1)} %middle_level.7.own_ref), channel_id=1, source_target_pairs={{0,8},{8,0},{16,24},{24,16},{1,9},{9,1},{17,25},{25,17},{2,10},{10... | collective-permute-start | bytes 294920 | tf_op jit(solution)/shard_map/ppermute | solution.py:24
  57.0 6.1 %collective-permute-start.10 = (bf16[3,64,256]{2,1,0:T(8,128)(2,1)S(1)}, bf16[3,64,256]{2,1,0:T(8,128)(2,1)S(1)}, u32[]{:S(2)}, u32[]{:S(2)}) collective-permute-start(bf16[3,64,256]{2,1,0:T(8,128)(2,1)S(1)} %middle_level.5.own_ref), channel_id=1, source_target_pairs={{0,8},{8,0},{16,24},{24,16},{1,9},{9,1},{17,25},{25,17},{2,10},{10... | collective-permute-start | bytes 294920 | tf_op jit(solution)/shard_map/ppermute | solution.py:24
  58.1 7.2 %collective-permute-start.13 = (bf16[3,64,256]{2,1,0:T(8,128)(2,1)S(1)}, bf16[3,64,256]{2,1,0:T(8,128)(2,1)S(1)}, u32[]{:S(2)}, u32[]{:S(2)}) collective-permute-start(bf16[3,64,256]{2,1,0:T(8,128)(2,1)S(1)} %middle_level.6.own_ref), channel_id=1, source_target_pairs={{0,8},{8,0},{16,24},{24,16},{1,9},{9,1},{17,25},{25,17},{2,10},{10... | collective-permute-start | bytes 294920 | tf_op jit(solution)/shard_map/ppermute | solution.py:24
  59.6 7.6 %collective-permute-start.4 = (bf16[3,64,256]{2,1,0:T(8,128)(2,1)S(1)}, bf16[3,64,256]{2,1,0:T(8,128)(2,1)S(1)}, u32[]{:S(2)}, u32[]{:S(2)}) collective-permute-start(bf16[3,64,256]{2,1,0:T(8,128)(2,1)S(1)} %middle_level.4.own_ref), channel_id=1, source_target_pairs={{0,8},{8,0},{16,24},{24,16},{1,9},{9,1},{17,25},{25,17},{2,10},{10... | collective-permute-start | bytes 294920 | tf_op jit(solution)/shard_map/ppermute | solution.py:24
